TPU v7x, 32 devices: a whole 2x2x4 slice. The times are simulated.
32 devices in a mesh: row: 4 (over x, core), col: 8 (over z, y).
Axes of the slice: x: 2, y: 2, z: 4, core: 2. Of those that a mesh axis runs over, the one named last changes fastest.
Arguments:
- amps: bfloat16 [4096, 4096], P(('row', 'col')), may hold values from -6 to 6
- integrals: bfloat16 [4096, 4096], P('row', 'col'), may hold values from -0.125 to 0.125
- amplitude_tile_mask: int32 [32, 32], P('row', 'col'), may hold values from 0 to 1, as said below
- integral_tile_mask: int32 [32, 32], P('row', 'col'), may hold values 0 or 1
Outputs:
- ladder: float32 [4096, 4096], P('row', 'col')
Inputs may be any that keep to these rules, and one draw needn't show every extreme that they name: `amplitude_tile_mask`: in every tile row, each aligned group of 4 tile columns holds exactly 2 nonzero tiles.
All inputs are finite; a program needn't handle non-finite values. No bound on the sum of `integral_tile_mask` on one device may be relied on, other than what follows from the above.
Results may differ from a plain program's by a relative error of at most 0.0003.
Values may be sent and summed in bfloat16 or wider, within the bound.
No kernel may reach another device: no remote copies, remote signals or barrier semaphores. Data moves between devices by JAX's collectives and lax.ppermute only.
A program may use at most 128 MiB of HBM per device.

v0:
```python
import jax
import jax.numpy as jnp
from jax import lax
from jax.sharding import PartitionSpec as P

TILE_EDGE = 128


def on_device(amps, integrals, amplitude_tile_mask, integral_tile_mask):
    tile_rows, kblock = amplitude_tile_mask.shape
    ktiles_local, ntiles_local = integral_tile_mask.shape
    local_row_block = tile_rows * TILE_EDGE
    tile = TILE_EDGE
    sparse_ints = (
        integrals.reshape(ktiles_local, tile, ntiles_local, tile)
        * integral_tile_mask[:, None, :, None].astype(integrals.dtype)
    ).reshape(integrals.shape)
    all_ints = lax.all_gather(sparse_ints, "row", axis=0, tiled=True)
    grid_amps = lax.all_to_all(amps, "col", split_axis=1, concat_axis=0, tiled=True)
    blocks = grid_amps.reshape(tile_rows, tile, kblock, tile) * amplitude_tile_mask[
        :, None, :, None
    ].astype(grid_amps.dtype)
    sparse_amplitude_tiles = blocks.reshape(local_row_block, kblock * tile)
    return jnp.dot(
        lax.all_gather(sparse_amplitude_tiles, "col", axis=1, tiled=True),
        all_ints,
        preferred_element_type=jnp.float32,
    )


def solution(mesh):
    placed = (P(("row", "col"), None), P("row", "col"), P("row", "col"), P("row", "col"))
    return jax.shard_map(
        on_device, mesh=mesh, in_specs=placed, out_specs=P("row", "col"), check_vma=False
    )
```

profile of v0, /device:TPU:0, one launch (start us, length us, event | category | flops | bytes accessed | tf_op | source)
XLA Modules:
  0.0 192.2 jit_solution(4629140158910523383)
XLA Ops:
  6.5 0.0 copy-start
  6.5 0.0 all-gather.5.cloned.1.call-start
  6.5 0.8 convert_element_type.9
  7.3 0.1 copy.12
  7.4 0.3 mul.25
  7.8 0.0 copy-start.1
  7.8 2.4 %bitcast_multiply_fusion = bf16[1024,512]{1,0:T(8,128)(2,1)} fusion(bf16[1024,512]{1,0:T(8,128)(2,1)} %param.5, bf16[128,8,4,128]{3,2,1,0:T(4,128)(2,1)S(1)} %bitcast.15), kind=kLoop, calls=%fused_computation | loop fusion | flops 524288 | bytes 3145728 | tf_op jit(solution)/shard_map/mul | solution.py:15
  10.2 0.0 all-gather.5.cloned.1.call-update
  10.2 0.0 copy-done
  10.2 1.3 copy.9
  11.5 7.3 %all-to-all-start = ((bf16[128,8,512]{0,2,1:T(8,128)(2,1)}), bf16[128,8,512]{0,2,1:T(8,128)(2,1)S(1)}, u32[]{:S(2)}, u32[]{:S(2)}) async-start(bf16[128,8,512]{0,2,1:T(8,128)(2,1)} %bitcast), calls=%async_computation | async-start | bytes 2097152 | tf_op jit(solution)/shard_map/all_to_all | solution.py:19
  18.8 0.0 all-gather.3.cloned.1.call-start
  18.9 0.0 copy-done.1
  18.9 0.1 copy.11
  19.0 25.6 %all-to-all-done = bf16[128,8,512]{0,2,1:T(8,128)(2,1)S(1)} async-done(((bf16[128,8,512]{0,2,1:T(8,128)(2,1)}), bf16[128,8,512]{0,2,1:T(8,128)(2,1)S(1)}, u32[]{:S(2)}, u32[]{:S(2)}) %all-to-all-start) | async-done | bytes 1048608 | tf_op jit(solution)/shard_map/all_to_all | solution.py:19
  44.6 0.5 copy.10
  45.1 0.3 mul.22
  45.5 1.2 bitcast_multiply_fusion.1
  46.7 0.0 all-gather.3.cloned.1.call-update
  46.7 0.8 all-gather.5.cloned.1.call-done
  47.5 127.5 %all-gather.3.cloned.1.call-done = bf16[1024,4096]{1,0:T(8,128)(2,1)} async-done(((bf16[1024,512]{1,0:T(8,128)(2,1)}), bf16[1024,4096]{1,0:T(8,128)(2,1)}) %all-gather.3.cloned.1.call-update) | async-done | bytes 8388624 | tf_op jit(solution)/shard_map/all_gather | solution.py:25
  175.0 10.4 %fusion = f32[1024,512]{1,0:T(8,128)} fusion(bf16[1024,4096]{1,0:T(8,128)(2,1)} %all-gather.3.cloned.1.call-done, bf16[4096,512]{1,0:T(8,128)(2,1)} %all-gather.5.cloned.1.call-done), kind=kOutput, calls=%fused_computation.2 | convolution fusion | flops 4294967296 | bytes 14680064 | tf_op jit(solution)/shard_map/dot_general | solution.py:24
  (1 shorter events, 0.0 us)
Async XLA Ops:
  6.5 3.7 %copy-start = (bf16[128,4096]{1,0:T(8,128)(2,1)S(1)}, bf16[128,4096]{1,0:T(8,128)(2,1)}, u32[]{:S(2)}) copy-start(bf16[128,4096]{1,0:T(8,128)(2,1)} %param.4) | copy-start | bytes 3145732
  6.5 41.0 %all-gather.5.cloned.1.call-start = ((), (), s32[]{:S(2)}) async-start(), calls=%async_computation.2 | async-start | bytes 5242880 | tf_op jit(solution)/shard_map/all_gather | solution.py:18
  7.8 11.1 %copy-start.1 = (s32[8,4]{0,1:T(4,128)S(1)}, s32[8,4]{0,1:T(4,128)}, u32[]{:S(2)}) copy-start(s32[8,4]{0,1:T(4,128)} %param.6) | copy-start | bytes 388
  11.5 33.0 %all-to-all-start = ((bf16[128,8,512]{0,2,1:T(8,128)(2,1)}), bf16[128,8,512]{0,2,1:T(8,128)(2,1)S(1)}, u32[]{:S(2)}, u32[]{:S(2)}) async-start(bf16[128,8,512]{0,2,1:T(8,128)(2,1)} %bitcast), calls=%async_computation | async-start | bytes 2097152 | tf_op jit(solution)/shard_map/all_to_all | solution.py:19
  18.8 156.2 %all-gather.3.cloned.1.call-start = ((), (), s32[]{:S(2)}) async-start(), calls=%async_computation.1 | async-start | bytes 9437184 | tf_op jit(solution)/shard_map/all_gather | solution.py:25
Sparse Core Ops, SparseCore 0:
  10.3 37.1 all-gather.4
  49.6 125.3 all-gather.2
where the time goes:
time: 192 us
  waiting for transfers between devices  154 us (80%)
  between operations  13.5 us (7%)
  matrix products  10.4 us (5%)
  starting transfers between devices  7.32 us (4%)
  other arithmetic  4.41 us (2%)
  local copies, waits for them, and re-layouts  2.71 us (1%)
    all_gather x1, waiting for transfers between devices, on_device(): lax.all_gather(sparse_amplitude_tiles, 'col', axis=1, tiled=True)  127 us
    all_to_all x1, waiting for transfers between devices, on_device(): lax.all_to_all(amps, 'col', split_axis=1, concat_axis=0, tiled=True)  25.6 us
    dot_general x1, matrix products, on_device(): jnp.dot(lax.all_gather(sparse_amplitude_tiles, 'col', axis=1, tiled=True)...  10.4 us
    all_to_all x1, starting transfers between devices, on_device(): lax.all_to_all(amps, 'col', split_axis=1, concat_axis=0, tiled=True)  7.28 us
  transfers between devices with their start and end apart: 3, of which 3 were waited for; matrix products, arithmetic and copies ran while one was open for 2% of the time, Pallas kernels for 0%

commit v1 on v0

v1 whole, which is shorter than its diff:
```python
import functools

import jax
import jax.numpy as jnp
from jax import lax
from jax.experimental import pallas as pl
from jax.experimental.pallas import tpu as pltpu
from jax.sharding import PartitionSpec as P

TILE = 128
GROUP = 4
KEEP = 2
VMEM_LIMIT = 40 * 1024 * 1024

_smem = pl.BlockSpec(memory_space=pltpu.SMEM)
_vmem = pl.BlockSpec(memory_space=pltpu.VMEM)
_any = pl.BlockSpec(memory_space=pl.ANY)


def ring_chip(pos, n):
    return jnp.where(pos < n // 2, 2 * pos, 2 * (n - 1 - pos) + 1)


def ring_pos(c, n):
    return jnp.where(c % 2 == 0, c // 2, n - 1 - c // 2)


def picks(mask_ref, row, first):
    m0, m1 = mask_ref[row, first], mask_ref[row, first + 1]
    m2, m3 = mask_ref[row, first + 2], mask_ref[row, first + 3]
    lo = jnp.where(m0 != 0, 0, jnp.where(m1 != 0, 1, 2))
    hi = jnp.where(m3 != 0, 3, jnp.where(m2 != 0, 2, 1))
    return lo, hi


def mask_ints_kernel(mask_ref, x_ref, o_ref):
    kt, nt = mask_ref.shape
    for q in range(kt):
        for n in range(nt):
            at = (pl.ds(q * TILE, TILE), pl.ds(n * TILE, TILE))
            x = x_ref[at]
            o_ref[at] = jnp.where(mask_ref[q, n] != 0, x, jnp.zeros_like(x))


def compress_kernel(n_row, kt_local, mask_ref, a_ref, *refs):
    outs, sem = refs[:-1], refs[-1]
    rows = a_ref.shape[0]
    r, c = lax.axis_index("row"), lax.axis_index("col")
    row = c * rows // TILE
    per_out = n_row // len(outs)
    copies = []
    for j in range(n_row):
        block = jnp.bitwise_xor(r, j)
        out, j_in = outs[j // per_out], j % per_out
        for g in range(kt_local // GROUP):
            first = block * kt_local + g * GROUP
            for s, p in enumerate(picks(mask_ref, row, first)):
                slot = (j_in * (kt_local // GROUP) + g) * KEEP + s
                src = pl.multiple_of((first + p) * TILE, TILE)
                copies.append(
                    pltpu.make_async_copy(
                        a_ref.at[:, pl.ds(src, TILE)],
                        out.at[:, pl.ds(slot * TILE, TILE)],
                        sem.at[len(copies)],
                    )
                )
    for copy in copies:
        copy.start()
    for copy in copies:
        copy.wait()


def ladder_kernel(n_row, n_col, shifts, mask_ref, *refs):
    n_units = 2 * len(shifts)
    units, ints = refs[:n_units], refs[n_units : n_units + n_row]
    o_ref, acc, sem = refs[-3:]
    rows = units[0].shape[0]
    kt_local = ints[0].shape[0] // TILE
    per_unit = n_row // 2
    r, c = lax.axis_index("row"), lax.axis_index("col")
    pos = ring_pos(c, n_col)
    copies = []
    for i, shift in enumerate(shifts):
        src = ring_chip(lax.rem(pos + (n_col - shift), n_col), n_col)
        row = src * rows // TILE
        total = jnp.zeros(acc.shape[1:], jnp.float32)
        for j in range(n_row):
            block = jnp.bitwise_xor(r, j)
            unit, j_in = units[2 * i + j // per_unit], j % per_unit
            for g in range(kt_local // GROUP):
                lo, hi = picks(mask_ref, row, block * kt_local + g * GROUP)
                rhs = jnp.concatenate(
                    [ints[j][pl.ds(pl.multiple_of((g * GROUP + p) * TILE, TILE), TILE), :] for p in (lo, hi)], axis=0
                )
                at = (j_in * (kt_local // GROUP) + g) * KEEP * TILE
                total += jnp.dot(unit[:, at : at + KEEP * TILE], rhs, preferred_element_type=jnp.float32)
        acc[i] = total
        copy = pltpu.make_async_copy(acc.at[i], o_ref.at[pl.ds(pl.multiple_of(src * rows, rows), rows), :], sem.at[i])
        copy.start()
        copies.append(copy)
    for copy in copies:
        copy.wait()


def ladder_rows(n_row, n_col, shifts, mask, units, ints, out_shape, out):
    rows, cols = units[0][0].shape[0], out_shape.shape[1]
    flat = [u for pair in units for u in pair]
    args = [mask, *flat, *ints]
    specs = [_smem] + [_vmem] * (len(flat) + len(ints))
    alias = {}
    if out is not None:
        alias = {len(args): 0}
        args.append(out)
        specs.append(_any)
    return pl.pallas_call(
        functools.partial(ladder_kernel, n_row, n_col, shifts),
        out_shape=out_shape,
        in_specs=specs,
        out_specs=_any,
        scratch_shapes=[pltpu.VMEM((len(shifts), rows, cols), jnp.float32), pltpu.SemaphoreType.DMA((len(shifts),))],
        input_output_aliases=alias,
        compiler_params=pltpu.CompilerParams(vmem_limit_bytes=VMEM_LIMIT),
    )(*args)


def on_device(n_row, n_col, amps, integrals, amplitude_tile_mask, integral_tile_mask):
    rows, depth = amps.shape
    tile_rows, kblock = amplitude_tile_mask.shape
    kt_local = integrals.shape[0] // TILE
    r, c = lax.axis_index("row"), lax.axis_index("col")

    sparse_ints = pl.pallas_call(
        mask_ints_kernel,
        out_shape=jax.ShapeDtypeStruct(integrals.shape, integrals.dtype),
        in_specs=[_smem, _vmem],
        out_specs=_vmem,
        compiler_params=pltpu.CompilerParams(vmem_limit_bytes=VMEM_LIMIT),
    )(integral_tile_mask, integrals)
    ints = [None] * n_row
    for j in range(0, n_row, 2):
        ints[j] = sparse_ints if j == 0 else lax.ppermute(sparse_ints, "row", [(i, i ^ j) for i in range(n_row)])
    for j in range(0, n_row, 2):
        ints[j + 1] = lax.ppermute(ints[j], "row", [(i, i ^ 1) for i in range(n_row)])

    mine = lax.broadcasted_iota(jnp.int32, (tile_rows, n_col * kblock), 1) // kblock == c
    mask = lax.psum(jnp.where(mine, jnp.tile(amplitude_tile_mask, (1, n_col)), 0), "col")

    half = (rows, depth * KEEP // GROUP // 2)
    own = pl.pallas_call(
        functools.partial(compress_kernel, n_row, kt_local),
        out_shape=[jax.ShapeDtypeStruct(half, amps.dtype)] * 2,
        in_specs=[_smem, _any],
        out_specs=[_vmem] * 2,
        scratch_shapes=[pltpu.SemaphoreType.DMA((depth // TILE * KEEP // GROUP,))],
        compiler_params=pltpu.CompilerParams(vmem_limit_bytes=VMEM_LIMIT),
    )(mask, amps)

    order = [2 * p if p < n_col // 2 else 2 * (n_col - 1 - p) + 1 for p in range(n_col)]
    up = [(order[p], order[(p + 1) % n_col]) for p in range(n_col)]
    down = [(d, s) for s, d in up]
    out_shape = jax.ShapeDtypeStruct((rows * n_col, integrals.shape[1]), jnp.float32)

    fwd, bwd = own, own
    held = {0: own}
    for k in range(1, n_col // 2):
        nf, nb = [], []
        for h in range(2):
            nf.append(lax.ppermute(fwd[h], "col", up))
            nb.append(lax.ppermute(bwd[h], "col", down))
        fwd, bwd = nf, nb
        held[k], held[n_col - k] = fwd, bwd
    held[n_col // 2] = [lax.ppermute(fwd[0], "col", up), lax.ppermute(bwd[1], "col", down)]

    out = None
    groups = [(0, 1, n_col - 1)] + [(k, n_col - k) for k in range(2, n_col // 2)] + [(n_col // 2,)]
    for shifts in groups:
        out = ladder_rows(n_row, n_col, shifts, mask, [held[s] for s in shifts], ints, out_shape, out)
    return out


def solution(mesh):
    placed = (P(("row", "col"), None), P("row", "col"), P("row", "col"), P("row", "col"))
    return jax.shard_map(
        functools.partial(on_device, mesh.shape["row"], mesh.shape["col"]),
        mesh=mesh,
        in_specs=placed,
        out_specs=P("row", "col"),
        check_vma=False,
    )
```

time: 192 us -> 70.3 us (0.37)
  waiting for transfers between devices: 154 us -> 27.1 us
  between operations: 13.5 us -> 0.1 us
  blocking collectives: 0 us -> 11.6 us
  starting transfers between devices: 7.32 us -> 18.8 us
  matrix products: 10.4 us -> 0 us
  Pallas kernels: 0 us -> 10.4 us
  other arithmetic: 4.41 us -> 0.02 us
    all_gather x2 -> x0, waiting for transfers between devices: 128 us -> none  [the longest x1 127 us: on_device(): lax.all_gather(sparse_amplitude_tiles, 'col', axis=1, tiled=True)]
    ppermute x0 -> x17, waiting for transfers between devices: none -> 27.1 us  [the longest x6 14.2 us: on_device(): nb.append(lax.ppermute(bwd[h], 'col', down))]
    all_to_all x1 -> x0, waiting for transfers between devices: 25.6 us -> none  [on_device(): lax.all_to_all(amps, 'col', split_axis=1, concat_axis=0, tiled=True)]
    ppermute x0 -> x17, starting transfers between devices: none -> 18.8 us  [the longest x6 8.57 us: on_device(): nb.append(lax.ppermute(bwd[h], 'col', down))]
    psum x0 -> x1, blocking collectives: none -> 11.6 us  [on_device(): lax.psum(jnp.where(mine, jnp.tile(amplitude_tile_mask, (1, n_col)), 0), '...]
    pallas_call x0 -> x6, Pallas kernels: none -> 10.4 us  [the longest x4 8.49 us: ladder_rows(): pl.pallas_call(functools.partial(ladder_kernel, n_row, n_col, shifts), ou...]
    dot_general x1 -> x0, matrix products: 10.4 us -> none  [on_device(): jnp.dot(lax.all_gather(sparse_amplitude_tiles, 'col', axis=1, tiled=True)...]
    all_to_all x1 -> x0, starting transfers between devices: 7.28 us -> none  [on_device(): lax.all_to_all(amps, 'col', split_axis=1, concat_axis=0, tiled=True)]
  transfers between devices with their start and end apart: 3 -> 17, of which waited for: 3 -> 8; matrix products, arithmetic and copies ran while one was open for 2% -> 0% of each run, Pallas kernels for 0% -> 11%
where the time goes in v1:
time: 70.3 us; the launch traced here: 70.1 us
  waiting for transfers between devices  27.1 us (39%)
  starting transfers between devices  18.8 us (27%)
  blocking collectives  11.6 us (17%)
  Pallas kernels  10.4 us (15%)
  local copies, waits for them, and re-layouts  2.07 us (3%)
    ppermute x6, waiting for transfers between devices, on_device(): nb.append(lax.ppermute(bwd[h], 'col', down))  14.2 us
    psum x1, blocking collectives, on_device(): lax.psum(jnp.where(mine, jnp.tile(amplitude_tile_mask, (1, n_col)), 0), '...  11.6 us
    ppermute x6, starting transfers between devices, on_device(): nb.append(lax.ppermute(bwd[h], 'col', down))  8.57 us
    pallas_call x4, Pallas kernels, ladder_rows(): pl.pallas_call(functools.partial(ladder_kernel, n_row, n_col, shifts), ou...  8.49 us
    ppermute x1, waiting for transfers between devices, on_device(): lax.ppermute(sparse_ints, 'row', [(i, i ^ j) for i in range(n_row)])  7.8 us
    ppermute x6, starting transfers between devices, on_device(): nf.append(lax.ppermute(fwd[h], 'col', up))  5.2 us
    ppermute x6, waiting for transfers between devices, on_device(): nf.append(lax.ppermute(fwd[h], 'col', up))  3.77 us
    ppermute x1, starting transfers between devices, on_device(): lax.ppermute(sparse_ints, 'row', [(i, i ^ j) for i in range(n_row)])  3 us
  transfers between devices with their start and end apart: 17, of which 8 were waited for; matrix products, arithmetic and copies ran while one was open for 0% of the time, Pallas kernels for 11%

profile of v1, /device:TPU:0, one launch (start us, length us, event | category | flops | bytes accessed | tf_op | source)
XLA Modules:
  0.0 70.1 jit_solution(15899632272698713624)
XLA Ops:
  0.8 1.2 %copy-done = bf16[1024,512]{1,0:T(8,128)(2,1)S(1)} copy-done((bf16[1024,512]{1,0:T(8,128)(2,1)S(1)}, bf16[1024,512]{1,0:T(8,128)(2,1)}, u32[]{:S(2)}) %copy-start) | copy-done | bytes 1048600
  2.0 0.8 %shard_map.47.refs_6_.refs_4_.refs_2_ = bf16[1024,512]{1,0:T(8,128)(2,1)S(1)} custom-call(s32[8,4]{1,0:T(8,128)S(1)} %copy.11.mask_ref, bf16[1024,512]{1,0:T(8,128)(2,1)S(1)} %copy-done), custom_call_target="tpu_custom_call" | custom-call | tf_op jit(solution)/shard_map/pallas_call | solution.py:132
  2.8 3.0 %collective-permute-start.9 = (bf16[1024,512]{1,0:T(8,128)(2,1)S(1)}, bf16[1024,512]{1,0:T(8,128)(2,1)S(1)}, u32[]{:S(2)}, u32[]{:S(2)}) collective-permute-start(bf16[1024,512]{1,0:T(8,128)(2,1)S(1)} %shard_map.47.refs_6_.refs_4_.refs_2_), channel_id=1, source_target_pairs={{0,16},{8,24},{16,0},{24,8},{1,17},{9,25},{17,1},{25,9},{2,18},{10... | collective-permute-start | bytes 3145736 | tf_op jit(solution)/shard_map/ppermute | solution.py:141
  6.0 11.6 %psum.7.mask_ref = s32[8,32]{1,0:T(8,128)S(1)} all-reduce(s32[8,32]{1,0:T(8,128)S(1)} %fusion), channel_id=1, replica_groups=mesh['row'=4,'col'=8] {'col'}, use_global_device_ids=true, to_apply=%region_0.1 | all-reduce | flops 256 | bytes 2048 | tf_op jit(solution)/shard_map/psum | solution.py:146
  17.6 1.1 %shard_map.46 = (bf16[128,1024]{1,0:T(8,128)(2,1)S(1)}, bf16[128,1024]{1,0:T(8,128)(2,1)S(1)}) custom-call(s32[8,32]{1,0:T(8,128)S(1)} %psum.7.mask_ref, bf16[128,4096]{1,0:T(8,128)(2,1)S(1)} %copy-done.1), custom_call_target="tpu_custom_call" | custom-call | tf_op jit(solution)/shard_map/pallas_call | solution.py:149
  19.2 1.6 %collective-permute-start.14 = (bf16[128,1024]{1,0:T(8,128)(2,1)S(1)}, bf16[128,1024]{1,0:T(8,128)(2,1)S(1)}, u32[]{:S(2)}, u32[]{:S(2)}) collective-permute-start(bf16[128,1024]{1,0:T(8,128)(2,1)S(1)} %get-tuple-element.7.refs_0_), channel_id=1, source_target_pairs={{2,0},{4,2},{6,4},{7,6},{5,7},{3,5},{1,3},{0,1},{10,8},{12,10},{14... | collective-permute-start | bytes 786440 | tf_op jit(solution)/shard_map/ppermute | solution.py:169
  21.2 7.8 %collective-permute-done.9.refs_8_.refs_6_.refs_4_ = bf16[1024,512]{1,0:T(8,128)(2,1)S(1)} collective-permute-done((bf16[1024,512]{1,0:T(8,128)(2,1)S(1)}, bf16[1024,512]{1,0:T(8,128)(2,1)S(1)}, u32[]{:S(2)}, u32[]{:S(2)}) %collective-permute-start.9) | collective-permute-done | bytes 1048608 | tf_op jit(solution)/shard_map/ppermute | solution.py:141
  29.0 1.8 %collective-permute-start.4 = (bf16[128,1024]{1,0:T(8,128)(2,1)S(1)}, bf16[128,1024]{1,0:T(8,128)(2,1)S(1)}, u32[]{:S(2)}, u32[]{:S(2)}) collective-permute-start(bf16[128,1024]{1,0:T(8,128)(2,1)S(1)} %get-tuple-element.8.refs_1_), channel_id=1, source_target_pairs={{2,0},{4,2},{6,4},{7,6},{5,7},{3,5},{1,3},{0,1},{10,8},{12,10},{14... | collective-permute-start | bytes 786440 | tf_op jit(solution)/shard_map/ppermute | solution.py:169
  31.2 1.7 %collective-permute-start.12 = (bf16[128,1024]{1,0:T(8,128)(2,1)S(1)}, bf16[128,1024]{1,0:T(8,128)(2,1)S(1)}, u32[]{:S(2)}, u32[]{:S(2)}) collective-permute-start(bf16[128,1024]{1,0:T(8,128)(2,1)S(1)} %collective-permute-done.11.refs_3_), channel_id=1, source_target_pairs={{0,2},{2,4},{4,6},{6,7},{7,5},{5,3},{3,1},{1,0},{8,10},{10,12},{12... | collective-permute-start | bytes 786440 | tf_op jit(solution)/shard_map/ppermute | solution.py:168
  32.9 4.9 %collective-permute-done.4.refs_5_ = bf16[128,1024]{1,0:T(8,128)(2,1)S(1)} collective-permute-done((bf16[128,1024]{1,0:T(8,128)(2,1)S(1)}, bf16[128,1024]{1,0:T(8,128)(2,1)S(1)}, u32[]{:S(2)}, u32[]{:S(2)}) %collective-permute-start.4) | collective-permute-done | bytes 262176 | tf_op jit(solution)/shard_map/ppermute | solution.py:169
  37.8 1.7 %collective-permute-start.5 = (bf16[128,1024]{1,0:T(8,128)(2,1)S(1)}, bf16[128,1024]{1,0:T(8,128)(2,1)S(1)}, u32[]{:S(2)}, u32[]{:S(2)}) collective-permute-start(bf16[128,1024]{1,0:T(8,128)(2,1)S(1)} %collective-permute-done.4.refs_5_), channel_id=1, source_target_pairs={{2,0},{4,2},{6,4},{7,6},{5,7},{3,5},{1,3},{0,1},{10,8},{12,10},{14... | collective-permute-start | bytes 786440 | tf_op jit(solution)/shard_map/ppermute | solution.py:169
  39.9 1.6 %collective-permute-start.15 = (bf16[128,1024]{1,0:T(8,128)(2,1)S(1)}, bf16[128,1024]{1,0:T(8,128)(2,1)S(1)}, u32[]{:S(2)}, u32[]{:S(2)}) collective-permute-start(bf16[128,1024]{1,0:T(8,128)(2,1)S(1)} %collective-permute-done.14.refs_4_), channel_id=1, source_target_pairs={{2,0},{4,2},{6,4},{7,6},{5,7},{3,5},{1,3},{0,1},{10,8},{12,10},{14... | collective-permute-start | bytes 786440 | tf_op jit(solution)/shard_map/ppermute | solution.py:169
  41.5 3.3 %collective-permute-done.12.refs_1_ = bf16[128,1024]{1,0:T(8,128)(2,1)S(1)} collective-permute-done((bf16[128,1024]{1,0:T(8,128)(2,1)S(1)}, bf16[128,1024]{1,0:T(8,128)(2,1)S(1)}, u32[]{:S(2)}, u32[]{:S(2)}) %collective-permute-start.12) | collective-permute-done | bytes 262176 | tf_op jit(solution)/shard_map/ppermute | solution.py:168
  45.2 1.8 %collective-permute-done.5.refs_3_ = bf16[128,1024]{1,0:T(8,128)(2,1)S(1)} collective-permute-done((bf16[128,1024]{1,0:T(8,128)(2,1)S(1)}, bf16[128,1024]{1,0:T(8,128)(2,1)S(1)}, u32[]{:S(2)}, u32[]{:S(2)}) %collective-permute-start.5) | collective-permute-done | bytes 262176 | tf_op jit(solution)/shard_map/ppermute | solution.py:169
  47.0 1.7 %collective-permute-start.6 = (bf16[128,1024]{1,0:T(8,128)(2,1)S(1)}, bf16[128,1024]{1,0:T(8,128)(2,1)S(1)}, u32[]{:S(2)}, u32[]{:S(2)}) collective-permute-start(bf16[128,1024]{1,0:T(8,128)(2,1)S(1)} %collective-permute-done.5.refs_3_), channel_id=1, source_target_pairs={{2,0},{4,2},{6,4},{7,6},{5,7},{3,5},{1,3},{0,1},{10,8},{12,10},{14... | collective-permute-start | bytes 786440 | tf_op jit(solution)/shard_map/ppermute | solution.py:169
  48.7 3.9 %collective-permute-done.15.refs_2_ = bf16[128,1024]{1,0:T(8,128)(2,1)S(1)} collective-permute-done((bf16[128,1024]{1,0:T(8,128)(2,1)S(1)}, bf16[128,1024]{1,0:T(8,128)(2,1)S(1)}, u32[]{:S(2)}, u32[]{:S(2)}) %collective-permute-start.15) | collective-permute-done | bytes 262176 | tf_op jit(solution)/shard_map/ppermute | solution.py:169
  52.6 1.8 %collective-permute-start.13 = (bf16[128,1024]{1,0:T(8,128)(2,1)S(1)}, bf16[128,1024]{1,0:T(8,128)(2,1)S(1)}, u32[]{:S(2)}, u32[]{:S(2)}) collective-permute-start(bf16[128,1024]{1,0:T(8,128)(2,1)S(1)} %collective-permute-done.12.refs_1_), channel_id=1, source_target_pairs={{0,2},{2,4},{4,6},{6,7},{7,5},{5,3},{3,1},{1,0},{8,10},{10,12},{12... | collective-permute-start | bytes 786440 | tf_op jit(solution)/shard_map/ppermute | solution.py:168
  54.7 3.6 %collective-permute-done.6.refs_3_ = bf16[128,1024]{1,0:T(8,128)(2,1)S(1)} collective-permute-done((bf16[128,1024]{1,0:T(8,128)(2,1)S(1)}, bf16[128,1024]{1,0:T(8,128)(2,1)S(1)}, u32[]{:S(2)}, u32[]{:S(2)}) %collective-permute-start.6) | collective-permute-done | bytes 262176 | tf_op jit(solution)/shard_map/ppermute | solution.py:169
  58.2 1.8 %collective-permute-start.3 = (bf16[128,1024]{1,0:T(8,128)(2,1)S(1)}, bf16[128,1024]{1,0:T(8,128)(2,1)S(1)}, u32[]{:S(2)}, u32[]{:S(2)}) collective-permute-start(bf16[128,1024]{1,0:T(8,128)(2,1)S(1)} %collective-permute-done.2.refs_0_), channel_id=1, source_target_pairs={{0,2},{2,4},{4,6},{6,7},{7,5},{5,3},{3,1},{1,0},{8,10},{10,12},{12... | collective-permute-start | bytes 786440 | tf_op jit(solution)/shard_map/ppermute | solution.py:172
  60.3 2.4 %shard_map.48.refs_8_ = f32[1024,512]{1,0:T(8,128)} custom-call(s32[8,32]{1,0:T(8,128)S(1)} %psum.7.mask_ref, bf16[128,1024]{1,0:T(8,128)(2,1)S(1)} %get-tuple-element.7.refs_0_, bf16[128,1024]{1,0:T(8,128)(2,1)S(1)} %get-tuple-element.8.refs_1_, bf16[128,1024]{1,0:T(8,128)(2,1)S(1)} %collective-permute-done.refs_2_, ...), custom_call_target="tpu_custom_call" | custom-call | tf_op jit(solution)/shard_map/pallas_call | solution.py:115
  62.7 2.1 %shard_map.49.refs_8_ = f32[1024,512]{1,0:T(8,128)} custom-call(s32[8,32]{1,0:T(8,128)S(1)} %psum.7.mask_ref, bf16[128,1024]{1,0:T(8,128)(2,1)S(1)} %collective-permute-done.1.refs_0_, bf16[128,1024]{1,0:T(8,128)(2,1)S(1)} %collective-permute-done.12.refs_1_, bf16[128,1024]{1,0:T(8,128)(2,1)S(1)} %collective-permute-done.15.refs_2_, ...), custom_call_target="tpu_custom_call", output_to_operand_aliasing={{}: (9, {})} | custom-call | tf_op jit(solution)/shard_map/pallas_call | solution.py:115
  64.9 2.1 %shard_map.50.refs_6_ = f32[1024,512]{1,0:T(8,128)} custom-call(s32[8,32]{1,0:T(8,128)S(1)} %psum.7.mask_ref, bf16[128,1024]{1,0:T(8,128)(2,1)S(1)} %collective-permute-done.2.refs_0_, bf16[128,1024]{1,0:T(8,128)(2,1)S(1)} %collective-permute-done.13.refs_1_, bf16[128,1024]{1,0:T(8,128)(2,1)S(1)} %collective-permute-done.16.refs_2_, ...), custom_call_target="tpu_custom_call", output_to_operand_aliasing={{}: (9, {})} | custom-call | tf_op jit(solution)/shard_map/pallas_call | solution.py:115
  67.0 1.3 %collective-permute-done.7.refs_1_ = bf16[128,1024]{1,0:T(8,128)(2,1)S(1)} collective-permute-done((bf16[128,1024]{1,0:T(8,128)(2,1)S(1)}, bf16[128,1024]{1,0:T(8,128)(2,1)S(1)}, u32[]{:S(2)}, u32[]{:S(2)}) %collective-permute-start.7) | collective-permute-done | bytes 262176 | tf_op jit(solution)/shard_map/ppermute | solution.py:172
  68.3 1.8 %shard_map.51 = f32[1024,512]{1,0:T(8,128)} custom-call(s32[8,32]{1,0:T(8,128)S(1)} %psum.7.mask_ref, bf16[128,1024]{1,0:T(8,128)(2,1)S(1)} %collective-permute-done.3.refs_0_, bf16[128,1024]{1,0:T(8,128)(2,1)S(1)} %collective-permute-done.7.refs_1_, bf16[1024,512]{1,0:T(8,128)(2,1)S(1)} %shard_map.47.refs_6_.refs_4_.refs_2_, ...), custom_call_target="tpu_custom_call", output_to_operand_aliasing={{}: (7, {})} | custom-call | tf_op jit(solution)/shard_map/pallas_call | solution.py:115
  (29 shorter events, 3.6 us)
Async XLA Ops:
  0.0 5.9 %copy-start.2 = (s32[8,4]{0,1:T(4,128)S(1)}, s32[8,4]{0,1:T(4,128)}, u32[]{:S(2)}) copy-start(s32[8,4]{0,1:T(4,128)} %param.6) | copy-start | bytes 388
  0.8 1.2 %copy-start = (bf16[1024,512]{1,0:T(8,128)(2,1)S(1)}, bf16[1024,512]{1,0:T(8,128)(2,1)}, u32[]{:S(2)}) copy-start(bf16[1024,512]{1,0:T(8,128)(2,1)} %x_ref.1) | copy-start | bytes 3145732
  2.0 15.6 %copy-start.1 = (bf16[128,4096]{1,0:T(8,128)(2,1)S(1)}, bf16[128,4096]{1,0:T(8,128)(2,1)}, u32[]{:S(2)}) copy-start(bf16[128,4096]{1,0:T(8,128)(2,1)} %a_ref.1) | copy-start | bytes 3145732
  2.8 26.2 %collective-permute-start.9 = (bf16[1024,512]{1,0:T(8,128)(2,1)S(1)}, bf16[1024,512]{1,0:T(8,128)(2,1)S(1)}, u32[]{:S(2)}, u32[]{:S(2)}) collective-permute-start(bf16[1024,512]{1,0:T(8,128)(2,1)S(1)} %shard_map.47.refs_6_.refs_4_.refs_2_), channel_id=1, source_target_pairs={{0,16},{8,24},{16,0},{24,8},{1,17},{9,25},{17,1},{25,9},{2,18},{10... | collective-permute-start | bytes 3145736 | tf_op jit(solution)/shard_map/ppermute | solution.py:141
  18.7 10.3 %collective-permute-start = (bf16[128,1024]{1,0:T(8,128)(2,1)S(1)}, bf16[128,1024]{1,0:T(8,128)(2,1)S(1)}, u32[]{:S(2)}, u32[]{:S(2)}) collective-permute-start(bf16[128,1024]{1,0:T(8,128)(2,1)S(1)} %get-tuple-element.7.refs_0_), channel_id=1, source_target_pairs={{0,2},{2,4},{4,6},{6,7},{7,5},{5,3},{3,1},{1,0},{8,10},{10,12},{12... | collective-permute-start | bytes 786440 | tf_op jit(solution)/shard_map/ppermute | solution.py:168
  19.2 40.8 %collective-permute-start.8 = (bf16[1024,512]{1,0:T(8,128)(2,1)S(1)}, bf16[1024,512]{1,0:T(8,128)(2,1)S(1)}, u32[]{:S(2)}, u32[]{:S(2)}) collective-permute-start(bf16[1024,512]{1,0:T(8,128)(2,1)S(1)} %shard_map.47.refs_6_.refs_4_.refs_2_), channel_id=1, source_target_pairs={{0,8},{8,0},{16,24},{24,16},{1,9},{9,1},{17,25},{25,17},{2,10},{10... | collective-permute-start | bytes 3145736 | tf_op jit(solution)/shard_map/ppermute | solution.py:143
  19.2 12.0 %collective-permute-start.14 = (bf16[128,1024]{1,0:T(8,128)(2,1)S(1)}, bf16[128,1024]{1,0:T(8,128)(2,1)S(1)}, u32[]{:S(2)}, u32[]{:S(2)}) collective-permute-start(bf16[128,1024]{1,0:T(8,128)(2,1)S(1)} %get-tuple-element.7.refs_0_), channel_id=1, source_target_pairs={{2,0},{4,2},{6,4},{7,6},{5,7},{3,5},{1,3},{0,1},{10,8},{12,10},{14... | collective-permute-start | bytes 786440 | tf_op jit(solution)/shard_map/ppermute | solution.py:169
  20.7 10.0 %collective-permute-start.11 = (bf16[128,1024]{1,0:T(8,128)(2,1)S(1)}, bf16[128,1024]{1,0:T(8,128)(2,1)S(1)}, u32[]{:S(2)}, u32[]{:S(2)}) collective-permute-start(bf16[128,1024]{1,0:T(8,128)(2,1)S(1)} %get-tuple-element.8.refs_1_), channel_id=1, source_target_pairs={{0,2},{2,4},{4,6},{6,7},{7,5},{5,3},{3,1},{1,0},{8,10},{10,12},{12... | collective-permute-start | bytes 786440 | tf_op jit(solution)/shard_map/ppermute | solution.py:168
  29.0 31.3 %collective-permute-start.10 = (bf16[1024,512]{1,0:T(8,128)(2,1)S(1)}, bf16[1024,512]{1,0:T(8,128)(2,1)S(1)}, u32[]{:S(2)}, u32[]{:S(2)}) collective-permute-start(bf16[1024,512]{1,0:T(8,128)(2,1)S(1)} %collective-permute-done.9.refs_8_.refs_6_.refs_4_), channel_id=1, source_target_pairs={{0,8},{8,0},{16,24},{24,16},{1,9},{9,1},{17,25},{25,17},{2,10},{10... | collective-permute-start | bytes 3145736 | tf_op jit(solution)/shard_map/ppermute | solution.py:143
  29.0 8.8 %collective-permute-start.4 = (bf16[128,1024]{1,0:T(8,128)(2,1)S(1)}, bf16[128,1024]{1,0:T(8,128)(2,1)S(1)}, u32[]{:S(2)}, u32[]{:S(2)}) collective-permute-start(bf16[128,1024]{1,0:T(8,128)(2,1)S(1)} %get-tuple-element.8.refs_1_), channel_id=1, source_target_pairs={{2,0},{4,2},{6,4},{7,6},{5,7},{3,5},{1,3},{0,1},{10,8},{12,10},{14... | collective-permute-start | bytes 786440 | tf_op jit(solution)/shard_map/ppermute | solution.py:169
  30.8 9.1 %collective-permute-start.1 = (bf16[128,1024]{1,0:T(8,128)(2,1)S(1)}, bf16[128,1024]{1,0:T(8,128)(2,1)S(1)}, u32[]{:S(2)}, u32[]{:S(2)}) collective-permute-start(bf16[128,1024]{1,0:T(8,128)(2,1)S(1)} %collective-permute-done.refs_2_), channel_id=1, source_target_pairs={{0,2},{2,4},{4,6},{6,7},{7,5},{5,3},{3,1},{1,0},{8,10},{10,12},{12... | collective-permute-start | bytes 786440 | tf_op jit(solution)/shard_map/ppermute | solution.py:168
  31.2 13.7 %collective-permute-start.12 = (bf16[128,1024]{1,0:T(8,128)(2,1)S(1)}, bf16[128,1024]{1,0:T(8,128)(2,1)S(1)}, u32[]{:S(2)}, u32[]{:S(2)}) collective-permute-start(bf16[128,1024]{1,0:T(8,128)(2,1)S(1)} %collective-permute-done.11.refs_3_), channel_id=1, source_target_pairs={{0,2},{2,4},{4,6},{6,7},{7,5},{5,3},{3,1},{1,0},{8,10},{10,12},{12... | collective-permute-start | bytes 786440 | tf_op jit(solution)/shard_map/ppermute | solution.py:168
  37.8 9.2 %collective-permute-start.5 = (bf16[128,1024]{1,0:T(8,128)(2,1)S(1)}, bf16[128,1024]{1,0:T(8,128)(2,1)S(1)}, u32[]{:S(2)}, u32[]{:S(2)}) collective-permute-start(bf16[128,1024]{1,0:T(8,128)(2,1)S(1)} %collective-permute-done.4.refs_5_), channel_id=1, source_target_pairs={{2,0},{4,2},{6,4},{7,6},{5,7},{3,5},{1,3},{0,1},{10,8},{12,10},{14... | collective-permute-start | bytes 786440 | tf_op jit(solution)/shard_map/ppermute | solution.py:169
  39.9 12.7 %collective-permute-start.15 = (bf16[128,1024]{1,0:T(8,128)(2,1)S(1)}, bf16[128,1024]{1,0:T(8,128)(2,1)S(1)}, u32[]{:S(2)}, u32[]{:S(2)}) collective-permute-start(bf16[128,1024]{1,0:T(8,128)(2,1)S(1)} %collective-permute-done.14.refs_4_), channel_id=1, source_target_pairs={{2,0},{4,2},{6,4},{7,6},{5,7},{3,5},{1,3},{0,1},{10,8},{12,10},{14... | collective-permute-start | bytes 786440 | tf_op jit(solution)/shard_map/ppermute | solution.py:169
  44.8 9.5 %collective-permute-start.2 = (bf16[128,1024]{1,0:T(8,128)(2,1)S(1)}, bf16[128,1024]{1,0:T(8,128)(2,1)S(1)}, u32[]{:S(2)}, u32[]{:S(2)}) collective-permute-start(bf16[128,1024]{1,0:T(8,128)(2,1)S(1)} %collective-permute-done.1.refs_0_), channel_id=1, source_target_pairs={{0,2},{2,4},{4,6},{6,7},{7,5},{5,3},{3,1},{1,0},{8,10},{10,12},{12... | collective-permute-start | bytes 786440 | tf_op jit(solution)/shard_map/ppermute | solution.py:168
  47.0 11.2 %collective-permute-start.6 = (bf16[128,1024]{1,0:T(8,128)(2,1)S(1)}, bf16[128,1024]{1,0:T(8,128)(2,1)S(1)}, u32[]{:S(2)}, u32[]{:S(2)}) collective-permute-start(bf16[128,1024]{1,0:T(8,128)(2,1)S(1)} %collective-permute-done.5.refs_3_), channel_id=1, source_target_pairs={{2,0},{4,2},{6,4},{7,6},{5,7},{3,5},{1,3},{0,1},{10,8},{12,10},{14... | collective-permute-start | bytes 786440 | tf_op jit(solution)/shard_map/ppermute | solution.py:169
  52.6 12.2 %collective-permute-start.13 = (bf16[128,1024]{1,0:T(8,128)(2,1)S(1)}, bf16[128,1024]{1,0:T(8,128)(2,1)S(1)}, u32[]{:S(2)}, u32[]{:S(2)}) collective-permute-start(bf16[128,1024]{1,0:T(8,128)(2,1)S(1)} %collective-permute-done.12.refs_1_), channel_id=1, source_target_pairs={{0,2},{2,4},{4,6},{6,7},{7,5},{5,3},{3,1},{1,0},{8,10},{10,12},{12... | collective-permute-start | bytes 786440 | tf_op jit(solution)/shard_map/ppermute | solution.py:168
  54.4 10.5 %collective-permute-start.16 = (bf16[128,1024]{1,0:T(8,128)(2,1)S(1)}, bf16[128,1024]{1,0:T(8,128)(2,1)S(1)}, u32[]{:S(2)}, u32[]{:S(2)}) collective-permute-start(bf16[128,1024]{1,0:T(8,128)(2,1)S(1)} %collective-permute-done.15.refs_2_), channel_id=1, source_target_pairs={{2,0},{4,2},{6,4},{7,6},{5,7},{3,5},{1,3},{0,1},{10,8},{12,10},{14... | collective-permute-start | bytes 786440 | tf_op jit(solution)/shard_map/ppermute | solution.py:169
  58.2 8.8 %collective-permute-start.3 = (bf16[128,1024]{1,0:T(8,128)(2,1)S(1)}, bf16[128,1024]{1,0:T(8,128)(2,1)S(1)}, u32[]{:S(2)}, u32[]{:S(2)}) collective-permute-start(bf16[128,1024]{1,0:T(8,128)(2,1)S(1)} %collective-permute-done.2.refs_0_), channel_id=1, source_target_pairs={{0,2},{2,4},{4,6},{6,7},{7,5},{5,3},{3,1},{1,0},{8,10},{10,12},{12... | collective-permute-start | bytes 786440 | tf_op jit(solution)/shard_map/ppermute | solution.py:172
  60.0 8.3 %collective-permute-start.7 = (bf16[128,1024]{1,0:T(8,128)(2,1)S(1)}, bf16[128,1024]{1,0:T(8,128)(2,1)S(1)}, u32[]{:S(2)}, u32[]{:S(2)}) collective-permute-start(bf16[128,1024]{1,0:T(8,128)(2,1)S(1)} %collective-permute-done.6.refs_3_), channel_id=1, source_target_pairs={{2,0},{4,2},{6,4},{7,6},{5,7},{3,5},{1,3},{0,1},{10,8},{12,10},{14... | collective-permute-start | bytes 786440 | tf_op jit(solution)/shard_map/ppermute | solution.py:172

commit v2 on v1

--- a/solution.py
+++ b/solution.py
@@ -14,7 +14,9 @@
 
 _smem = pl.BlockSpec(memory_space=pltpu.SMEM)
 _vmem = pl.BlockSpec(memory_space=pltpu.VMEM)
+_hbm = pl.BlockSpec(memory_space=pltpu.HBM)
 _any = pl.BlockSpec(memory_space=pl.ANY)
+_params = pltpu.CompilerParams(vmem_limit_bytes=VMEM_LIMIT)
 
 
 def ring_chip(pos, n):
@@ -33,13 +35,21 @@
     return lo, hi
 
 
-def mask_ints_kernel(mask_ref, x_ref, o_ref):
-    kt, nt = mask_ref.shape
-    for q in range(kt):
-        for n in range(nt):
-            at = (pl.ds(q * TILE, TILE), pl.ds(n * TILE, TILE))
-            x = x_ref[at]
-            o_ref[at] = jnp.where(mask_ref[q, n] != 0, x, jnp.zeros_like(x))
+def mask_ints_kernel(mask_ref, x_ref, *refs):
+    outs, buf, sem = refs[:-2], refs[-2], refs[-1]
+    nt, kt = mask_ref.shape
+    copies = []
+    for g in range(len(outs)):
+        at = pl.ds(g * GROUP * TILE, GROUP * TILE)
+        copies.append(pltpu.make_async_copy(x_ref.at[at, :], buf.at[g], sem.at[g]))
+        copies[-1].start()
+    for g, out in enumerate(outs):
+        copies[g].wait()
+        for q in range(GROUP):
+            for t in range(nt):
+                at = (pl.ds(q * TILE, TILE), pl.ds(t * TILE, TILE))
+                x = buf[g, at[0], at[1]]
+                out[at] = jnp.where(mask_ref[t, g * GROUP + q] != 0, x, jnp.zeros_like(x))
 
 
 def compress_kernel(n_row, kt_local, mask_ref, a_ref, *refs):
@@ -70,12 +80,11 @@
         copy.wait()
 
 
-def ladder_kernel(n_row, n_col, shifts, mask_ref, *refs):
+def ladder_kernel(n_row, n_col, kt_local, shifts, mask_ref, *refs):
     n_units = 2 * len(shifts)
-    units, ints = refs[:n_units], refs[n_units : n_units + n_row]
+    units, ints = refs[:n_units], refs[n_units:]
     o_ref, acc, sem = refs[-3:]
     rows = units[0].shape[0]
-    kt_local = ints[0].shape[0] // TILE
     per_unit = n_row // 2
     r, c = lax.axis_index("row"), lax.axis_index("col")
     pos = ring_pos(c, n_col)
@@ -89,9 +98,8 @@
             unit, j_in = units[2 * i + j // per_unit], j % per_unit
             for g in range(kt_local // GROUP):
                 lo, hi = picks(mask_ref, row, block * kt_local + g * GROUP)
-                rhs = jnp.concatenate(
-                    [ints[j][pl.ds(pl.multiple_of((g * GROUP + p) * TILE, TILE), TILE), :] for p in (lo, hi)], axis=0
-                )
+                held = ints[j * (kt_local // GROUP) + g]
+                rhs = jnp.concatenate([held[pl.ds(pl.multiple_of(p * TILE, TILE), TILE), :] for p in (lo, hi)], axis=0)
                 at = (j_in * (kt_local // GROUP) + g) * KEEP * TILE
                 total += jnp.dot(unit[:, at : at + KEEP * TILE], rhs, preferred_element_type=jnp.float32)
         acc[i] = total
@@ -102,7 +110,7 @@
         copy.wait()
 
 
-def ladder_rows(n_row, n_col, shifts, mask, units, ints, out_shape, out):
+def ladder_rows(n_row, n_col, kt_local, shifts, mask, units, ints, out_shape, out):
     rows, cols = units[0][0].shape[0], out_shape.shape[1]
     flat = [u for pair in units for u in pair]
     args = [mask, *flat, *ints]
@@ -113,13 +121,13 @@
         args.append(out)
         specs.append(_any)
     return pl.pallas_call(
-        functools.partial(ladder_kernel, n_row, n_col, shifts),
+        functools.partial(ladder_kernel, n_row, n_col, kt_local, shifts),
         out_shape=out_shape,
         in_specs=specs,
         out_specs=_any,
         scratch_shapes=[pltpu.VMEM((len(shifts), rows, cols), jnp.float32), pltpu.SemaphoreType.DMA((len(shifts),))],
         input_output_aliases=alias,
-        compiler_params=pltpu.CompilerParams(vmem_limit_bytes=VMEM_LIMIT),
+        compiler_params=_params,
     )(*args)
 
 
@@ -127,20 +135,19 @@
     rows, depth = amps.shape
     tile_rows, kblock = amplitude_tile_mask.shape
     kt_local = integrals.shape[0] // TILE
-    r, c = lax.axis_index("row"), lax.axis_index("col")
-
-    sparse_ints = pl.pallas_call(
-        mask_ints_kernel,
-        out_shape=jax.ShapeDtypeStruct(integrals.shape, integrals.dtype),
-        in_specs=[_smem, _vmem],
-        out_specs=_vmem,
-        compiler_params=pltpu.CompilerParams(vmem_limit_bytes=VMEM_LIMIT),
-    )(integral_tile_mask, integrals)
-    ints = [None] * n_row
-    for j in range(0, n_row, 2):
-        ints[j] = sparse_ints if j == 0 else lax.ppermute(sparse_ints, "row", [(i, i ^ j) for i in range(n_row)])
-    for j in range(0, n_row, 2):
-        ints[j + 1] = lax.ppermute(ints[j], "row", [(i, i ^ 1) for i in range(n_row)])
+    n_groups = kt_local // GROUP
+    c = lax.axis_index("col")
+    piece = jax.ShapeDtypeStruct((GROUP * TILE, integrals.shape[1]), integrals.dtype)
+
+    def masked_ints(x):
+        return pl.pallas_call(
+            mask_ints_kernel,
+            out_shape=[piece] * n_groups,
+            in_specs=[_smem, _hbm],
+            out_specs=[_vmem] * n_groups,
+            scratch_shapes=[pltpu.VMEM((n_groups, *piece.shape), piece.dtype), pltpu.SemaphoreType.DMA((n_groups,))],
+            compiler_params=_params,
+        )(integral_tile_mask.T, x)
 
     mine = lax.broadcasted_iota(jnp.int32, (tile_rows, n_col * kblock), 1) // kblock == c
     mask = lax.psum(jnp.where(mine, jnp.tile(amplitude_tile_mask, (1, n_col)), 0), "col")
@@ -149,10 +156,10 @@
     own = pl.pallas_call(
         functools.partial(compress_kernel, n_row, kt_local),
         out_shape=[jax.ShapeDtypeStruct(half, amps.dtype)] * 2,
-        in_specs=[_smem, _any],
+        in_specs=[_smem, _hbm],
         out_specs=[_vmem] * 2,
         scratch_shapes=[pltpu.SemaphoreType.DMA((depth // TILE * KEEP // GROUP,))],
-        compiler_params=pltpu.CompilerParams(vmem_limit_bytes=VMEM_LIMIT),
+        compiler_params=_params,
     )(mask, amps)
 
     order = [2 * p if p < n_col // 2 else 2 * (n_col - 1 - p) + 1 for p in range(n_col)]
@@ -160,21 +167,44 @@
     down = [(d, s) for s, d in up]
     out_shape = jax.ShapeDtypeStruct((rows * n_col, integrals.shape[1]), jnp.float32)
 
-    fwd, bwd = own, own
-    held = {0: own}
-    for k in range(1, n_col // 2):
-        nf, nb = [], []
-        for h in range(2):
-            nf.append(lax.ppermute(fwd[h], "col", up))
-            nb.append(lax.ppermute(bwd[h], "col", down))
-        fwd, bwd = nf, nb
-        held[k], held[n_col - k] = fwd, bwd
-    held[n_col // 2] = [lax.ppermute(fwd[0], "col", up), lax.ppermute(bwd[1], "col", down)]
+    last = n_col // 2
+    held = {k: [None, None] for k in range(n_col)}
+    held[0] = list(own)
+    turns = [(k, t) for k in range(1, last + 1) for t in range(2 if k < last else 1)]
+    for k, t in turns:
+        b = (n_col - k) % n_col
+        held[k][t] = lax.ppermute(held[k - 1][t], "col", up)
+        held[b][1 - t] = lax.ppermute(held[(b + 1) % n_col][1 - t], "col", down)
+
+    def after(turn, values):
+        if turn is None:
+            return values
+        k, t = turns[turn]
+        b = (n_col - k) % n_col
+        *values, held[k][t], held[b][1 - t] = lax.optimization_barrier((*values, held[k][t], held[b][1 - t]))
+        return values
+
+    def swap(x, j):
+        return lax.ppermute(x, "row", [(i, i ^ j) for i in range(n_row)])
+
+    x = integrals
+    if True:
+        own = list(own)
+        x, own[0], own[1] = lax.optimization_barrier((x, own[0], own[1]))
+        held[0] = [own[0], own[1]]
+    pieces = {0: list(masked_ints(x))}
+    for j in range(2, n_row, 2):
+        pieces[j] = list((swap(p, j) for p in pieces[0]))
+    for j in range(0, n_row, 2):
+        pieces[j + 1] = [None] * n_groups
+        for g in range(n_groups):
+            (pieces[j][g],) = after({(0, 0): 1, (0, 1): 2, (2, 0): 3, (2, 1): 4}[(min(j, 2), g)], (pieces[j][g],))
+            pieces[j + 1][g] = swap(pieces[j][g], 1)
+    ints = [p for j in range(n_row) for p in pieces[j]]
 
     out = None
-    groups = [(0, 1, n_col - 1)] + [(k, n_col - k) for k in range(2, n_col // 2)] + [(n_col // 2,)]
-    for shifts in groups:
-        out = ladder_rows(n_row, n_col, shifts, mask, [held[s] for s in shifts], ints, out_shape, out)
+    for shifts in [(0, 1, n_col - 1)] + [(k, n_col - k) for k in range(2, last)] + [(last,)]:
+        out = ladder_rows(n_row, n_col, kt_local, shifts, mask, [held[s] for s in shifts], ints, out_shape, out)
     return out
 
 

time: 70.3 us -> 63.5 us (0.903)
  waiting for transfers between devices: 27.1 us -> 18.3 us
  local copies, waits for them, and re-layouts: 2.07 us -> 3.88 us
  blocking collectives: 11.6 us -> 13.1 us
  starting transfers between devices: 18.8 us -> 17.7 us
    ppermute x17 -> x20, waiting for transfers between devices: 27.1 us -> 18.3 us  [the longest x7 14 us: on_device(): held[k][t] = lax.ppermute(held[k - 1][t], 'col', up)]
    psum x1, blocking collectives: 11.6 us -> 13.1 us  [on_device(): lax.psum(jnp.where(mine, jnp.tile(amplitude_tile_mask, (1, n_col)), 0), '...]
    ppermute x17 -> x20, starting transfers between devices: 18.8 us -> 17.7 us  [the longest x7 10.5 us: on_device(): held[b][1 - t] = lax.ppermute(held[(b + 1) % n_col][1 - t], 'col', down)]
    unnamed x7 -> x6, local copies, waits for them, and re-layouts: 2 us -> 3.13 us
  transfers between devices with their start and end apart: 17 -> 20, of which waited for: 8 -> 11; matrix products, arithmetic and copies ran while one was open for 0% -> 0% of each run, Pallas kernels for 11% -> 12%
where the time goes in v2:
time: 63.5 us; the launch traced here: 63.3 us
  waiting for transfers between devices  18.3 us (29%)
  starting transfers between devices  17.7 us (28%)
  blocking collectives  13.1 us (21%)
  Pallas kernels  10.3 us (16%)
  local copies, waits for them, and re-layouts  3.88 us (6%)
    ppermute x7, waiting for transfers between devices, on_device(): held[k][t] = lax.ppermute(held[k - 1][t], 'col', up)  14 us
    psum x1, blocking collectives, on_device(): lax.psum(jnp.where(mine, jnp.tile(amplitude_tile_mask, (1, n_col)), 0), '...  13.1 us
    ppermute x7, starting transfers between devices, on_device(): held[b][1 - t] = lax.ppermute(held[(b + 1) % n_col][1 - t], 'col', down)  10.5 us
    pallas_call x4, Pallas kernels, ladder_rows(): pl.pallas_call(functools.partial(ladder_kernel, n_row, n_col, kt_local, s...  8.32 us
    ppermute x7, waiting for transfers between devices, on_device(): held[b][1 - t] = lax.ppermute(held[(b + 1) % n_col][1 - t], 'col', down)  4.29 us
    ppermute x7, starting transfers between devices, on_device(): held[k][t] = lax.ppermute(held[k - 1][t], 'col', up)  3.63 us
    ppermute x6, starting transfers between devices, swap(): return lax.ppermute(x, 'row', [(i, i ^ j) for i in range(n_row)])  3.52 us
    unnamed x6, local copies, waits for them, and re-layouts  3.13 us
  transfers between devices with their start and end apart: 20, of which 11 were waited for; matrix products, arithmetic and copies ran while one was open for 0% of the time, Pallas kernels for 12%

profile of v2, /device:TPU:0, one launch (start us, length us, event | category | flops | bytes accessed | tf_op | source)
XLA Modules:
  0.0 63.3 jit_solution(1242654385031959461)
XLA Ops:
  0.8 13.1 %psum.7.mask_ref = s32[8,32]{1,0:T(8,128)S(1)} all-reduce(s32[8,32]{1,0:T(8,128)S(1)} %fusion), channel_id=1, replica_groups=mesh['row'=4,'col'=8] {'col'}, use_global_device_ids=true, to_apply=%region_0.1 | all-reduce | flops 256 | bytes 2048 | tf_op jit(solution)/shard_map/psum | solution.py:153
  13.8 1.2 %copy-done = bf16[128,4096]{1,0:T(8,128)(2,1)S(1)} copy-done((bf16[128,4096]{1,0:T(8,128)(2,1)S(1)}, bf16[128,4096]{1,0:T(8,128)(2,1)}, u32[]{:S(2)}) %copy-start) | copy-done | bytes 1048600
  15.1 1.1 %shard_map.46 = (bf16[128,1024]{1,0:T(8,128)(2,1)S(1)}, bf16[128,1024]{1,0:T(8,128)(2,1)S(1)}) custom-call(s32[8,32]{1,0:T(8,128)S(1)} %psum.7.mask_ref, bf16[128,4096]{1,0:T(8,128)(2,1)S(1)} %copy-done), custom_call_target="tpu_custom_call" | custom-call | tf_op jit(solution)/shard_map/pallas_call | solution.py:156
  16.6 1.6 %collective-permute-start.4 = (bf16[128,1024]{1,0:T(8,128)(2,1)S(1)}, bf16[128,1024]{1,0:T(8,128)(2,1)S(1)}, u32[]{:S(2)}, u32[]{:S(2)}) collective-permute-start(bf16[128,1024]{1,0:T(8,128)(2,1)S(1)} %get-tuple-element.40.refs_1_), channel_id=1, source_target_pairs={{2,0},{4,2},{6,4},{7,6},{5,7},{3,5},{1,3},{0,1},{10,8},{12,10},{14... | collective-permute-start | bytes 786440 | tf_op jit(solution)/shard_map/ppermute | solution.py:177
  18.7 1.2 %copy-done.1 = bf16[1024,512]{1,0:T(8,128)(2,1)S(1)} copy-done((bf16[1024,512]{1,0:T(8,128)(2,1)S(1)}, bf16[1024,512]{1,0:T(8,128)(2,1)}, u32[]{:S(2)}) %copy-start.1) | copy-done | bytes 1048600
  20.6 0.9 %shard_map.47 = (bf16[512,512]{1,0:T(8,128)(2,1)S(1)}, bf16[512,512]{1,0:T(8,128)(2,1)S(1)}) custom-call(s32[4,8]{1,0:T(4,128)S(1)} %bitcast.2, bf16[1024,512]{1,0:T(8,128)(2,1)S(1)} %copy-done.1), custom_call_target="tpu_custom_call" | custom-call | tf_op jit(solution)/shard_map/pallas_call | solution.py:143
  21.5 1.6 %collective-permute-start.12 = (bf16[512,512]{1,0:T(8,128)(2,1)S(1)}, bf16[512,512]{1,0:T(8,128)(2,1)S(1)}, u32[]{:S(2)}, u32[]{:S(2)}) collective-permute-start(bf16[512,512]{1,0:T(8,128)(2,1)S(1)} %get-tuple-element.28.refs_6_.refs_4_.refs_2_), channel_id=1, source_target_pairs={{0,16},{8,24},{16,0},{24,8},{1,17},{9,25},{17,1},{25,9},{2,18},{10... | collective-permute-start | bytes 1572872 | tf_op jit(solution)/shard_map/ppermute | solution.py:188
  23.0 1.6 %collective-permute-start.9 = (bf16[128,1024]{1,0:T(8,128)(2,1)S(1)}, bf16[128,1024]{1,0:T(8,128)(2,1)S(1)}, u32[]{:S(2)}, u32[]{:S(2)}) collective-permute-start(bf16[128,1024]{1,0:T(8,128)(2,1)S(1)} %get-tuple-element.39.refs_0_), channel_id=1, source_target_pairs={{2,0},{4,2},{6,4},{7,6},{5,7},{3,5},{1,3},{0,1},{10,8},{12,10},{14... | collective-permute-start | bytes 786440 | tf_op jit(solution)/shard_map/ppermute | solution.py:177
  25.9 1.5 %collective-permute-start.15 = (bf16[512,512]{1,0:T(8,128)(2,1)S(1)}, bf16[512,512]{1,0:T(8,128)(2,1)S(1)}, u32[]{:S(2)}, u32[]{:S(2)}) collective-permute-start(bf16[512,512]{1,0:T(8,128)(2,1)S(1)} %get-tuple-element.30.refs_7_.refs_5_.refs_3_), channel_id=1, source_target_pairs={{0,16},{8,24},{16,0},{24,8},{1,17},{9,25},{17,1},{25,9},{2,18},{10... | collective-permute-start | bytes 1572872 | tf_op jit(solution)/shard_map/ppermute | solution.py:188
  27.4 3.6 %collective-permute-done.8.refs_3_ = bf16[128,1024]{1,0:T(8,128)(2,1)S(1)} collective-permute-done((bf16[128,1024]{1,0:T(8,128)(2,1)S(1)}, bf16[128,1024]{1,0:T(8,128)(2,1)S(1)}, u32[]{:S(2)}, u32[]{:S(2)}) %collective-permute-start.8) | collective-permute-done | bytes 262176 | tf_op jit(solution)/shard_map/ppermute | solution.py:176
  30.9 1.5 %collective-permute-start.5 = (bf16[128,1024]{1,0:T(8,128)(2,1)S(1)}, bf16[128,1024]{1,0:T(8,128)(2,1)S(1)}, u32[]{:S(2)}, u32[]{:S(2)}) collective-permute-start(bf16[128,1024]{1,0:T(8,128)(2,1)S(1)} %collective-permute-done.4.refs_5_), channel_id=1, source_target_pairs={{2,0},{4,2},{6,4},{7,6},{5,7},{3,5},{1,3},{0,1},{10,8},{12,10},{14... | collective-permute-start | bytes 786440 | tf_op jit(solution)/shard_map/ppermute | solution.py:177
  33.0 3.6 %collective-permute-done.1.refs_0_ = bf16[128,1024]{1,0:T(8,128)(2,1)S(1)} collective-permute-done((bf16[128,1024]{1,0:T(8,128)(2,1)S(1)}, bf16[128,1024]{1,0:T(8,128)(2,1)S(1)}, u32[]{:S(2)}, u32[]{:S(2)}) %collective-permute-start.1) | collective-permute-done | bytes 262176 | tf_op jit(solution)/shard_map/ppermute | solution.py:176
  36.6 1.5 %collective-permute-start.14 = (bf16[128,1024]{1,0:T(8,128)(2,1)S(1)}, bf16[128,1024]{1,0:T(8,128)(2,1)S(1)}, u32[]{:S(2)}, u32[]{:S(2)}) collective-permute-start(bf16[128,1024]{1,0:T(8,128)(2,1)S(1)} %collective-permute-done.9.refs_4_), channel_id=1, source_target_pairs={{2,0},{4,2},{6,4},{7,6},{5,7},{3,5},{1,3},{0,1},{10,8},{12,10},{14... | collective-permute-start | bytes 786440 | tf_op jit(solution)/shard_map/ppermute | solution.py:177
  38.0 1.8 %collective-permute-done.5.refs_3_ = bf16[128,1024]{1,0:T(8,128)(2,1)S(1)} collective-permute-done((bf16[128,1024]{1,0:T(8,128)(2,1)S(1)}, bf16[128,1024]{1,0:T(8,128)(2,1)S(1)}, u32[]{:S(2)}, u32[]{:S(2)}) %collective-permute-start.5) | collective-permute-done | bytes 262176 | tf_op jit(solution)/shard_map/ppermute | solution.py:177
  40.6 1.3 %collective-permute-start.6 = (bf16[128,1024]{1,0:T(8,128)(2,1)S(1)}, bf16[128,1024]{1,0:T(8,128)(2,1)S(1)}, u32[]{:S(2)}, u32[]{:S(2)}) collective-permute-start(bf16[128,1024]{1,0:T(8,128)(2,1)S(1)} %collective-permute-done.5.refs_3_), channel_id=1, source_target_pairs={{2,0},{4,2},{6,4},{7,6},{5,7},{3,5},{1,3},{0,1},{10,8},{12,10},{14... | collective-permute-start | bytes 786440 | tf_op jit(solution)/shard_map/ppermute | solution.py:177
  41.9 1.0 %collective-permute-done.14.refs_2_ = bf16[128,1024]{1,0:T(8,128)(2,1)S(1)} collective-permute-done((bf16[128,1024]{1,0:T(8,128)(2,1)S(1)}, bf16[128,1024]{1,0:T(8,128)(2,1)S(1)}, u32[]{:S(2)}, u32[]{:S(2)}) %collective-permute-start.14) | collective-permute-done | bytes 262176 | tf_op jit(solution)/shard_map/ppermute | solution.py:177
  43.4 2.8 %collective-permute-done.2.refs_0_ = bf16[128,1024]{1,0:T(8,128)(2,1)S(1)} collective-permute-done((bf16[128,1024]{1,0:T(8,128)(2,1)S(1)}, bf16[128,1024]{1,0:T(8,128)(2,1)S(1)}, u32[]{:S(2)}, u32[]{:S(2)}) %collective-permute-start.2) | collective-permute-done | bytes 262176 | tf_op jit(solution)/shard_map/ppermute | solution.py:176
  47.4 1.6 %collective-permute-start.19 = (bf16[128,1024]{1,0:T(8,128)(2,1)S(1)}, bf16[128,1024]{1,0:T(8,128)(2,1)S(1)}, u32[]{:S(2)}, u32[]{:S(2)}) collective-permute-start(bf16[128,1024]{1,0:T(8,128)(2,1)S(1)} %collective-permute-done.14.refs_2_), channel_id=1, source_target_pairs={{2,0},{4,2},{6,4},{7,6},{5,7},{3,5},{1,3},{0,1},{10,8},{12,10},{14... | collective-permute-start | bytes 786440 | tf_op jit(solution)/shard_map/ppermute | solution.py:177
  49.5 1.6 %collective-permute-start.7 = (bf16[128,1024]{1,0:T(8,128)(2,1)S(1)}, bf16[128,1024]{1,0:T(8,128)(2,1)S(1)}, u32[]{:S(2)}, u32[]{:S(2)}) collective-permute-start(bf16[128,1024]{1,0:T(8,128)(2,1)S(1)} %collective-permute-done.6.refs_3_), channel_id=1, source_target_pairs={{2,0},{4,2},{6,4},{7,6},{5,7},{3,5},{1,3},{0,1},{10,8},{12,10},{14... | collective-permute-start | bytes 786440 | tf_op jit(solution)/shard_map/ppermute | solution.py:177
  51.0 2.4 %shard_map.48.refs_12_ = f32[1024,512]{1,0:T(8,128)} custom-call(s32[8,32]{1,0:T(8,128)S(1)} %psum.7.mask_ref, bf16[128,1024]{1,0:T(8,128)(2,1)S(1)} %get-tuple-element.39.refs_0_, bf16[128,1024]{1,0:T(8,128)(2,1)S(1)} %get-tuple-element.40.refs_1_, bf16[128,1024]{1,0:T(8,128)(2,1)S(1)} %collective-permute-done.refs_2_, ...), custom_call_target="tpu_custom_call" | custom-call | tf_op jit(solution)/shard_map/pallas_call | solution.py:123
  53.4 2.1 %shard_map.49.refs_12_ = f32[1024,512]{1,0:T(8,128)} custom-call(s32[8,32]{1,0:T(8,128)S(1)} %psum.7.mask_ref, bf16[128,1024]{1,0:T(8,128)(2,1)S(1)} %collective-permute-done.1.refs_0_, bf16[128,1024]{1,0:T(8,128)(2,1)S(1)} %collective-permute-done.13.refs_1_, ...), custom_call_target="tpu_custom_call", output_to_operand_aliasing={{}: (13, {})} | custom-call | tf_op jit(solution)/shard_map/pallas_call | solution.py:123
  56.6 2.1 %shard_map.50.refs_10_ = f32[1024,512]{1,0:T(8,128)} custom-call(s32[8,32]{1,0:T(8,128)S(1)} %psum.7.mask_ref, bf16[128,1024]{1,0:T(8,128)(2,1)S(1)} %collective-permute-done.2.refs_0_, bf16[128,1024]{1,0:T(8,128)(2,1)S(1)} %collective-permute-done.18.refs_1_, ...), custom_call_target="tpu_custom_call", output_to_operand_aliasing={{}: (13, {})} | custom-call | tf_op jit(solution)/shard_map/pallas_call | solution.py:123
  58.7 2.6 %collective-permute-done.3.refs_0_ = bf16[128,1024]{1,0:T(8,128)(2,1)S(1)} collective-permute-done((bf16[128,1024]{1,0:T(8,128)(2,1)S(1)}, bf16[128,1024]{1,0:T(8,128)(2,1)S(1)}, u32[]{:S(2)}, u32[]{:S(2)}) %collective-permute-start.3) | collective-permute-done | bytes 262176 | tf_op jit(solution)/shard_map/ppermute | solution.py:176
  61.5 1.8 %shard_map.51 = f32[1024,512]{1,0:T(8,128)} custom-call(s32[8,32]{1,0:T(8,128)S(1)} %psum.7.mask_ref, bf16[128,1024]{1,0:T(8,128)(2,1)S(1)} %collective-permute-done.3.refs_0_, bf16[128,1024]{1,0:T(8,128)(2,1)S(1)} %collective-permute-done.7.refs_1_, bf16[512,512]{1,0:T(8,128)(2,1)S(1)} %get-tuple-element.28.refs_6_.refs_4_.refs_2_, ...), custom_call_target="tpu_custom_call", output_to_operand_aliasing={{}: (11, {})} | custom-call | tf_op jit(solution)/shard_map/pallas_call | solution.py:123
  (34 shorter events, 8.4 us)
Async XLA Ops:
  13.8 1.2 %copy-start = (bf16[128,4096]{1,0:T(8,128)(2,1)S(1)}, bf16[128,4096]{1,0:T(8,128)(2,1)}, u32[]{:S(2)}) copy-start(bf16[128,4096]{1,0:T(8,128)(2,1)} %a_ref.1) | copy-start | bytes 3145732
  16.1 9.3 %collective-permute-start = (bf16[128,1024]{1,0:T(8,128)(2,1)S(1)}, bf16[128,1024]{1,0:T(8,128)(2,1)S(1)}, u32[]{:S(2)}, u32[]{:S(2)}) collective-permute-start(bf16[128,1024]{1,0:T(8,128)(2,1)S(1)} %get-tuple-element.39.refs_0_), channel_id=1, source_target_pairs={{0,2},{2,4},{4,6},{6,7},{7,5},{5,3},{3,1},{1,0},{8,10},{10,12},{12... | collective-permute-start | bytes 786440 | tf_op jit(solution)/shard_map/ppermute | solution.py:176
  16.6 9.2 %collective-permute-start.4 = (bf16[128,1024]{1,0:T(8,128)(2,1)S(1)}, bf16[128,1024]{1,0:T(8,128)(2,1)S(1)}, u32[]{:S(2)}, u32[]{:S(2)}) collective-permute-start(bf16[128,1024]{1,0:T(8,128)(2,1)S(1)} %get-tuple-element.40.refs_1_), channel_id=1, source_target_pairs={{2,0},{4,2},{6,4},{7,6},{5,7},{3,5},{1,3},{0,1},{10,8},{12,10},{14... | collective-permute-start | bytes 786440 | tf_op jit(solution)/shard_map/ppermute | solution.py:177
  18.2 12.7 %collective-permute-start.8 = (bf16[128,1024]{1,0:T(8,128)(2,1)S(1)}, bf16[128,1024]{1,0:T(8,128)(2,1)S(1)}, u32[]{:S(2)}, u32[]{:S(2)}) collective-permute-start(bf16[128,1024]{1,0:T(8,128)(2,1)S(1)} %get-tuple-element.40.refs_1_), channel_id=1, source_target_pairs={{0,2},{2,4},{4,6},{6,7},{7,5},{5,3},{3,1},{1,0},{8,10},{10,12},{12... | collective-permute-start | bytes 786440 | tf_op jit(solution)/shard_map/ppermute | solution.py:176
  18.7 1.2 %copy-start.1 = (bf16[1024,512]{1,0:T(8,128)(2,1)S(1)}, bf16[1024,512]{1,0:T(8,128)(2,1)}, u32[]{:S(2)}) copy-start(bf16[1024,512]{1,0:T(8,128)(2,1)} %x_ref) | copy-start | bytes 3145732
  19.9 0.7 %copy-start.2 = (s32[8,4]{0,1:T(4,128)S(1)}, s32[8,4]{0,1:T(4,128)}, u32[]{:S(2)}) copy-start(s32[8,4]{0,1:T(4,128)} %param.7) | copy-start | bytes 388
  21.5 19.1 %collective-permute-start.12 = (bf16[512,512]{1,0:T(8,128)(2,1)S(1)}, bf16[512,512]{1,0:T(8,128)(2,1)S(1)}, u32[]{:S(2)}, u32[]{:S(2)}) collective-permute-start(bf16[512,512]{1,0:T(8,128)(2,1)S(1)} %get-tuple-element.28.refs_6_.refs_4_.refs_2_), channel_id=1, source_target_pairs={{0,16},{8,24},{16,0},{24,8},{1,17},{9,25},{17,1},{25,9},{2,18},{10... | collective-permute-start | bytes 1572872 | tf_op jit(solution)/shard_map/ppermute | solution.py:188
  23.0 9.4 %collective-permute-start.9 = (bf16[128,1024]{1,0:T(8,128)(2,1)S(1)}, bf16[128,1024]{1,0:T(8,128)(2,1)S(1)}, u32[]{:S(2)}, u32[]{:S(2)}) collective-permute-start(bf16[128,1024]{1,0:T(8,128)(2,1)S(1)} %get-tuple-element.39.refs_0_), channel_id=1, source_target_pairs={{2,0},{4,2},{6,4},{7,6},{5,7},{3,5},{1,3},{0,1},{10,8},{12,10},{14... | collective-permute-start | bytes 786440 | tf_op jit(solution)/shard_map/ppermute | solution.py:177
  25.4 11.1 %collective-permute-start.1 = (bf16[128,1024]{1,0:T(8,128)(2,1)S(1)}, bf16[128,1024]{1,0:T(8,128)(2,1)S(1)}, u32[]{:S(2)}, u32[]{:S(2)}) collective-permute-start(bf16[128,1024]{1,0:T(8,128)(2,1)S(1)} %collective-permute-done.refs_2_), channel_id=1, source_target_pairs={{0,2},{2,4},{4,6},{6,7},{7,5},{5,3},{3,1},{1,0},{8,10},{10,12},{12... | collective-permute-start | bytes 786440 | tf_op jit(solution)/shard_map/ppermute | solution.py:176
  25.9 17.1 %collective-permute-start.15 = (bf16[512,512]{1,0:T(8,128)(2,1)S(1)}, bf16[512,512]{1,0:T(8,128)(2,1)S(1)}, u32[]{:S(2)}, u32[]{:S(2)}) collective-permute-start(bf16[512,512]{1,0:T(8,128)(2,1)S(1)} %get-tuple-element.30.refs_7_.refs_5_.refs_3_), channel_id=1, source_target_pairs={{0,16},{8,24},{16,0},{24,8},{1,17},{9,25},{17,1},{25,9},{2,18},{10... | collective-permute-start | bytes 1572872 | tf_op jit(solution)/shard_map/ppermute | solution.py:188
  30.9 8.9 %collective-permute-start.5 = (bf16[128,1024]{1,0:T(8,128)(2,1)S(1)}, bf16[128,1024]{1,0:T(8,128)(2,1)S(1)}, u32[]{:S(2)}, u32[]{:S(2)}) collective-permute-start(bf16[128,1024]{1,0:T(8,128)(2,1)S(1)} %collective-permute-done.4.refs_5_), channel_id=1, source_target_pairs={{2,0},{4,2},{6,4},{7,6},{5,7},{3,5},{1,3},{0,1},{10,8},{12,10},{14... | collective-permute-start | bytes 786440 | tf_op jit(solution)/shard_map/ppermute | solution.py:177
  32.4 9.5 %collective-permute-start.13 = (bf16[128,1024]{1,0:T(8,128)(2,1)S(1)}, bf16[128,1024]{1,0:T(8,128)(2,1)S(1)}, u32[]{:S(2)}, u32[]{:S(2)}) collective-permute-start(bf16[128,1024]{1,0:T(8,128)(2,1)S(1)} %collective-permute-done.8.refs_3_), channel_id=1, source_target_pairs={{0,2},{2,4},{4,6},{6,7},{7,5},{5,3},{3,1},{1,0},{8,10},{10,12},{12... | collective-permute-start | bytes 786440 | tf_op jit(solution)/shard_map/ppermute | solution.py:176
  36.6 6.4 %collective-permute-start.14 = (bf16[128,1024]{1,0:T(8,128)(2,1)S(1)}, bf16[128,1024]{1,0:T(8,128)(2,1)S(1)}, u32[]{:S(2)}, u32[]{:S(2)}) collective-permute-start(bf16[128,1024]{1,0:T(8,128)(2,1)S(1)} %collective-permute-done.9.refs_4_), channel_id=1, source_target_pairs={{2,0},{4,2},{6,4},{7,6},{5,7},{3,5},{1,3},{0,1},{10,8},{12,10},{14... | collective-permute-start | bytes 786440 | tf_op jit(solution)/shard_map/ppermute | solution.py:177
  39.9 6.4 %collective-permute-start.2 = (bf16[128,1024]{1,0:T(8,128)(2,1)S(1)}, bf16[128,1024]{1,0:T(8,128)(2,1)S(1)}, u32[]{:S(2)}, u32[]{:S(2)}) collective-permute-start(bf16[128,1024]{1,0:T(8,128)(2,1)S(1)} %collective-permute-done.1.refs_0_), channel_id=1, source_target_pairs={{0,2},{2,4},{4,6},{6,7},{7,5},{5,3},{3,1},{1,0},{8,10},{10,12},{12... | collective-permute-start | bytes 786440 | tf_op jit(solution)/shard_map/ppermute | solution.py:176
  40.6 6.4 %collective-permute-start.6 = (bf16[128,1024]{1,0:T(8,128)(2,1)S(1)}, bf16[128,1024]{1,0:T(8,128)(2,1)S(1)}, u32[]{:S(2)}, u32[]{:S(2)}) collective-permute-start(bf16[128,1024]{1,0:T(8,128)(2,1)S(1)} %collective-permute-done.5.refs_3_), channel_id=1, source_target_pairs={{2,0},{4,2},{6,4},{7,6},{5,7},{3,5},{1,3},{0,1},{10,8},{12,10},{14... | collective-permute-start | bytes 786440 | tf_op jit(solution)/shard_map/ppermute | solution.py:177
  41.9 5.5 %collective-permute-start.10 = (bf16[512,512]{1,0:T(8,128)(2,1)S(1)}, bf16[512,512]{1,0:T(8,128)(2,1)S(1)}, u32[]{:S(2)}, u32[]{:S(2)}) collective-permute-start(bf16[512,512]{1,0:T(8,128)(2,1)S(1)} %get-tuple-element.28.refs_6_.refs_4_.refs_2_), channel_id=1, source_target_pairs={{0,8},{8,0},{16,24},{24,16},{1,9},{9,1},{17,25},{25,17},{2,10},{10... | collective-permute-start | bytes 1572872 | tf_op jit(solution)/shard_map/ppermute | solution.py:188
  42.9 6.1 %collective-permute-start.16 = (bf16[512,512]{1,0:T(8,128)(2,1)S(1)}, bf16[512,512]{1,0:T(8,128)(2,1)S(1)}, u32[]{:S(2)}, u32[]{:S(2)}) collective-permute-start(bf16[512,512]{1,0:T(8,128)(2,1)S(1)} %collective-permute-done.12.refs_10_.refs_8_.refs_6_), channel_id=1, source_target_pairs={{0,8},{8,0},{16,24},{24,16},{1,9},{9,1},{17,25},{25,17},{2,10},{10... | collective-permute-start | bytes 1572872 | tf_op jit(solution)/shard_map/ppermute | solution.py:188
  43.0 6.5 %collective-permute-start.11 = (bf16[512,512]{1,0:T(8,128)(2,1)S(1)}, bf16[512,512]{1,0:T(8,128)(2,1)S(1)}, u32[]{:S(2)}, u32[]{:S(2)}) collective-permute-start(bf16[512,512]{1,0:T(8,128)(2,1)S(1)} %get-tuple-element.30.refs_7_.refs_5_.refs_3_), channel_id=1, source_target_pairs={{0,8},{8,0},{16,24},{24,16},{1,9},{9,1},{17,25},{25,17},{2,10},{10... | collective-permute-start | bytes 1572872 | tf_op jit(solution)/shard_map/ppermute | solution.py:188
  47.0 4.1 %collective-permute-start.17 = (bf16[512,512]{1,0:T(8,128)(2,1)S(1)}, bf16[512,512]{1,0:T(8,128)(2,1)S(1)}, u32[]{:S(2)}, u32[]{:S(2)}) collective-permute-start(bf16[512,512]{1,0:T(8,128)(2,1)S(1)} %collective-permute-done.15.refs_11_.refs_9_.refs_7_), channel_id=1, source_target_pairs={{0,8},{8,0},{16,24},{24,16},{1,9},{9,1},{17,25},{25,17},{2,10},{10... | collective-permute-start | bytes 1572872 | tf_op jit(solution)/shard_map/ppermute | solution.py:188
  47.0 9.1 %collective-permute-start.18 = (bf16[128,1024]{1,0:T(8,128)(2,1)S(1)}, bf16[128,1024]{1,0:T(8,128)(2,1)S(1)}, u32[]{:S(2)}, u32[]{:S(2)}) collective-permute-start(bf16[128,1024]{1,0:T(8,128)(2,1)S(1)} %collective-permute-done.13.refs_1_), channel_id=1, source_target_pairs={{0,2},{2,4},{4,6},{6,7},{7,5},{5,3},{3,1},{1,0},{8,10},{10,12},{12... | collective-permute-start | bytes 786440 | tf_op jit(solution)/shard_map/ppermute | solution.py:176
  47.4 9.1 %collective-permute-start.19 = (bf16[128,1024]{1,0:T(8,128)(2,1)S(1)}, bf16[128,1024]{1,0:T(8,128)(2,1)S(1)}, u32[]{:S(2)}, u32[]{:S(2)}) collective-permute-start(bf16[128,1024]{1,0:T(8,128)(2,1)S(1)} %collective-permute-done.14.refs_2_), channel_id=1, source_target_pairs={{2,0},{4,2},{6,4},{7,6},{5,7},{3,5},{1,3},{0,1},{10,8},{12,10},{14... | collective-permute-start | bytes 786440 | tf_op jit(solution)/shard_map/ppermute | solution.py:177
  49.0 12.3 %collective-permute-start.3 = (bf16[128,1024]{1,0:T(8,128)(2,1)S(1)}, bf16[128,1024]{1,0:T(8,128)(2,1)S(1)}, u32[]{:S(2)}, u32[]{:S(2)}) collective-permute-start(bf16[128,1024]{1,0:T(8,128)(2,1)S(1)} %collective-permute-done.2.refs_0_), channel_id=1, source_target_pairs={{0,2},{2,4},{4,6},{6,7},{7,5},{5,3},{3,1},{1,0},{8,10},{10,12},{12... | collective-permute-start | bytes 786440 | tf_op jit(solution)/shard_map/ppermute | solution.py:176
  49.5 12.0 %collective-permute-start.7 = (bf16[128,1024]{1,0:T(8,128)(2,1)S(1)}, bf16[128,1024]{1,0:T(8,128)(2,1)S(1)}, u32[]{:S(2)}, u32[]{:S(2)}) collective-permute-start(bf16[128,1024]{1,0:T(8,128)(2,1)S(1)} %collective-permute-done.6.refs_3_), channel_id=1, source_target_pairs={{2,0},{4,2},{6,4},{7,6},{5,7},{3,5},{1,3},{0,1},{10,8},{12,10},{14... | collective-permute-start | bytes 786440 | tf_op jit(solution)/shard_map/ppermute | solution.py:177

commit v3 on v2

--- a/solution.py
+++ b/solution.py
@@ -80,37 +80,62 @@
         copy.wait()
 
 
-def ladder_kernel(n_row, n_col, kt_local, shifts, mask_ref, *refs):
+def ladder_kernel(n_row, n_col, kt_local, shifts, ahead, mask_ref, *refs):
     n_units = 2 * len(shifts)
-    units, ints = refs[:n_units], refs[n_units:]
-    o_ref, acc, sem = refs[-3:]
+    n_ints = n_row * (kt_local // GROUP)
+    units, ints = refs[:n_units], refs[n_units : n_units + n_ints]
+    acc, sem = refs[-2:]
+    o_ref, next_ref = (refs[-3], None) if ahead is None else (refs[-4], refs[-3])
     rows = units[0].shape[0]
     per_unit = n_row // 2
     r, c = lax.axis_index("row"), lax.axis_index("col")
-    pos = ring_pos(c, n_col)
+
+    def source(shift):
+        return ring_chip(lax.rem(ring_pos(c, n_col) + (n_col - shift), n_col), n_col)
+
+    def tiles(row, j, g):
+        first = (jnp.bitwise_xor(r, j) * (kt_local // GROUP) + g) * GROUP
+        held = ints[j * (kt_local // GROUP) + g]
+        return [held[pl.ds(pl.multiple_of(p * TILE, TILE), TILE), :] for p in picks(mask_ref, row, first)]
+
     copies = []
     for i, shift in enumerate(shifts):
-        src = ring_chip(lax.rem(pos + (n_col - shift), n_col), n_col)
-        row = src * rows // TILE
+        src = source(shift)
         total = jnp.zeros(acc.shape[1:], jnp.float32)
         for j in range(n_row):
-            block = jnp.bitwise_xor(r, j)
             unit, j_in = units[2 * i + j // per_unit], j % per_unit
             for g in range(kt_local // GROUP):
-                lo, hi = picks(mask_ref, row, block * kt_local + g * GROUP)
-                held = ints[j * (kt_local // GROUP) + g]
-                rhs = jnp.concatenate([held[pl.ds(pl.multiple_of(p * TILE, TILE), TILE), :] for p in (lo, hi)], axis=0)
+                rhs = jnp.concatenate(tiles(src * rows // TILE, j, g), axis=0)
                 at = (j_in * (kt_local // GROUP) + g) * KEEP * TILE
                 total += jnp.dot(unit[:, at : at + KEEP * TILE], rhs, preferred_element_type=jnp.float32)
         acc[i] = total
         copy = pltpu.make_async_copy(acc.at[i], o_ref.at[pl.ds(pl.multiple_of(src * rows, rows), rows), :], sem.at[i])
         copy.start()
         copies.append(copy)
+    if ahead is not None:
+        row = source(ahead) * rows // TILE
+        for j in range(n_row):
+            for g in range(kt_local // GROUP):
+                for s, tile in enumerate(tiles(row, j, g)):
+                    at = ((j * (kt_local // GROUP) + g) * KEEP + s) * TILE
+                    next_ref[at : at + TILE, :] = tile
     for copy in copies:
         copy.wait()
 
 
-def ladder_rows(n_row, n_col, kt_local, shifts, mask, units, ints, out_shape, out):
+def last_kernel(n_col, shift, *refs):
+    lo, hi, ints, _, o_ref, acc, sem = refs
+    rows, depth = lo.shape
+    pos = ring_pos(lax.axis_index("col"), n_col)
+    src = ring_chip(lax.rem(pos + (n_col - shift), n_col), n_col)
+    total = jnp.dot(lo[...], ints[:depth, :], preferred_element_type=jnp.float32)
+    acc[...] = total + jnp.dot(hi[...], ints[depth:, :], preferred_element_type=jnp.float32)
+    copy = pltpu.make_async_copy(acc, o_ref.at[pl.ds(pl.multiple_of(src * rows, rows), rows), :], sem)
+    copy.start()
+    copy.wait()
+
+
+def ladder_rows(n_row, n_col, kt_local, shifts, ahead, mask, units, ints, out_shape, out):
     rows, cols = units[0][0].shape[0], out_shape.shape[1]
     flat = [u for pair in units for u in pair]
     args = [mask, *flat, *ints]
@@ -120,11 +145,15 @@
         alias = {len(args): 0}
         args.append(out)
         specs.append(_any)
+    shapes, places = [out_shape], [_any]
+    if ahead is not None:
+        shapes.append(jax.ShapeDtypeStruct((2 * flat[0].shape[1], cols), ints[0].dtype))
+        places.append(_vmem)
     return pl.pallas_call(
-        functools.partial(ladder_kernel, n_row, n_col, kt_local, shifts),
-        out_shape=out_shape,
+        functools.partial(ladder_kernel, n_row, n_col, kt_local, shifts, ahead),
+        out_shape=shapes,
         in_specs=specs,
-        out_specs=_any,
+        out_specs=places,
         scratch_shapes=[pltpu.VMEM((len(shifts), rows, cols), jnp.float32), pltpu.SemaphoreType.DMA((len(shifts),))],
         input_output_aliases=alias,
         compiler_params=_params,
@@ -147,7 +176,7 @@
             out_specs=[_vmem] * n_groups,
             scratch_shapes=[pltpu.VMEM((n_groups, *piece.shape), piece.dtype), pltpu.SemaphoreType.DMA((n_groups,))],
             compiler_params=_params,
-        )(integral_tile_mask.T, x)
+        )(integral_tile_mask.T, pltpu.with_memory_space_constraint(x, pltpu.HBM))
 
     mine = lax.broadcasted_iota(jnp.int32, (tile_rows, n_col * kblock), 1) // kblock == c
     mask = lax.psum(jnp.where(mine, jnp.tile(amplitude_tile_mask, (1, n_col)), 0), "col")
@@ -160,7 +189,7 @@
         out_specs=[_vmem] * 2,
         scratch_shapes=[pltpu.SemaphoreType.DMA((depth // TILE * KEEP // GROUP,))],
         compiler_params=_params,
-    )(mask, amps)
+    )(mask, pltpu.with_memory_space_constraint(amps, pltpu.HBM))
 
     order = [2 * p if p < n_col // 2 else 2 * (n_col - 1 - p) + 1 for p in range(n_col)]
     up = [(order[p], order[(p + 1) % n_col]) for p in range(n_col)]
@@ -176,12 +205,15 @@
         held[k][t] = lax.ppermute(held[k - 1][t], "col", up)
         held[b][1 - t] = lax.ppermute(held[(b + 1) % n_col][1 - t], "col", down)
 
-    def after(turn, values):
+    def after(turn, values, way):
         if turn is None:
             return values
         k, t = turns[turn]
         b = (n_col - k) % n_col
-        *values, held[k][t], held[b][1 - t] = lax.optimization_barrier((*values, held[k][t], held[b][1 - t]))
+        if way != "d":
+            *values, held[k][t] = lax.optimization_barrier((*values, held[k][t]))
+        if way != "u":
+            *values, held[b][1 - t] = lax.optimization_barrier((*values, held[b][1 - t]))
         return values
 
     def swap(x, j):
@@ -194,18 +226,29 @@
         held[0] = [own[0], own[1]]
     pieces = {0: list(masked_ints(x))}
     for j in range(2, n_row, 2):
-        pieces[j] = list((swap(p, j) for p in pieces[0]))
+        late = [pieces[0][0], *after(1, pieces[0][1:], 'b')]
+        pieces[j] = [swap(p, j) for p in late]
     for j in range(0, n_row, 2):
         pieces[j + 1] = [None] * n_groups
         for g in range(n_groups):
-            (pieces[j][g],) = after({(0, 0): 1, (0, 1): 2, (2, 0): 3, (2, 1): 4}[(min(j, 2), g)], (pieces[j][g],))
+            (pieces[j][g],) = after((0, 4, 4, 5)[min(j, 2) + g], (pieces[j][g],), 'bbub'[min(j, 2) + g])
             pieces[j + 1][g] = swap(pieces[j][g], 1)
     ints = [p for j in range(n_row) for p in pieces[j]]
 
     out = None
-    for shifts in [(0, 1, n_col - 1)] + [(k, n_col - k) for k in range(2, last)] + [(last,)]:
-        out = ladder_rows(n_row, n_col, kt_local, shifts, mask, [held[s] for s in shifts], ints, out_shape, out)
-    return out
+    groups = [(0, 1, n_col - 1, 2, n_col - 2)] + [(k, n_col - k) for k in range(3, last)]
+    for shifts in groups:
+        ahead = last if shifts == groups[-1] else None
+        out, *tiles = ladder_rows(n_row, n_col, kt_local, shifts, ahead, mask, [held[s] for s in shifts], ints, out_shape, out)
+    return pl.pallas_call(
+        functools.partial(last_kernel, n_col, last),
+        out_shape=out_shape,
+        in_specs=[_vmem] * 3 + [_any],
+        out_specs=_any,
+        scratch_shapes=[pltpu.VMEM((rows, integrals.shape[1]), jnp.float32), pltpu.SemaphoreType.DMA],
+        input_output_aliases={3: 0},
+        compiler_params=_params,
+    )(*held[last], *tiles, out)
 
 
 def solution(mesh):

time: 63.5 us -> 61.3 us (0.965)
  local copies, waits for them, and re-layouts: 3.88 us -> 1.43 us
  waiting for transfers between devices: 18.3 us -> 19.4 us
    pallas_call x4 -> x2, Pallas kernels: 8.32 us -> 5.03 us  [ladder_rows(): pl.pallas_call(functools.partial(ladder_kernel, n_row, n_col, kt_local, s...]
    unnamed x6 -> x2, local copies, waits for them, and re-layouts: 3.13 us -> 0.68 us
    ppermute x7, waiting for transfers between devices: 14 us -> 15.9 us  [on_device(): held[k][t] = lax.ppermute(held[k - 1][t], 'col', up)]
    pallas_call x0 -> x1, Pallas kernels: none -> 1.16 us  [on_device(): pl.pallas_call(functools.partial(last_kernel, n_col, last), out_shape=out...]
    pallas_call x1, Pallas kernels: 0.9 us -> 1.9 us  [masked_ints(): pl.pallas_call(mask_ints_kernel, out_shape=[piece] * n_groups, in_specs=[...]
    ppermute x7, waiting for transfers between devices: 4.29 us -> 3.49 us  [on_device(): held[b][1 - t] = lax.ppermute(held[(b + 1) % n_col][1 - t], 'col', down)]
    pallas_call x1, Pallas kernels: 1.06 us -> 1.79 us  [on_device(): pl.pallas_call(functools.partial(compress_kernel, n_row, kt_local), out_s...]
  transfers between devices with their start and end apart: 20 -> 20, of which waited for: 11 -> 10; matrix products, arithmetic and copies ran while one was open for 0% -> 0% of each run, Pallas kernels for 12% -> 11%
where the time goes in v3:
time: 61.3 us; the launch traced here: 61 us
  waiting for transfers between devices  19.4 us (32%)
  starting transfers between devices  17.2 us (28%)
  blocking collectives  13.1 us (21%)
  Pallas kernels  9.89 us (16%)
  local copies, waits for them, and re-layouts  1.43 us (2%)
    ppermute x7, waiting for transfers between devices, on_device(): held[k][t] = lax.ppermute(held[k - 1][t], 'col', up)  15.9 us
    psum x1, blocking collectives, on_device(): lax.psum(jnp.where(mine, jnp.tile(amplitude_tile_mask, (1, n_col)), 0), '...  13.1 us
    ppermute x7, starting transfers between devices, on_device(): held[b][1 - t] = lax.ppermute(held[(b + 1) % n_col][1 - t], 'col', down)  10.9 us
    pallas_call x2, Pallas kernels, ladder_rows(): pl.pallas_call(functools.partial(ladder_kernel, n_row, n_col, kt_local, s...  5.03 us
    ppermute x7, waiting for transfers between devices, on_device(): held[b][1 - t] = lax.ppermute(held[(b + 1) % n_col][1 - t], 'col', down)  3.49 us
    ppermute x7, starting transfers between devices, on_device(): held[k][t] = lax.ppermute(held[k - 1][t], 'col', up)  3.3 us
    ppermute x6, starting transfers between devices, swap(): return lax.ppermute(x, 'row', [(i, i ^ j) for i in range(n_row)])  2.99 us
    pallas_call x1, Pallas kernels, masked_ints(): pl.pallas_call(mask_ints_kernel, out_shape=[piece] * n_groups, in_specs=[...  1.9 us
  transfers between devices with their start and end apart: 20, of which 10 were waited for; matrix products, arithmetic and copies ran while one was open for 0% of the time, Pallas kernels for 11%

profile of v3, /device:TPU:0, one launch (start us, length us, event | category | flops | bytes accessed | tf_op | source)
XLA Modules:
  0.0 61.0 jit_solution(14155359823203819345)
XLA Ops:
  0.8 13.1 %psum.7.mask_ref = s32[8,32]{1,0:T(8,128)S(1)} all-reduce(s32[8,32]{1,0:T(8,128)S(1)} %fusion), channel_id=1, replica_groups=mesh['row'=4,'col'=8] {'col'}, use_global_device_ids=true, to_apply=%region_0.1 | all-reduce | flops 256 | bytes 2048 | tf_op jit(solution)/shard_map/psum | solution.py:182
  13.8 1.8 %shard_map.46 = (bf16[128,1024]{1,0:T(8,128)(2,1)S(1)}, bf16[128,1024]{1,0:T(8,128)(2,1)S(1)}) custom-call(s32[8,32]{1,0:T(8,128)S(1)} %psum.7.mask_ref, bf16[128,4096]{1,0:T(8,128)(2,1)} %a_ref.1), custom_call_target="tpu_custom_call" | custom-call | tf_op jit(solution)/shard_map/pallas_call | solution.py:185
  16.1 1.6 %collective-permute-start.10 = (bf16[128,1024]{1,0:T(8,128)(2,1)S(1)}, bf16[128,1024]{1,0:T(8,128)(2,1)S(1)}, u32[]{:S(2)}, u32[]{:S(2)}) collective-permute-start(bf16[128,1024]{1,0:T(8,128)(2,1)S(1)} %get-tuple-element.51.refs_0_), channel_id=1, source_target_pairs={{2,0},{4,2},{6,4},{7,6},{5,7},{3,5},{1,3},{0,1},{10,8},{12,10},{14... | collective-permute-start | bytes 786440 | tf_op jit(solution)/shard_map/ppermute | solution.py:206
  18.2 1.6 %collective-permute-start.4 = (bf16[128,1024]{1,0:T(8,128)(2,1)S(1)}, bf16[128,1024]{1,0:T(8,128)(2,1)S(1)}, u32[]{:S(2)}, u32[]{:S(2)}) collective-permute-start(bf16[128,1024]{1,0:T(8,128)(2,1)S(1)} %get-tuple-element.52.refs_1_), channel_id=1, source_target_pairs={{2,0},{4,2},{6,4},{7,6},{5,7},{3,5},{1,3},{0,1},{10,8},{12,10},{14... | collective-permute-start | bytes 786440 | tf_op jit(solution)/shard_map/ppermute | solution.py:206
  20.4 1.9 %shard_map.47 = (bf16[512,512]{1,0:T(8,128)(2,1)S(1)}, bf16[512,512]{1,0:T(8,128)(2,1)S(1)}) custom-call(s32[4,8]{1,0:T(4,128)S(1)} %bitcast.2, bf16[1024,512]{1,0:T(8,128)(2,1)} %x_ref), custom_call_target="tpu_custom_call" | custom-call | tf_op jit(solution)/shard_map/pallas_call | solution.py:172
  22.3 2.6 %collective-permute-done.9.refs_3_ = bf16[128,1024]{1,0:T(8,128)(2,1)S(1)} collective-permute-done((bf16[128,1024]{1,0:T(8,128)(2,1)S(1)}, bf16[128,1024]{1,0:T(8,128)(2,1)S(1)}, u32[]{:S(2)}, u32[]{:S(2)}) %collective-permute-start.9) | collective-permute-done | bytes 262176 | tf_op jit(solution)/shard_map/ppermute | solution.py:205
  25.4 1.5 %collective-permute-start.11 = (bf16[512,512]{1,0:T(8,128)(2,1)S(1)}, bf16[512,512]{1,0:T(8,128)(2,1)S(1)}, u32[]{:S(2)}, u32[]{:S(2)}) collective-permute-start(bf16[512,512]{1,0:T(8,128)(2,1)S(1)} %get-tuple-element.48.refs_11_.refs_5_), channel_id=1, source_target_pairs={{0,16},{8,24},{16,0},{24,8},{1,17},{9,25},{17,1},{25,9},{2,18},{10... | collective-permute-start | bytes 1572872 | tf_op jit(solution)/shard_map/ppermute | solution.py:220
  26.9 1.6 %collective-permute-start.14 = (bf16[128,1024]{1,0:T(8,128)(2,1)S(1)}, bf16[128,1024]{1,0:T(8,128)(2,1)S(1)}, u32[]{:S(2)}, u32[]{:S(2)}) collective-permute-start(bf16[128,1024]{1,0:T(8,128)(2,1)S(1)} %collective-permute-done.10.refs_4_), channel_id=1, source_target_pairs={{2,0},{4,2},{6,4},{7,6},{5,7},{3,5},{1,3},{0,1},{10,8},{12,10},{14... | collective-permute-start | bytes 786440 | tf_op jit(solution)/shard_map/ppermute | solution.py:206
  28.5 2.1 %collective-permute-done.refs_2_ = bf16[128,1024]{1,0:T(8,128)(2,1)S(1)} collective-permute-done((bf16[128,1024]{1,0:T(8,128)(2,1)S(1)}, bf16[128,1024]{1,0:T(8,128)(2,1)S(1)}, u32[]{:S(2)}, u32[]{:S(2)}) %collective-permute-start) | collective-permute-done | bytes 262176 | tf_op jit(solution)/shard_map/ppermute | solution.py:205
  31.0 1.6 %collective-permute-start.5 = (bf16[128,1024]{1,0:T(8,128)(2,1)S(1)}, bf16[128,1024]{1,0:T(8,128)(2,1)S(1)}, u32[]{:S(2)}, u32[]{:S(2)}) collective-permute-start(bf16[128,1024]{1,0:T(8,128)(2,1)S(1)} %collective-permute-done.4.refs_5_), channel_id=1, source_target_pairs={{2,0},{4,2},{6,4},{7,6},{5,7},{3,5},{1,3},{0,1},{10,8},{12,10},{14... | collective-permute-start | bytes 786440 | tf_op jit(solution)/shard_map/ppermute | solution.py:206
  32.6 3.6 %collective-permute-done.12.refs_7_ = bf16[128,1024]{1,0:T(8,128)(2,1)S(1)} collective-permute-done((bf16[128,1024]{1,0:T(8,128)(2,1)S(1)}, bf16[128,1024]{1,0:T(8,128)(2,1)S(1)}, u32[]{:S(2)}, u32[]{:S(2)}) %collective-permute-start.12) | collective-permute-done | bytes 262176 | tf_op jit(solution)/shard_map/ppermute | solution.py:205
  36.2 1.5 %collective-permute-start.8 = (bf16[512,512]{1,0:T(8,128)(2,1)S(1)}, bf16[512,512]{1,0:T(8,128)(2,1)S(1)}, u32[]{:S(2)}, u32[]{:S(2)}) collective-permute-start(bf16[512,512]{1,0:T(8,128)(2,1)S(1)} %get-tuple-element.47.refs_10_.refs_4_), channel_id=1, source_target_pairs={{0,16},{8,24},{16,0},{24,8},{1,17},{9,25},{17,1},{25,9},{2,18},{10... | collective-permute-start | bytes 1572872 | tf_op jit(solution)/shard_map/ppermute | solution.py:220
  38.1 3.7 %collective-permute-done.1.refs_6_ = bf16[128,1024]{1,0:T(8,128)(2,1)S(1)} collective-permute-done((bf16[128,1024]{1,0:T(8,128)(2,1)S(1)}, bf16[128,1024]{1,0:T(8,128)(2,1)S(1)}, u32[]{:S(2)}, u32[]{:S(2)}) %collective-permute-start.1) | collective-permute-done | bytes 262176 | tf_op jit(solution)/shard_map/ppermute | solution.py:205
  41.8 1.5 %collective-permute-start.15 = (bf16[128,1024]{1,0:T(8,128)(2,1)S(1)}, bf16[128,1024]{1,0:T(8,128)(2,1)S(1)}, u32[]{:S(2)}, u32[]{:S(2)}) collective-permute-start(bf16[128,1024]{1,0:T(8,128)(2,1)S(1)} %collective-permute-done.14.refs_8_), channel_id=1, source_target_pairs={{2,0},{4,2},{6,4},{7,6},{5,7},{3,5},{1,3},{0,1},{10,8},{12,10},{14... | collective-permute-start | bytes 786440 | tf_op jit(solution)/shard_map/ppermute | solution.py:206
  43.8 1.5 %collective-permute-start.6 = (bf16[128,1024]{1,0:T(8,128)(2,1)S(1)}, bf16[128,1024]{1,0:T(8,128)(2,1)S(1)}, u32[]{:S(2)}, u32[]{:S(2)}) collective-permute-start(bf16[128,1024]{1,0:T(8,128)(2,1)S(1)} %collective-permute-done.5.refs_9_), channel_id=1, source_target_pairs={{2,0},{4,2},{6,4},{7,6},{5,7},{3,5},{1,3},{0,1},{10,8},{12,10},{14... | collective-permute-start | bytes 786440 | tf_op jit(solution)/shard_map/ppermute | solution.py:206
  45.3 0.8 %collective-permute-done.13.refs_1_ = bf16[128,1024]{1,0:T(8,128)(2,1)S(1)} collective-permute-done((bf16[128,1024]{1,0:T(8,128)(2,1)S(1)}, bf16[128,1024]{1,0:T(8,128)(2,1)S(1)}, u32[]{:S(2)}, u32[]{:S(2)}) %collective-permute-start.13) | collective-permute-done | bytes 262176 | tf_op jit(solution)/shard_map/ppermute | solution.py:205
  46.1 2.0 %collective-permute-done.15.refs_2_ = bf16[128,1024]{1,0:T(8,128)(2,1)S(1)} collective-permute-done((bf16[128,1024]{1,0:T(8,128)(2,1)S(1)}, bf16[128,1024]{1,0:T(8,128)(2,1)S(1)}, u32[]{:S(2)}, u32[]{:S(2)}) %collective-permute-start.15) | collective-permute-done | bytes 262176 | tf_op jit(solution)/shard_map/ppermute | solution.py:206
  48.2 1.5 %collective-permute-done.2.refs_0_ = bf16[128,1024]{1,0:T(8,128)(2,1)S(1)} collective-permute-done((bf16[128,1024]{1,0:T(8,128)(2,1)S(1)}, bf16[128,1024]{1,0:T(8,128)(2,1)S(1)}, u32[]{:S(2)}, u32[]{:S(2)}) %collective-permute-start.2) | collective-permute-done | bytes 262176 | tf_op jit(solution)/shard_map/ppermute | solution.py:205
  49.7 1.3 %collective-permute-done.6.refs_3_ = bf16[128,1024]{1,0:T(8,128)(2,1)S(1)} collective-permute-done((bf16[128,1024]{1,0:T(8,128)(2,1)S(1)}, bf16[128,1024]{1,0:T(8,128)(2,1)S(1)}, u32[]{:S(2)}, u32[]{:S(2)}) %collective-permute-start.6) | collective-permute-done | bytes 262176 | tf_op jit(solution)/shard_map/ppermute | solution.py:206
  51.4 1.6 %collective-permute-start.7 = (bf16[128,1024]{1,0:T(8,128)(2,1)S(1)}, bf16[128,1024]{1,0:T(8,128)(2,1)S(1)}, u32[]{:S(2)}, u32[]{:S(2)}) collective-permute-start(bf16[128,1024]{1,0:T(8,128)(2,1)S(1)} %collective-permute-done.6.refs_3_), channel_id=1, source_target_pairs={{2,0},{4,2},{6,4},{7,6},{5,7},{3,5},{1,3},{0,1},{10,8},{12,10},{14... | collective-permute-start | bytes 786440 | tf_op jit(solution)/shard_map/ppermute | solution.py:206
  53.0 2.9 %shard_map.48.refs_12_ = f32[1024,512]{1,0:T(8,128)} custom-call(s32[8,32]{1,0:T(8,128)S(1)} %psum.7.mask_ref, bf16[128,1024]{1,0:T(8,128)(2,1)S(1)} %get-tuple-element.51.refs_0_, bf16[128,1024]{1,0:T(8,128)(2,1)S(1)} %get-tuple-element.52.refs_1_, bf16[128,1024]{1,0:T(8,128)(2,1)S(1)} %collective-permute-done.refs_2_, ...), custom_call_target="tpu_custom_call" | custom-call | tf_op jit(solution)/shard_map/pallas_call | solution.py:152
  56.0 2.1 %shard_map.49 = (f32[1024,512]{1,0:T(8,128)}, bf16[2048,512]{1,0:T(8,128)(2,1)S(1)}) custom-call(s32[8,32]{1,0:T(8,128)S(1)} %psum.7.mask_ref, bf16[128,1024]{1,0:T(8,128)(2,1)S(1)} %collective-permute-done.2.refs_0_, bf16[128,1024]{1,0:T(8,128)(2,1)S(1)} %collective-permute-done.13.refs_1_, ...), custom_call_target="tpu_custom_call", output_to_operand_aliasing={{0}: (13, {})} | custom-call | tf_op jit(solution)/shard_map/pallas_call | solution.py:152
  58.1 1.6 %collective-permute-done.3.refs_0_ = bf16[128,1024]{1,0:T(8,128)(2,1)S(1)} collective-permute-done((bf16[128,1024]{1,0:T(8,128)(2,1)S(1)}, bf16[128,1024]{1,0:T(8,128)(2,1)S(1)}, u32[]{:S(2)}, u32[]{:S(2)}) %collective-permute-start.3) | collective-permute-done | bytes 262176 | tf_op jit(solution)/shard_map/ppermute | solution.py:205
  59.9 1.2 %shard_map.50 = f32[1024,512]{1,0:T(8,128)} custom-call(bf16[128,1024]{1,0:T(8,128)(2,1)S(1)} %collective-permute-done.3.refs_0_, bf16[128,1024]{1,0:T(8,128)(2,1)S(1)} %collective-permute-done.7.refs_1_, bf16[2048,512]{1,0:T(8,128)(2,1)S(1)} %get-tuple-element.57.refs_2_, f32[1024,512]{1,0:T(8,128)} %get-tuple-element.58.refs_3_), custom_call_target="tpu_custom_call", output_to_operand_aliasing={{}: (3, {})} | custom-call | tf_op jit(solution)/shard_map/pallas_call | solution.py:243
  (29 shorter events, 5.0 us)
Async XLA Ops:
  15.6 9.3 %collective-permute-start.9 = (bf16[128,1024]{1,0:T(8,128)(2,1)S(1)}, bf16[128,1024]{1,0:T(8,128)(2,1)S(1)}, u32[]{:S(2)}, u32[]{:S(2)}) collective-permute-start(bf16[128,1024]{1,0:T(8,128)(2,1)S(1)} %get-tuple-element.52.refs_1_), channel_id=1, source_target_pairs={{0,2},{2,4},{4,6},{6,7},{7,5},{5,3},{3,1},{1,0},{8,10},{10,12},{12... | collective-permute-start | bytes 786440 | tf_op jit(solution)/shard_map/ppermute | solution.py:205
  16.1 9.2 %collective-permute-start.10 = (bf16[128,1024]{1,0:T(8,128)(2,1)S(1)}, bf16[128,1024]{1,0:T(8,128)(2,1)S(1)}, u32[]{:S(2)}, u32[]{:S(2)}) collective-permute-start(bf16[128,1024]{1,0:T(8,128)(2,1)S(1)} %get-tuple-element.51.refs_0_), channel_id=1, source_target_pairs={{2,0},{4,2},{6,4},{7,6},{5,7},{3,5},{1,3},{0,1},{10,8},{12,10},{14... | collective-permute-start | bytes 786440 | tf_op jit(solution)/shard_map/ppermute | solution.py:206
  17.7 12.8 %collective-permute-start = (bf16[128,1024]{1,0:T(8,128)(2,1)S(1)}, bf16[128,1024]{1,0:T(8,128)(2,1)S(1)}, u32[]{:S(2)}, u32[]{:S(2)}) collective-permute-start(bf16[128,1024]{1,0:T(8,128)(2,1)S(1)} %get-tuple-element.51.refs_0_), channel_id=1, source_target_pairs={{0,2},{2,4},{4,6},{6,7},{7,5},{5,3},{3,1},{1,0},{8,10},{10,12},{12... | collective-permute-start | bytes 786440 | tf_op jit(solution)/shard_map/ppermute | solution.py:205
  18.2 12.8 %collective-permute-start.4 = (bf16[128,1024]{1,0:T(8,128)(2,1)S(1)}, bf16[128,1024]{1,0:T(8,128)(2,1)S(1)}, u32[]{:S(2)}, u32[]{:S(2)}) collective-permute-start(bf16[128,1024]{1,0:T(8,128)(2,1)S(1)} %get-tuple-element.52.refs_1_), channel_id=1, source_target_pairs={{2,0},{4,2},{6,4},{7,6},{5,7},{3,5},{1,3},{0,1},{10,8},{12,10},{14... | collective-permute-start | bytes 786440 | tf_op jit(solution)/shard_map/ppermute | solution.py:206
  19.7 0.7 %copy-start = (s32[8,4]{0,1:T(4,128)S(1)}, s32[8,4]{0,1:T(4,128)}, u32[]{:S(2)}) copy-start(s32[8,4]{0,1:T(4,128)} %param.7) | copy-start | bytes 388
  24.9 11.2 %collective-permute-start.12 = (bf16[128,1024]{1,0:T(8,128)(2,1)S(1)}, bf16[128,1024]{1,0:T(8,128)(2,1)S(1)}, u32[]{:S(2)}, u32[]{:S(2)}) collective-permute-start(bf16[128,1024]{1,0:T(8,128)(2,1)S(1)} %collective-permute-done.9.refs_3_), channel_id=1, source_target_pairs={{0,2},{2,4},{4,6},{6,7},{7,5},{5,3},{3,1},{1,0},{8,10},{10,12},{12... | collective-permute-start | bytes 786440 | tf_op jit(solution)/shard_map/ppermute | solution.py:205
  25.4 18.4 %collective-permute-start.11 = (bf16[512,512]{1,0:T(8,128)(2,1)S(1)}, bf16[512,512]{1,0:T(8,128)(2,1)S(1)}, u32[]{:S(2)}, u32[]{:S(2)}) collective-permute-start(bf16[512,512]{1,0:T(8,128)(2,1)S(1)} %get-tuple-element.48.refs_11_.refs_5_), channel_id=1, source_target_pairs={{0,16},{8,24},{16,0},{24,8},{1,17},{9,25},{17,1},{25,9},{2,18},{10... | collective-permute-start | bytes 1572872 | tf_op jit(solution)/shard_map/ppermute | solution.py:220
  26.9 10.8 %collective-permute-start.14 = (bf16[128,1024]{1,0:T(8,128)(2,1)S(1)}, bf16[128,1024]{1,0:T(8,128)(2,1)S(1)}, u32[]{:S(2)}, u32[]{:S(2)}) collective-permute-start(bf16[128,1024]{1,0:T(8,128)(2,1)S(1)} %collective-permute-done.10.refs_4_), channel_id=1, source_target_pairs={{2,0},{4,2},{6,4},{7,6},{5,7},{3,5},{1,3},{0,1},{10,8},{12,10},{14... | collective-permute-start | bytes 786440 | tf_op jit(solution)/shard_map/ppermute | solution.py:206
  30.6 11.2 %collective-permute-start.1 = (bf16[128,1024]{1,0:T(8,128)(2,1)S(1)}, bf16[128,1024]{1,0:T(8,128)(2,1)S(1)}, u32[]{:S(2)}, u32[]{:S(2)}) collective-permute-start(bf16[128,1024]{1,0:T(8,128)(2,1)S(1)} %collective-permute-done.refs_2_), channel_id=1, source_target_pairs={{0,2},{2,4},{4,6},{6,7},{7,5},{5,3},{3,1},{1,0},{8,10},{10,12},{12... | collective-permute-start | bytes 786440 | tf_op jit(solution)/shard_map/ppermute | solution.py:205
  31.0 12.3 %collective-permute-start.5 = (bf16[128,1024]{1,0:T(8,128)(2,1)S(1)}, bf16[128,1024]{1,0:T(8,128)(2,1)S(1)}, u32[]{:S(2)}, u32[]{:S(2)}) collective-permute-start(bf16[128,1024]{1,0:T(8,128)(2,1)S(1)} %collective-permute-done.4.refs_5_), channel_id=1, source_target_pairs={{2,0},{4,2},{6,4},{7,6},{5,7},{3,5},{1,3},{0,1},{10,8},{12,10},{14... | collective-permute-start | bytes 786440 | tf_op jit(solution)/shard_map/ppermute | solution.py:206
  36.2 13.5 %collective-permute-start.8 = (bf16[512,512]{1,0:T(8,128)(2,1)S(1)}, bf16[512,512]{1,0:T(8,128)(2,1)S(1)}, u32[]{:S(2)}, u32[]{:S(2)}) collective-permute-start(bf16[512,512]{1,0:T(8,128)(2,1)S(1)} %get-tuple-element.47.refs_10_.refs_4_), channel_id=1, source_target_pairs={{0,16},{8,24},{16,0},{24,8},{1,17},{9,25},{17,1},{25,9},{2,18},{10... | collective-permute-start | bytes 1572872 | tf_op jit(solution)/shard_map/ppermute | solution.py:220
  37.7 8.5 %collective-permute-start.13 = (bf16[128,1024]{1,0:T(8,128)(2,1)S(1)}, bf16[128,1024]{1,0:T(8,128)(2,1)S(1)}, u32[]{:S(2)}, u32[]{:S(2)}) collective-permute-start(bf16[128,1024]{1,0:T(8,128)(2,1)S(1)} %collective-permute-done.12.refs_7_), channel_id=1, source_target_pairs={{0,2},{2,4},{4,6},{6,7},{7,5},{5,3},{3,1},{1,0},{8,10},{10,12},{12... | collective-permute-start | bytes 786440 | tf_op jit(solution)/shard_map/ppermute | solution.py:205
  41.8 6.4 %collective-permute-start.15 = (bf16[128,1024]{1,0:T(8,128)(2,1)S(1)}, bf16[128,1024]{1,0:T(8,128)(2,1)S(1)}, u32[]{:S(2)}, u32[]{:S(2)}) collective-permute-start(bf16[128,1024]{1,0:T(8,128)(2,1)S(1)} %collective-permute-done.14.refs_8_), channel_id=1, source_target_pairs={{2,0},{4,2},{6,4},{7,6},{5,7},{3,5},{1,3},{0,1},{10,8},{12,10},{14... | collective-permute-start | bytes 786440 | tf_op jit(solution)/shard_map/ppermute | solution.py:206
  43.3 6.4 %collective-permute-start.2 = (bf16[128,1024]{1,0:T(8,128)(2,1)S(1)}, bf16[128,1024]{1,0:T(8,128)(2,1)S(1)}, u32[]{:S(2)}, u32[]{:S(2)}) collective-permute-start(bf16[128,1024]{1,0:T(8,128)(2,1)S(1)} %collective-permute-done.1.refs_6_), channel_id=1, source_target_pairs={{0,2},{2,4},{4,6},{6,7},{7,5},{5,3},{3,1},{1,0},{8,10},{10,12},{12... | collective-permute-start | bytes 786440 | tf_op jit(solution)/shard_map/ppermute | solution.py:205
  43.8 7.1 %collective-permute-start.6 = (bf16[128,1024]{1,0:T(8,128)(2,1)S(1)}, bf16[128,1024]{1,0:T(8,128)(2,1)S(1)}, u32[]{:S(2)}, u32[]{:S(2)}) collective-permute-start(bf16[128,1024]{1,0:T(8,128)(2,1)S(1)} %collective-permute-done.5.refs_9_), channel_id=1, source_target_pairs={{2,0},{4,2},{6,4},{7,6},{5,7},{3,5},{1,3},{0,1},{10,8},{12,10},{14... | collective-permute-start | bytes 786440 | tf_op jit(solution)/shard_map/ppermute | solution.py:206
  46.1 5.3 %collective-permute-start.16 = (bf16[512,512]{1,0:T(8,128)(2,1)S(1)}, bf16[512,512]{1,0:T(8,128)(2,1)S(1)}, u32[]{:S(2)}, u32[]{:S(2)}) collective-permute-start(bf16[512,512]{1,0:T(8,128)(2,1)S(1)} %get-tuple-element.47.refs_10_.refs_4_), channel_id=1, source_target_pairs={{0,8},{8,0},{16,24},{24,16},{1,9},{9,1},{17,25},{25,17},{2,10},{10... | collective-permute-start | bytes 1572872 | tf_op jit(solution)/shard_map/ppermute | solution.py:220
  48.2 4.8 %collective-permute-start.19 = (bf16[512,512]{1,0:T(8,128)(2,1)S(1)}, bf16[512,512]{1,0:T(8,128)(2,1)S(1)}, u32[]{:S(2)}, u32[]{:S(2)}) collective-permute-start(bf16[512,512]{1,0:T(8,128)(2,1)S(1)} %collective-permute-done.11.refs_15_.refs_9_), channel_id=1, source_target_pairs={{0,8},{8,0},{16,24},{24,16},{1,9},{9,1},{17,25},{25,17},{2,10},{10... | collective-permute-start | bytes 1572872 | tf_op jit(solution)/shard_map/ppermute | solution.py:220
  49.7 3.3 %collective-permute-start.18 = (bf16[512,512]{1,0:T(8,128)(2,1)S(1)}, bf16[512,512]{1,0:T(8,128)(2,1)S(1)}, u32[]{:S(2)}, u32[]{:S(2)}) collective-permute-start(bf16[512,512]{1,0:T(8,128)(2,1)S(1)} %collective-permute-done.8.refs_14_.refs_8_), channel_id=1, source_target_pairs={{0,8},{8,0},{16,24},{24,16},{1,9},{9,1},{17,25},{25,17},{2,10},{10... | collective-permute-start | bytes 1572872 | tf_op jit(solution)/shard_map/ppermute | solution.py:220
  51.0 2.0 %collective-permute-start.17 = (bf16[512,512]{1,0:T(8,128)(2,1)S(1)}, bf16[512,512]{1,0:T(8,128)(2,1)S(1)}, u32[]{:S(2)}, u32[]{:S(2)}) collective-permute-start(bf16[512,512]{1,0:T(8,128)(2,1)S(1)} %get-tuple-element.48.refs_11_.refs_5_), channel_id=1, source_target_pairs={{0,8},{8,0},{16,24},{24,16},{1,9},{9,1},{17,25},{25,17},{2,10},{10... | collective-permute-start | bytes 1572872 | tf_op jit(solution)/shard_map/ppermute | solution.py:220
  51.0 8.7 %collective-permute-start.3 = (bf16[128,1024]{1,0:T(8,128)(2,1)S(1)}, bf16[128,1024]{1,0:T(8,128)(2,1)S(1)}, u32[]{:S(2)}, u32[]{:S(2)}) collective-permute-start(bf16[128,1024]{1,0:T(8,128)(2,1)S(1)} %collective-permute-done.2.refs_0_), channel_id=1, source_target_pairs={{0,2},{2,4},{4,6},{6,7},{7,5},{5,3},{3,1},{1,0},{8,10},{10,12},{12... | collective-permute-start | bytes 786440 | tf_op jit(solution)/shard_map/ppermute | solution.py:205
  51.4 8.4 %collective-permute-start.7 = (bf16[128,1024]{1,0:T(8,128)(2,1)S(1)}, bf16[128,1024]{1,0:T(8,128)(2,1)S(1)}, u32[]{:S(2)}, u32[]{:S(2)}) collective-permute-start(bf16[128,1024]{1,0:T(8,128)(2,1)S(1)} %collective-permute-done.6.refs_3_), channel_id=1, source_target_pairs={{2,0},{4,2},{6,4},{7,6},{5,7},{3,5},{1,3},{0,1},{10,8},{12,10},{14... | collective-permute-start | bytes 786440 | tf_op jit(solution)/shard_map/ppermute | solution.py:206

commit v4 on v3

--- a/solution.py
+++ b/solution.py
@@ -27,9 +27,8 @@
     return jnp.where(c % 2 == 0, c // 2, n - 1 - c // 2)
 
 
-def picks(mask_ref, row, first):
-    m0, m1 = mask_ref[row, first], mask_ref[row, first + 1]
-    m2, m3 = mask_ref[row, first + 2], mask_ref[row, first + 3]
+def picks(mask_ref, tile_rows, row, group):
+    m0, m1, m2, m3 = (mask_ref[i, group * tile_rows + row] for i in range(GROUP))
     lo = jnp.where(m0 != 0, 0, jnp.where(m1 != 0, 1, 2))
     hi = jnp.where(m3 != 0, 3, jnp.where(m2 != 0, 2, 1))
     return lo, hi
@@ -52,32 +51,46 @@
                 out[at] = jnp.where(mask_ref[t, g * GROUP + q] != 0, x, jnp.zeros_like(x))
 
 
-def compress_kernel(n_row, kt_local, mask_ref, a_ref, *refs):
-    outs, sem = refs[:-1], refs[-1]
-    rows = a_ref.shape[0]
-    r, c = lax.axis_index("row"), lax.axis_index("col")
-    row = c * rows // TILE
-    per_out = n_row // len(outs)
-    copies = []
-    for j in range(n_row):
-        block = jnp.bitwise_xor(r, j)
-        out, j_in = outs[j // per_out], j % per_out
-        for g in range(kt_local // GROUP):
-            first = block * kt_local + g * GROUP
-            for s, p in enumerate(picks(mask_ref, row, first)):
-                slot = (j_in * (kt_local // GROUP) + g) * KEEP + s
-                src = pl.multiple_of((first + p) * TILE, TILE)
-                copies.append(
-                    pltpu.make_async_copy(
-                        a_ref.at[:, pl.ds(src, TILE)],
-                        out.at[:, pl.ds(slot * TILE, TILE)],
-                        sem.at[len(copies)],
-                    )
-                )
+def stage_kernel(mask_ref, a_ref, o_ref, held_ref, m_ref, sem):
+    half = a_ref.shape[0] // 2
+    copies = [
+        pltpu.make_async_copy(a_ref.at[pl.ds(i * half, half), :], held_ref.at[pl.ds(i * half, half), :], sem.at[i]) for i in range(2)
+    ]
+    copies.insert(0, pltpu.make_async_copy(mask_ref, m_ref, sem.at[2]))
     for copy in copies:
         copy.start()
+    tile_rows, wide = m_ref.shape[1], o_ref.shape[1]
+    row = lax.broadcasted_iota(jnp.int32, (tile_rows, wide), 0)
+    at = lax.broadcasted_iota(jnp.int32, (tile_rows, wide), 1)
+    spread = (at == lax.axis_index("col") * tile_rows + row).astype(jnp.float32).astype(jnp.bfloat16)
+    copies.pop(0).wait()
+    piece = m_ref[...].astype(jnp.float32).astype(jnp.bfloat16)
+    o_ref[...] = jnp.dot(piece, spread, preferred_element_type=jnp.float32).astype(jnp.int32)
     for copy in copies:
         copy.wait()
+
+
+def compress_kernel(n_row, n_col, tile_rows, mask_ref, a_ref, *outs):
+    rows, depth = a_ref.shape
+    wide = GROUP * TILE
+    n_groups = depth // wide // n_row
+    r, c = lax.axis_index("row"), lax.axis_index("col")
+    mask = mask_ref[...].astype(jnp.float32)
+    at = lax.broadcasted_iota(jnp.int32, mask.shape, 1)
+    per_out = n_row // len(outs)
+    for j in range(n_row):
+        out, j_in = outs[j // per_out], j % per_out
+        for g in range(n_groups):
+            group = jnp.bitwise_xor(r, j) * n_groups + g
+            m = jnp.sum(jnp.where(at == group * tile_rows + c * rows // TILE, mask, 0.0), axis=1, keepdims=True)
+            m0, m1, m2, m3 = (m[i : i + 1, :] for i in range(GROUP))
+            low = (m0, (1 - m0) * m1, (1 - m0) * (1 - m1))
+            high = (m3, (1 - m3) * m2, (1 - m3) * (1 - m2))
+            x = [a_ref[:, pl.ds(pl.multiple_of(group * wide + i * TILE, TILE), TILE)] for i in range(GROUP)]
+            slot = (j_in * n_groups + g) * KEEP
+            for s, (weights, order) in enumerate(((low, (0, 1, 2)), (high, (3, 2, 1)))):
+                parts = [x[i] * jnp.broadcast_to(w, x[i].shape).astype(x[i].dtype) for w, i in zip(weights, order)]
+                out[:, (slot + s) * TILE : (slot + s + 1) * TILE] = parts[0] + parts[1] + parts[2]
 
 
 def ladder_kernel(n_row, n_col, kt_local, shifts, ahead, mask_ref, *refs):
@@ -88,15 +101,16 @@
     o_ref, next_ref = (refs[-3], None) if ahead is None else (refs[-4], refs[-3])
     rows = units[0].shape[0]
     per_unit = n_row // 2
+    tile_rows = n_col * rows // TILE
     r, c = lax.axis_index("row"), lax.axis_index("col")
 
     def source(shift):
         return ring_chip(lax.rem(ring_pos(c, n_col) + (n_col - shift), n_col), n_col)
 
     def tiles(row, j, g):
-        first = (jnp.bitwise_xor(r, j) * (kt_local // GROUP) + g) * GROUP
+        group = jnp.bitwise_xor(r, j) * (kt_local // GROUP) + g
         held = ints[j * (kt_local // GROUP) + g]
-        return [held[pl.ds(pl.multiple_of(p * TILE, TILE), TILE), :] for p in picks(mask_ref, row, first)]
+        return [held[pl.ds(pl.multiple_of(p * TILE, TILE), TILE), :] for p in picks(mask_ref, tile_rows, row, group)]
 
     copies = []
     for i, shift in enumerate(shifts):
@@ -165,7 +179,6 @@
     tile_rows, kblock = amplitude_tile_mask.shape
     kt_local = integrals.shape[0] // TILE
     n_groups = kt_local // GROUP
-    c = lax.axis_index("col")
     piece = jax.ShapeDtypeStruct((GROUP * TILE, integrals.shape[1]), integrals.dtype)
 
     def masked_ints(x):
@@ -178,18 +191,27 @@
             compiler_params=_params,
         )(integral_tile_mask.T, pltpu.with_memory_space_constraint(x, pltpu.HBM))
 
-    mine = lax.broadcasted_iota(jnp.int32, (tile_rows, n_col * kblock), 1) // kblock == c
-    mask = lax.psum(jnp.where(mine, jnp.tile(amplitude_tile_mask, (1, n_col)), 0), "col")
+    placed, amps = pl.pallas_call(
+        stage_kernel,
+        out_shape=[
+            jax.ShapeDtypeStruct((kblock, n_col * tile_rows), jnp.int32),
+            jax.ShapeDtypeStruct(amps.shape, amps.dtype),
+        ],
+        in_specs=[_hbm, _hbm],
+        out_specs=[_vmem] * 2,
+        scratch_shapes=[pltpu.VMEM((kblock, tile_rows), jnp.int32), pltpu.SemaphoreType.DMA((3,))],
+        compiler_params=_params,
+    )(pltpu.with_memory_space_constraint(amplitude_tile_mask.T, pltpu.HBM), pltpu.with_memory_space_constraint(amps, pltpu.HBM))
+    mask = lax.psum(placed, "col")
 
     half = (rows, depth * KEEP // GROUP // 2)
     own = pl.pallas_call(
-        functools.partial(compress_kernel, n_row, kt_local),
+        functools.partial(compress_kernel, n_row, n_col, tile_rows),
         out_shape=[jax.ShapeDtypeStruct(half, amps.dtype)] * 2,
-        in_specs=[_smem, _hbm],
+        in_specs=[_vmem, _vmem],
         out_specs=[_vmem] * 2,
-        scratch_shapes=[pltpu.SemaphoreType.DMA((depth // TILE * KEEP // GROUP,))],
-        compiler_params=_params,
-    )(mask, pltpu.with_memory_space_constraint(amps, pltpu.HBM))
+        compiler_params=_params,
+    )(mask, amps)
 
     order = [2 * p if p < n_col // 2 else 2 * (n_col - 1 - p) + 1 for p in range(n_col)]
     up = [(order[p], order[(p + 1) % n_col]) for p in range(n_col)]
@@ -219,12 +241,8 @@
     def swap(x, j):
         return lax.ppermute(x, "row", [(i, i ^ j) for i in range(n_row)])
 
-    x = integrals
-    if True:
-        own = list(own)
-        x, own[0], own[1] = lax.optimization_barrier((x, own[0], own[1]))
-        held[0] = [own[0], own[1]]
-    pieces = {0: list(masked_ints(x))}
+    late, *held[0] = lax.optimization_barrier((integrals, *held[0]))
+    pieces = {0: list(masked_ints(late))}
     for j in range(2, n_row, 2):
         late = [pieces[0][0], *after(1, pieces[0][1:], 'b')]
         pieces[j] = [swap(p, j) for p in late]

time: 61.3 us -> 60.3 us (0.984)
  local copies, waits for them, and re-layouts: 1.43 us -> 0.01 us
  waiting for transfers between devices: 19.4 us -> 20.1 us
    another operation x2 -> x0, local copies, waits for them, and re-layouts: 0.75 us -> none  [on_device(): jnp.tile(amplitude_tile_mask, (1, n_col))]
    ppermute x7, waiting for transfers between devices: 15.9 us -> 16.6 us  [on_device(): held[k][t] = lax.ppermute(held[k - 1][t], 'col', up)]
    unnamed x2, local copies, waits for them, and re-layouts: 0.68 us -> 0.01 us
    pallas_call x1 -> x2, Pallas kernels: 1.79 us -> 1.68 us  [the longest x1 1.25 us: on_device(): pl.pallas_call(stage_kernel, out_shape=[jax.ShapeDtypeStruct((kblock, n_c...]
where the time goes in v4:
time: 60.3 us; the launch traced here: 60.2 us
  waiting for transfers between devices  20.1 us (33%)
  starting transfers between devices  17.2 us (29%)
  blocking collectives  13.1 us (22%)
  Pallas kernels  9.73 us (16%)
    ppermute x7, waiting for transfers between devices, on_device(): held[k][t] = lax.ppermute(held[k - 1][t], 'col', up)  16.6 us
    psum x1, blocking collectives, on_device(): mask = lax.psum(placed, 'col')  13.1 us
    ppermute x7, starting transfers between devices, on_device(): held[b][1 - t] = lax.ppermute(held[(b + 1) % n_col][1 - t], 'col', down)  10.9 us
    pallas_call x2, Pallas kernels, ladder_rows(): pl.pallas_call(functools.partial(ladder_kernel, n_row, n_col, kt_local, s...  4.98 us
    ppermute x7, waiting for transfers between devices, on_device(): held[b][1 - t] = lax.ppermute(held[(b + 1) % n_col][1 - t], 'col', down)  3.49 us
    ppermute x7, starting transfers between devices, on_device(): held[k][t] = lax.ppermute(held[k - 1][t], 'col', up)  3.3 us
    ppermute x6, starting transfers between devices, swap(): return lax.ppermute(x, 'row', [(i, i ^ j) for i in range(n_row)])  2.99 us
    pallas_call x1, Pallas kernels, masked_ints(): pl.pallas_call(mask_ints_kernel, out_shape=[piece] * n_groups, in_specs=[...  1.9 us
  transfers between devices with their start and end apart: 20, of which 10 were waited for; matrix products, arithmetic and copies ran while one was open for 0% of the time, Pallas kernels for 11%

profile of v4, /device:TPU:0, one launch (start us, length us, event | category | flops | bytes accessed | tf_op | source)
XLA Modules:
  0.0 60.2 jit_solution(6980135624361274929)
XLA Ops:
  0.0 1.3 %shard_map.46 = (s32[4,64]{1,0:T(4,128)S(1)}, bf16[128,4096]{1,0:T(8,128)(2,1)S(1)}) custom-call(s32[4,8]{1,0:T(4,128)} %bitcast.3, bf16[128,4096]{1,0:T(8,128)(2,1)} %a_ref.1), custom_call_target="tpu_custom_call" | custom-call | tf_op jit(solution)/shard_map/pallas_call | solution.py:194
  1.3 13.1 %psum.7.mask_ref = s32[4,64]{1,0:T(4,128)S(1)} all-reduce(s32[4,64]{1,0:T(4,128)S(1)} %get-tuple-element.34), channel_id=1, replica_groups=mesh['row'=4,'col'=8] {'col'}, use_global_device_ids=true, to_apply=%region_0.0 | all-reduce | flops 256 | bytes 2048 | tf_op jit(solution)/shard_map/psum | solution.py:205
  15.3 1.6 %collective-permute-start.10 = (bf16[128,1024]{1,0:T(8,128)(2,1)S(1)}, bf16[128,1024]{1,0:T(8,128)(2,1)S(1)}, u32[]{:S(2)}, u32[]{:S(2)}) collective-permute-start(bf16[128,1024]{1,0:T(8,128)(2,1)S(1)} %get-tuple-element.55.refs_0_), channel_id=1, source_target_pairs={{2,0},{4,2},{6,4},{7,6},{5,7},{3,5},{1,3},{0,1},{10,8},{12,10},{14... | collective-permute-start | bytes 786440 | tf_op jit(solution)/shard_map/ppermute | solution.py:228
  17.3 1.6 %collective-permute-start.4 = (bf16[128,1024]{1,0:T(8,128)(2,1)S(1)}, bf16[128,1024]{1,0:T(8,128)(2,1)S(1)}, u32[]{:S(2)}, u32[]{:S(2)}) collective-permute-start(bf16[128,1024]{1,0:T(8,128)(2,1)S(1)} %get-tuple-element.56.refs_1_), channel_id=1, source_target_pairs={{2,0},{4,2},{6,4},{7,6},{5,7},{3,5},{1,3},{0,1},{10,8},{12,10},{14... | collective-permute-start | bytes 786440 | tf_op jit(solution)/shard_map/ppermute | solution.py:228
  18.9 1.9 %shard_map.48 = (bf16[512,512]{1,0:T(8,128)(2,1)S(1)}, bf16[512,512]{1,0:T(8,128)(2,1)S(1)}) custom-call(s32[4,8]{1,0:T(4,128)S(1)} %bitcast.2, bf16[1024,512]{1,0:T(8,128)(2,1)} %x_ref), custom_call_target="tpu_custom_call" | custom-call | tf_op jit(solution)/shard_map/pallas_call | solution.py:185
  20.8 3.3 %collective-permute-done.9.refs_3_ = bf16[128,1024]{1,0:T(8,128)(2,1)S(1)} collective-permute-done((bf16[128,1024]{1,0:T(8,128)(2,1)S(1)}, bf16[128,1024]{1,0:T(8,128)(2,1)S(1)}, u32[]{:S(2)}, u32[]{:S(2)}) %collective-permute-start.9) | collective-permute-done | bytes 262176 | tf_op jit(solution)/shard_map/ppermute | solution.py:227
  24.5 1.5 %collective-permute-start.11 = (bf16[512,512]{1,0:T(8,128)(2,1)S(1)}, bf16[512,512]{1,0:T(8,128)(2,1)S(1)}, u32[]{:S(2)}, u32[]{:S(2)}) collective-permute-start(bf16[512,512]{1,0:T(8,128)(2,1)S(1)} %get-tuple-element.52.refs_11_.refs_5_), channel_id=1, source_target_pairs={{0,16},{8,24},{16,0},{24,8},{1,17},{9,25},{17,1},{25,9},{2,18},{10... | collective-permute-start | bytes 1572872 | tf_op jit(solution)/shard_map/ppermute | solution.py:242
  26.0 1.6 %collective-permute-start.14 = (bf16[128,1024]{1,0:T(8,128)(2,1)S(1)}, bf16[128,1024]{1,0:T(8,128)(2,1)S(1)}, u32[]{:S(2)}, u32[]{:S(2)}) collective-permute-start(bf16[128,1024]{1,0:T(8,128)(2,1)S(1)} %collective-permute-done.10.refs_4_), channel_id=1, source_target_pairs={{2,0},{4,2},{6,4},{7,6},{5,7},{3,5},{1,3},{0,1},{10,8},{12,10},{14... | collective-permute-start | bytes 786440 | tf_op jit(solution)/shard_map/ppermute | solution.py:228
  27.6 2.1 %collective-permute-done.refs_2_ = bf16[128,1024]{1,0:T(8,128)(2,1)S(1)} collective-permute-done((bf16[128,1024]{1,0:T(8,128)(2,1)S(1)}, bf16[128,1024]{1,0:T(8,128)(2,1)S(1)}, u32[]{:S(2)}, u32[]{:S(2)}) %collective-permute-start) | collective-permute-done | bytes 262176 | tf_op jit(solution)/shard_map/ppermute | solution.py:227
  30.2 1.6 %collective-permute-start.5 = (bf16[128,1024]{1,0:T(8,128)(2,1)S(1)}, bf16[128,1024]{1,0:T(8,128)(2,1)S(1)}, u32[]{:S(2)}, u32[]{:S(2)}) collective-permute-start(bf16[128,1024]{1,0:T(8,128)(2,1)S(1)} %collective-permute-done.4.refs_5_), channel_id=1, source_target_pairs={{2,0},{4,2},{6,4},{7,6},{5,7},{3,5},{1,3},{0,1},{10,8},{12,10},{14... | collective-permute-start | bytes 786440 | tf_op jit(solution)/shard_map/ppermute | solution.py:228
  31.7 3.6 %collective-permute-done.12.refs_7_ = bf16[128,1024]{1,0:T(8,128)(2,1)S(1)} collective-permute-done((bf16[128,1024]{1,0:T(8,128)(2,1)S(1)}, bf16[128,1024]{1,0:T(8,128)(2,1)S(1)}, u32[]{:S(2)}, u32[]{:S(2)}) %collective-permute-start.12) | collective-permute-done | bytes 262176 | tf_op jit(solution)/shard_map/ppermute | solution.py:227
  35.3 1.5 %collective-permute-start.8 = (bf16[512,512]{1,0:T(8,128)(2,1)S(1)}, bf16[512,512]{1,0:T(8,128)(2,1)S(1)}, u32[]{:S(2)}, u32[]{:S(2)}) collective-permute-start(bf16[512,512]{1,0:T(8,128)(2,1)S(1)} %get-tuple-element.51.refs_10_.refs_4_), channel_id=1, source_target_pairs={{0,16},{8,24},{16,0},{24,8},{1,17},{9,25},{17,1},{25,9},{2,18},{10... | collective-permute-start | bytes 1572872 | tf_op jit(solution)/shard_map/ppermute | solution.py:242
  37.3 3.7 %collective-permute-done.1.refs_6_ = bf16[128,1024]{1,0:T(8,128)(2,1)S(1)} collective-permute-done((bf16[128,1024]{1,0:T(8,128)(2,1)S(1)}, bf16[128,1024]{1,0:T(8,128)(2,1)S(1)}, u32[]{:S(2)}, u32[]{:S(2)}) %collective-permute-start.1) | collective-permute-done | bytes 262176 | tf_op jit(solution)/shard_map/ppermute | solution.py:227
  40.9 1.5 %collective-permute-start.15 = (bf16[128,1024]{1,0:T(8,128)(2,1)S(1)}, bf16[128,1024]{1,0:T(8,128)(2,1)S(1)}, u32[]{:S(2)}, u32[]{:S(2)}) collective-permute-start(bf16[128,1024]{1,0:T(8,128)(2,1)S(1)} %collective-permute-done.14.refs_8_), channel_id=1, source_target_pairs={{2,0},{4,2},{6,4},{7,6},{5,7},{3,5},{1,3},{0,1},{10,8},{12,10},{14... | collective-permute-start | bytes 786440 | tf_op jit(solution)/shard_map/ppermute | solution.py:228
  43.0 1.5 %collective-permute-start.6 = (bf16[128,1024]{1,0:T(8,128)(2,1)S(1)}, bf16[128,1024]{1,0:T(8,128)(2,1)S(1)}, u32[]{:S(2)}, u32[]{:S(2)}) collective-permute-start(bf16[128,1024]{1,0:T(8,128)(2,1)S(1)} %collective-permute-done.5.refs_9_), channel_id=1, source_target_pairs={{2,0},{4,2},{6,4},{7,6},{5,7},{3,5},{1,3},{0,1},{10,8},{12,10},{14... | collective-permute-start | bytes 786440 | tf_op jit(solution)/shard_map/ppermute | solution.py:228
  44.5 0.8 %collective-permute-done.13.refs_1_ = bf16[128,1024]{1,0:T(8,128)(2,1)S(1)} collective-permute-done((bf16[128,1024]{1,0:T(8,128)(2,1)S(1)}, bf16[128,1024]{1,0:T(8,128)(2,1)S(1)}, u32[]{:S(2)}, u32[]{:S(2)}) %collective-permute-start.13) | collective-permute-done | bytes 262176 | tf_op jit(solution)/shard_map/ppermute | solution.py:227
  45.3 2.0 %collective-permute-done.15.refs_2_ = bf16[128,1024]{1,0:T(8,128)(2,1)S(1)} collective-permute-done((bf16[128,1024]{1,0:T(8,128)(2,1)S(1)}, bf16[128,1024]{1,0:T(8,128)(2,1)S(1)}, u32[]{:S(2)}, u32[]{:S(2)}) %collective-permute-start.15) | collective-permute-done | bytes 262176 | tf_op jit(solution)/shard_map/ppermute | solution.py:228
  47.3 1.5 %collective-permute-done.2.refs_0_ = bf16[128,1024]{1,0:T(8,128)(2,1)S(1)} collective-permute-done((bf16[128,1024]{1,0:T(8,128)(2,1)S(1)}, bf16[128,1024]{1,0:T(8,128)(2,1)S(1)}, u32[]{:S(2)}, u32[]{:S(2)}) %collective-permute-start.2) | collective-permute-done | bytes 262176 | tf_op jit(solution)/shard_map/ppermute | solution.py:227
  48.8 1.3 %collective-permute-done.6.refs_3_ = bf16[128,1024]{1,0:T(8,128)(2,1)S(1)} collective-permute-done((bf16[128,1024]{1,0:T(8,128)(2,1)S(1)}, bf16[128,1024]{1,0:T(8,128)(2,1)S(1)}, u32[]{:S(2)}, u32[]{:S(2)}) %collective-permute-start.6) | collective-permute-done | bytes 262176 | tf_op jit(solution)/shard_map/ppermute | solution.py:228
  50.6 1.6 %collective-permute-start.7 = (bf16[128,1024]{1,0:T(8,128)(2,1)S(1)}, bf16[128,1024]{1,0:T(8,128)(2,1)S(1)}, u32[]{:S(2)}, u32[]{:S(2)}) collective-permute-start(bf16[128,1024]{1,0:T(8,128)(2,1)S(1)} %collective-permute-done.6.refs_3_), channel_id=1, source_target_pairs={{2,0},{4,2},{6,4},{7,6},{5,7},{3,5},{1,3},{0,1},{10,8},{12,10},{14... | collective-permute-start | bytes 786440 | tf_op jit(solution)/shard_map/ppermute | solution.py:228
  52.2 2.9 %shard_map.49.refs_12_ = f32[1024,512]{1,0:T(8,128)} custom-call(s32[4,64]{1,0:T(4,128)S(1)} %psum.7.mask_ref, bf16[128,1024]{1,0:T(8,128)(2,1)S(1)} %get-tuple-element.55.refs_0_, bf16[128,1024]{1,0:T(8,128)(2,1)S(1)} %get-tuple-element.56.refs_1_, bf16[128,1024]{1,0:T(8,128)(2,1)S(1)} %collective-permute-done.refs_2_, ...), custom_call_target="tpu_custom_call" | custom-call | tf_op jit(solution)/shard_map/pallas_call | solution.py:166
  55.1 2.1 %shard_map.50 = (f32[1024,512]{1,0:T(8,128)}, bf16[2048,512]{1,0:T(8,128)(2,1)S(1)}) custom-call(s32[4,64]{1,0:T(4,128)S(1)} %psum.7.mask_ref, bf16[128,1024]{1,0:T(8,128)(2,1)S(1)} %collective-permute-done.2.refs_0_, bf16[128,1024]{1,0:T(8,128)(2,1)S(1)} %collective-permute-done.13.refs_1_, ...), custom_call_target="tpu_custom_call", output_to_operand_aliasing={{0}: (13, {})} | custom-call | tf_op jit(solution)/shard_map/pallas_call | solution.py:166
  57.2 1.7 %collective-permute-done.3.refs_0_ = bf16[128,1024]{1,0:T(8,128)(2,1)S(1)} collective-permute-done((bf16[128,1024]{1,0:T(8,128)(2,1)S(1)}, bf16[128,1024]{1,0:T(8,128)(2,1)S(1)}, u32[]{:S(2)}, u32[]{:S(2)}) %collective-permute-start.3) | collective-permute-done | bytes 262176 | tf_op jit(solution)/shard_map/ppermute | solution.py:227
  59.0 1.2 %shard_map.51 = f32[1024,512]{1,0:T(8,128)} custom-call(bf16[128,1024]{1,0:T(8,128)(2,1)S(1)} %collective-permute-done.3.refs_0_, bf16[128,1024]{1,0:T(8,128)(2,1)S(1)} %collective-permute-done.7.refs_1_, bf16[2048,512]{1,0:T(8,128)(2,1)S(1)} %get-tuple-element.61.refs_2_, f32[1024,512]{1,0:T(8,128)} %get-tuple-element.62.refs_3_), custom_call_target="tpu_custom_call", output_to_operand_aliasing={{}: (3, {})} | custom-call | tf_op jit(solution)/shard_map/pallas_call | solution.py:261
  (25 shorter events, 3.9 us)
Async XLA Ops:
  0.0 18.9 %copy-start = (s32[8,4]{0,1:T(4,128)S(1)}, s32[8,4]{0,1:T(4,128)}, u32[]{:S(2)}) copy-start(s32[8,4]{0,1:T(4,128)} %param.7) | copy-start | bytes 388
  14.8 9.3 %collective-permute-start.9 = (bf16[128,1024]{1,0:T(8,128)(2,1)S(1)}, bf16[128,1024]{1,0:T(8,128)(2,1)S(1)}, u32[]{:S(2)}, u32[]{:S(2)}) collective-permute-start(bf16[128,1024]{1,0:T(8,128)(2,1)S(1)} %get-tuple-element.56.refs_1_), channel_id=1, source_target_pairs={{0,2},{2,4},{4,6},{6,7},{7,5},{5,3},{3,1},{1,0},{8,10},{10,12},{12... | collective-permute-start | bytes 786440 | tf_op jit(solution)/shard_map/ppermute | solution.py:227
  15.3 9.2 %collective-permute-start.10 = (bf16[128,1024]{1,0:T(8,128)(2,1)S(1)}, bf16[128,1024]{1,0:T(8,128)(2,1)S(1)}, u32[]{:S(2)}, u32[]{:S(2)}) collective-permute-start(bf16[128,1024]{1,0:T(8,128)(2,1)S(1)} %get-tuple-element.55.refs_0_), channel_id=1, source_target_pairs={{2,0},{4,2},{6,4},{7,6},{5,7},{3,5},{1,3},{0,1},{10,8},{12,10},{14... | collective-permute-start | bytes 786440 | tf_op jit(solution)/shard_map/ppermute | solution.py:228
  16.9 12.8 %collective-permute-start = (bf16[128,1024]{1,0:T(8,128)(2,1)S(1)}, bf16[128,1024]{1,0:T(8,128)(2,1)S(1)}, u32[]{:S(2)}, u32[]{:S(2)}) collective-permute-start(bf16[128,1024]{1,0:T(8,128)(2,1)S(1)} %get-tuple-element.55.refs_0_), channel_id=1, source_target_pairs={{0,2},{2,4},{4,6},{6,7},{7,5},{5,3},{3,1},{1,0},{8,10},{10,12},{12... | collective-permute-start | bytes 786440 | tf_op jit(solution)/shard_map/ppermute | solution.py:227
  17.3 12.8 %collective-permute-start.4 = (bf16[128,1024]{1,0:T(8,128)(2,1)S(1)}, bf16[128,1024]{1,0:T(8,128)(2,1)S(1)}, u32[]{:S(2)}, u32[]{:S(2)}) collective-permute-start(bf16[128,1024]{1,0:T(8,128)(2,1)S(1)} %get-tuple-element.56.refs_1_), channel_id=1, source_target_pairs={{2,0},{4,2},{6,4},{7,6},{5,7},{3,5},{1,3},{0,1},{10,8},{12,10},{14... | collective-permute-start | bytes 786440 | tf_op jit(solution)/shard_map/ppermute | solution.py:228
  24.1 11.2 %collective-permute-start.12 = (bf16[128,1024]{1,0:T(8,128)(2,1)S(1)}, bf16[128,1024]{1,0:T(8,128)(2,1)S(1)}, u32[]{:S(2)}, u32[]{:S(2)}) collective-permute-start(bf16[128,1024]{1,0:T(8,128)(2,1)S(1)} %collective-permute-done.9.refs_3_), channel_id=1, source_target_pairs={{0,2},{2,4},{4,6},{6,7},{7,5},{5,3},{3,1},{1,0},{8,10},{10,12},{12... | collective-permute-start | bytes 786440 | tf_op jit(solution)/shard_map/ppermute | solution.py:227
  24.5 18.4 %collective-permute-start.11 = (bf16[512,512]{1,0:T(8,128)(2,1)S(1)}, bf16[512,512]{1,0:T(8,128)(2,1)S(1)}, u32[]{:S(2)}, u32[]{:S(2)}) collective-permute-start(bf16[512,512]{1,0:T(8,128)(2,1)S(1)} %get-tuple-element.52.refs_11_.refs_5_), channel_id=1, source_target_pairs={{0,16},{8,24},{16,0},{24,8},{1,17},{9,25},{17,1},{25,9},{2,18},{10... | collective-permute-start | bytes 1572872 | tf_op jit(solution)/shard_map/ppermute | solution.py:242
  26.0 10.8 %collective-permute-start.14 = (bf16[128,1024]{1,0:T(8,128)(2,1)S(1)}, bf16[128,1024]{1,0:T(8,128)(2,1)S(1)}, u32[]{:S(2)}, u32[]{:S(2)}) collective-permute-start(bf16[128,1024]{1,0:T(8,128)(2,1)S(1)} %collective-permute-done.10.refs_4_), channel_id=1, source_target_pairs={{2,0},{4,2},{6,4},{7,6},{5,7},{3,5},{1,3},{0,1},{10,8},{12,10},{14... | collective-permute-start | bytes 786440 | tf_op jit(solution)/shard_map/ppermute | solution.py:228
  29.7 11.2 %collective-permute-start.1 = (bf16[128,1024]{1,0:T(8,128)(2,1)S(1)}, bf16[128,1024]{1,0:T(8,128)(2,1)S(1)}, u32[]{:S(2)}, u32[]{:S(2)}) collective-permute-start(bf16[128,1024]{1,0:T(8,128)(2,1)S(1)} %collective-permute-done.refs_2_), channel_id=1, source_target_pairs={{0,2},{2,4},{4,6},{6,7},{7,5},{5,3},{3,1},{1,0},{8,10},{10,12},{12... | collective-permute-start | bytes 786440 | tf_op jit(solution)/shard_map/ppermute | solution.py:227
  30.2 12.3 %collective-permute-start.5 = (bf16[128,1024]{1,0:T(8,128)(2,1)S(1)}, bf16[128,1024]{1,0:T(8,128)(2,1)S(1)}, u32[]{:S(2)}, u32[]{:S(2)}) collective-permute-start(bf16[128,1024]{1,0:T(8,128)(2,1)S(1)} %collective-permute-done.4.refs_5_), channel_id=1, source_target_pairs={{2,0},{4,2},{6,4},{7,6},{5,7},{3,5},{1,3},{0,1},{10,8},{12,10},{14... | collective-permute-start | bytes 786440 | tf_op jit(solution)/shard_map/ppermute | solution.py:228
  35.3 13.5 %collective-permute-start.8 = (bf16[512,512]{1,0:T(8,128)(2,1)S(1)}, bf16[512,512]{1,0:T(8,128)(2,1)S(1)}, u32[]{:S(2)}, u32[]{:S(2)}) collective-permute-start(bf16[512,512]{1,0:T(8,128)(2,1)S(1)} %get-tuple-element.51.refs_10_.refs_4_), channel_id=1, source_target_pairs={{0,16},{8,24},{16,0},{24,8},{1,17},{9,25},{17,1},{25,9},{2,18},{10... | collective-permute-start | bytes 1572872 | tf_op jit(solution)/shard_map/ppermute | solution.py:242
  36.8 8.5 %collective-permute-start.13 = (bf16[128,1024]{1,0:T(8,128)(2,1)S(1)}, bf16[128,1024]{1,0:T(8,128)(2,1)S(1)}, u32[]{:S(2)}, u32[]{:S(2)}) collective-permute-start(bf16[128,1024]{1,0:T(8,128)(2,1)S(1)} %collective-permute-done.12.refs_7_), channel_id=1, source_target_pairs={{0,2},{2,4},{4,6},{6,7},{7,5},{5,3},{3,1},{1,0},{8,10},{10,12},{12... | collective-permute-start | bytes 786440 | tf_op jit(solution)/shard_map/ppermute | solution.py:227
  40.9 6.4 %collective-permute-start.15 = (bf16[128,1024]{1,0:T(8,128)(2,1)S(1)}, bf16[128,1024]{1,0:T(8,128)(2,1)S(1)}, u32[]{:S(2)}, u32[]{:S(2)}) collective-permute-start(bf16[128,1024]{1,0:T(8,128)(2,1)S(1)} %collective-permute-done.14.refs_8_), channel_id=1, source_target_pairs={{2,0},{4,2},{6,4},{7,6},{5,7},{3,5},{1,3},{0,1},{10,8},{12,10},{14... | collective-permute-start | bytes 786440 | tf_op jit(solution)/shard_map/ppermute | solution.py:228
  42.5 6.4 %collective-permute-start.2 = (bf16[128,1024]{1,0:T(8,128)(2,1)S(1)}, bf16[128,1024]{1,0:T(8,128)(2,1)S(1)}, u32[]{:S(2)}, u32[]{:S(2)}) collective-permute-start(bf16[128,1024]{1,0:T(8,128)(2,1)S(1)} %collective-permute-done.1.refs_6_), channel_id=1, source_target_pairs={{0,2},{2,4},{4,6},{6,7},{7,5},{5,3},{3,1},{1,0},{8,10},{10,12},{12... | collective-permute-start | bytes 786440 | tf_op jit(solution)/shard_map/ppermute | solution.py:227
  43.0 7.1 %collective-permute-start.6 = (bf16[128,1024]{1,0:T(8,128)(2,1)S(1)}, bf16[128,1024]{1,0:T(8,128)(2,1)S(1)}, u32[]{:S(2)}, u32[]{:S(2)}) collective-permute-start(bf16[128,1024]{1,0:T(8,128)(2,1)S(1)} %collective-permute-done.5.refs_9_), channel_id=1, source_target_pairs={{2,0},{4,2},{6,4},{7,6},{5,7},{3,5},{1,3},{0,1},{10,8},{12,10},{14... | collective-permute-start | bytes 786440 | tf_op jit(solution)/shard_map/ppermute | solution.py:228
  45.3 5.3 %collective-permute-start.16 = (bf16[512,512]{1,0:T(8,128)(2,1)S(1)}, bf16[512,512]{1,0:T(8,128)(2,1)S(1)}, u32[]{:S(2)}, u32[]{:S(2)}) collective-permute-start(bf16[512,512]{1,0:T(8,128)(2,1)S(1)} %get-tuple-element.51.refs_10_.refs_4_), channel_id=1, source_target_pairs={{0,8},{8,0},{16,24},{24,16},{1,9},{9,1},{17,25},{25,17},{2,10},{10... | collective-permute-start | bytes 1572872 | tf_op jit(solution)/shard_map/ppermute | solution.py:242
  47.3 4.8 %collective-permute-start.19 = (bf16[512,512]{1,0:T(8,128)(2,1)S(1)}, bf16[512,512]{1,0:T(8,128)(2,1)S(1)}, u32[]{:S(2)}, u32[]{:S(2)}) collective-permute-start(bf16[512,512]{1,0:T(8,128)(2,1)S(1)} %collective-permute-done.11.refs_15_.refs_9_), channel_id=1, source_target_pairs={{0,8},{8,0},{16,24},{24,16},{1,9},{9,1},{17,25},{25,17},{2,10},{10... | collective-permute-start | bytes 1572872 | tf_op jit(solution)/shard_map/ppermute | solution.py:242
  48.8 3.3 %collective-permute-start.18 = (bf16[512,512]{1,0:T(8,128)(2,1)S(1)}, bf16[512,512]{1,0:T(8,128)(2,1)S(1)}, u32[]{:S(2)}, u32[]{:S(2)}) collective-permute-start(bf16[512,512]{1,0:T(8,128)(2,1)S(1)} %collective-permute-done.8.refs_14_.refs_8_), channel_id=1, source_target_pairs={{0,8},{8,0},{16,24},{24,16},{1,9},{9,1},{17,25},{25,17},{2,10},{10... | collective-permute-start | bytes 1572872 | tf_op jit(solution)/shard_map/ppermute | solution.py:242
  50.1 2.0 %collective-permute-start.17 = (bf16[512,512]{1,0:T(8,128)(2,1)S(1)}, bf16[512,512]{1,0:T(8,128)(2,1)S(1)}, u32[]{:S(2)}, u32[]{:S(2)}) collective-permute-start(bf16[512,512]{1,0:T(8,128)(2,1)S(1)} %get-tuple-element.52.refs_11_.refs_5_), channel_id=1, source_target_pairs={{0,8},{8,0},{16,24},{24,16},{1,9},{9,1},{17,25},{25,17},{2,10},{10... | collective-permute-start | bytes 1572872 | tf_op jit(solution)/shard_map/ppermute | solution.py:242
  50.1 8.7 %collective-permute-start.3 = (bf16[128,1024]{1,0:T(8,128)(2,1)S(1)}, bf16[128,1024]{1,0:T(8,128)(2,1)S(1)}, u32[]{:S(2)}, u32[]{:S(2)}) collective-permute-start(bf16[128,1024]{1,0:T(8,128)(2,1)S(1)} %collective-permute-done.2.refs_0_), channel_id=1, source_target_pairs={{0,2},{2,4},{4,6},{6,7},{7,5},{5,3},{3,1},{1,0},{8,10},{10,12},{12... | collective-permute-start | bytes 786440 | tf_op jit(solution)/shard_map/ppermute | solution.py:227
  50.6 8.4 %collective-permute-start.7 = (bf16[128,1024]{1,0:T(8,128)(2,1)S(1)}, bf16[128,1024]{1,0:T(8,128)(2,1)S(1)}, u32[]{:S(2)}, u32[]{:S(2)}) collective-permute-start(bf16[128,1024]{1,0:T(8,128)(2,1)S(1)} %collective-permute-done.6.refs_3_), channel_id=1, source_target_pairs={{2,0},{4,2},{6,4},{7,6},{5,7},{3,5},{1,3},{0,1},{10,8},{12,10},{14... | collective-permute-start | bytes 786440 | tf_op jit(solution)/shard_map/ppermute | solution.py:228

commit v5 on v4

--- a/solution.py
+++ b/solution.py
@@ -34,30 +34,19 @@
     return lo, hi
 
 
-def mask_ints_kernel(mask_ref, x_ref, *refs):
-    outs, buf, sem = refs[:-2], refs[-2], refs[-1]
-    nt, kt = mask_ref.shape
-    copies = []
-    for g in range(len(outs)):
-        at = pl.ds(g * GROUP * TILE, GROUP * TILE)
-        copies.append(pltpu.make_async_copy(x_ref.at[at, :], buf.at[g], sem.at[g]))
-        copies[-1].start()
-    for g, out in enumerate(outs):
-        copies[g].wait()
-        for q in range(GROUP):
-            for t in range(nt):
-                at = (pl.ds(q * TILE, TILE), pl.ds(t * TILE, TILE))
-                x = buf[g, at[0], at[1]]
-                out[at] = jnp.where(mask_ref[t, g * GROUP + q] != 0, x, jnp.zeros_like(x))
-
-
-def stage_kernel(mask_ref, a_ref, o_ref, held_ref, m_ref, sem):
+def stage_kernel(mask_ref, a_ref, int_mask_ref, x_ref, o_ref, held_ref, *refs):
+    pieces, (m_ref, sem), inner, (held_mask, mask_sem) = refs[:-6], refs[-6:-4], refs[-4:-2], refs[-2:]
+    load = pltpu.make_async_copy(int_mask_ref, held_mask, mask_sem)
+    load.start()
     half = a_ref.shape[0] // 2
     copies = [
         pltpu.make_async_copy(a_ref.at[pl.ds(i * half, half), :], held_ref.at[pl.ds(i * half, half), :], sem.at[i]) for i in range(2)
     ]
+    loads = []
+    for g in range(len(pieces)):
+        loads.append(pltpu.make_async_copy(x_ref.at[pl.ds(g * GROUP * TILE, GROUP * TILE), :], inner[0].at[g], inner[1].at[g]))
     copies.insert(0, pltpu.make_async_copy(mask_ref, m_ref, sem.at[2]))
-    for copy in copies:
+    for copy in copies[:1] + loads + copies[1:]:
         copy.start()
     tile_rows, wide = m_ref.shape[1], o_ref.shape[1]
     row = lax.broadcasted_iota(jnp.int32, (tile_rows, wide), 0)
@@ -66,6 +55,14 @@
     copies.pop(0).wait()
     piece = m_ref[...].astype(jnp.float32).astype(jnp.bfloat16)
     o_ref[...] = jnp.dot(piece, spread, preferred_element_type=jnp.float32).astype(jnp.int32)
+    load.wait()
+    for g, out in enumerate(pieces):
+        loads[g].wait()
+        for q in range(GROUP):
+            for t in range(held_mask.shape[0]):
+                at = (pl.ds(q * TILE, TILE), pl.ds(t * TILE, TILE))
+                x = inner[0][g, at[0], at[1]]
+                out[at] = jnp.where(held_mask[t, g * GROUP + q] != 0, x, jnp.zeros_like(x))
     for copy in copies:
         copy.wait()
 
@@ -181,28 +178,36 @@
     n_groups = kt_local // GROUP
     piece = jax.ShapeDtypeStruct((GROUP * TILE, integrals.shape[1]), integrals.dtype)
 
-    def masked_ints(x):
-        return pl.pallas_call(
-            mask_ints_kernel,
-            out_shape=[piece] * n_groups,
-            in_specs=[_smem, _hbm],
-            out_specs=[_vmem] * n_groups,
-            scratch_shapes=[pltpu.VMEM((n_groups, *piece.shape), piece.dtype), pltpu.SemaphoreType.DMA((n_groups,))],
-            compiler_params=_params,
-        )(integral_tile_mask.T, pltpu.with_memory_space_constraint(x, pltpu.HBM))
-
-    placed, amps = pl.pallas_call(
+    placed, amps, *masked = pl.pallas_call(
         stage_kernel,
         out_shape=[
             jax.ShapeDtypeStruct((kblock, n_col * tile_rows), jnp.int32),
             jax.ShapeDtypeStruct(amps.shape, amps.dtype),
+            *[piece] * n_groups,
         ],
-        in_specs=[_hbm, _hbm],
-        out_specs=[_vmem] * 2,
-        scratch_shapes=[pltpu.VMEM((kblock, tile_rows), jnp.int32), pltpu.SemaphoreType.DMA((3,))],
-        compiler_params=_params,
-    )(pltpu.with_memory_space_constraint(amplitude_tile_mask.T, pltpu.HBM), pltpu.with_memory_space_constraint(amps, pltpu.HBM))
+        in_specs=[_hbm] * 4,
+        out_specs=[_vmem] * (2 + n_groups),
+        scratch_shapes=[
+            pltpu.VMEM((kblock, tile_rows), jnp.int32),
+            pltpu.SemaphoreType.DMA((3,)),
+            pltpu.VMEM((n_groups, *piece.shape), piece.dtype),
+            pltpu.SemaphoreType.DMA((n_groups,)),
+            pltpu.SMEM(integral_tile_mask.shape[::-1], jnp.int32),
+            pltpu.SemaphoreType.DMA,
+        ],
+        compiler_params=_params,
+    )(
+        pltpu.with_memory_space_constraint(amplitude_tile_mask.T, pltpu.HBM),
+        pltpu.with_memory_space_constraint(amps, pltpu.HBM),
+        pltpu.with_memory_space_constraint(integral_tile_mask.T, pltpu.HBM),
+        pltpu.with_memory_space_constraint(integrals, pltpu.HBM),
+    )
+    def swap(x, j):
+        return lax.ppermute(x, "row", [(i, i ^ j) for i in range(n_row)])
+
+    sibling = [swap(p, 1) for p in masked]
     mask = lax.psum(placed, "col")
+    amps, *sibling = lax.optimization_barrier((amps, *sibling))
 
     half = (rows, depth * KEEP // GROUP // 2)
     own = pl.pallas_call(
@@ -238,19 +243,17 @@
             *values, held[b][1 - t] = lax.optimization_barrier((*values, held[b][1 - t]))
         return values
 
-    def swap(x, j):
-        return lax.ppermute(x, "row", [(i, i ^ j) for i in range(n_row)])
-
-    late, *held[0] = lax.optimization_barrier((integrals, *held[0]))
-    pieces = {0: list(masked_ints(late))}
+    masked[0], masked[1], *held[0] = lax.optimization_barrier((masked[0], masked[1], *held[0]))
+    pieces = {0: masked, 1: sibling}
     for j in range(2, n_row, 2):
-        late = [pieces[0][0], *after(1, pieces[0][1:], 'b')]
-        pieces[j] = [swap(p, j) for p in late]
-    for j in range(0, n_row, 2):
-        pieces[j + 1] = [None] * n_groups
-        for g in range(n_groups):
-            (pieces[j][g],) = after((0, 4, 4, 5)[min(j, 2) + g], (pieces[j][g],), 'bbub'[min(j, 2) + g])
-            pieces[j + 1][g] = swap(pieces[j][g], 1)
+        pieces[j] = []
+        for p, turn in zip(masked, (0, 1)):
+            (p,) = after(turn, (p,), "b")
+            pieces[j].append(swap(p, j))
+        pieces[j + 1] = []
+        for g, turn in enumerate((4, 5)):
+            (pieces[j][g],) = after(turn, (pieces[j][g],), "b")
+            pieces[j + 1].append(swap(pieces[j][g], 1))
     ints = [p for j in range(n_row) for p in pieces[j]]
 
     out = None

time: 60.3 us -> 62.2 us (1.032)
  waiting for transfers between devices: 20.1 us -> 22.8 us
  Pallas kernels: 9.73 us -> 8.32 us
    ppermute x7, waiting for transfers between devices: 16.6 us -> 19.5 us  [on_device(): held[k][t] = lax.ppermute(held[k - 1][t], 'col', up)]
    pallas_call x1 -> x0, Pallas kernels: 1.9 us -> none  [masked_ints(): pl.pallas_call(mask_ints_kernel, out_shape=[piece] * n_groups, in_specs=[...]
  transfers between devices with their start and end apart: 20 -> 20, of which waited for: 10 -> 9; matrix products, arithmetic and copies ran while one was open for 0% -> 0% of each run, Pallas kernels for 11% -> 8%
where the time goes in v5:
time: 62.2 us; the launch traced here: 62 us
  waiting for transfers between devices  22.8 us (37%)
  starting transfers between devices  17.8 us (29%)
  blocking collectives  13 us (21%)
  Pallas kernels  8.32 us (13%)
    ppermute x7, waiting for transfers between devices, on_device(): held[k][t] = lax.ppermute(held[k - 1][t], 'col', up)  19.5 us
    psum x1, blocking collectives, on_device(): mask = lax.psum(placed, 'col')  13 us
    ppermute x7, starting transfers between devices, on_device(): held[b][1 - t] = lax.ppermute(held[(b + 1) % n_col][1 - t], 'col', down)  11.1 us
    pallas_call x2, Pallas kernels, ladder_rows(): pl.pallas_call(functools.partial(ladder_kernel, n_row, n_col, kt_local, s...  5.14 us
    ppermute x6, starting transfers between devices, swap(): return lax.ppermute(x, 'row', [(i, i ^ j) for i in range(n_row)])  3.58 us
    ppermute x7, waiting for transfers between devices, on_device(): held[b][1 - t] = lax.ppermute(held[(b + 1) % n_col][1 - t], 'col', down)  3.31 us
    ppermute x7, starting transfers between devices, on_device(): held[k][t] = lax.ppermute(held[k - 1][t], 'col', up)  3.11 us
    pallas_call x1, Pallas kernels, on_device(): pl.pallas_call(stage_kernel, out_shape=[jax.ShapeDtypeStruct((kblock, n_c...  1.58 us
  transfers between devices with their start and end apart: 20, of which 9 were waited for; matrix products, arithmetic and copies ran while one was open for 0% of the time, Pallas kernels for 8%

profile of v5, /device:TPU:0, one launch (start us, length us, event | category | flops | bytes accessed | tf_op | source)
XLA Modules:
  0.0 62.0 jit_solution(4411817961996205268)
XLA Ops:
  0.0 1.6 %shard_map.46 = (s32[4,64]{1,0:T(4,128)S(1)}, bf16[128,4096]{1,0:T(8,128)(2,1)S(1)}, bf16[512,512]{1,0:T(8,128)(2,1)S(1)}, bf16[512,512]{1,0:T(8,128)(2,1)S(1)}) custom-call(s32[4,8]{1,0:T(4,128)} %bitcast.2, bf16[128,4096]{1,0:T(8,128)(2,1)} %a_ref.1, s32[4,8]{1,0:T(4,128)} %bitcast.3, bf16[1024,512]{1,0:T(8,128)(2,1)} %x_ref.1), custom_call_target="tpu_custom_call" | custom-call | tf_op jit(solution)/shard_map/pallas_call | solution.py:181
  1.6 0.5 collective-permute-start
  2.2 13.0 %psum.7.mask_ref = s32[4,64]{1,0:T(4,128)S(1)} all-reduce(s32[4,64]{1,0:T(4,128)S(1)} %get-tuple-element.36), channel_id=1, replica_groups=mesh['row'=4,'col'=8] {'col'}, use_global_device_ids=true, to_apply=%region_0.0 | all-reduce | flops 256 | bytes 2048 | tf_op jit(solution)/shard_map/psum | solution.py:209
  16.2 1.6 %collective-permute-start.6 = (bf16[128,1024]{1,0:T(8,128)(2,1)S(1)}, bf16[128,1024]{1,0:T(8,128)(2,1)S(1)}, u32[]{:S(2)}, u32[]{:S(2)}) collective-permute-start(bf16[128,1024]{1,0:T(8,128)(2,1)S(1)} %get-tuple-element.60.refs_1_), channel_id=1, source_target_pairs={{2,0},{4,2},{6,4},{7,6},{5,7},{3,5},{1,3},{0,1},{10,8},{12,10},{14... | collective-permute-start | bytes 786440 | tf_op jit(solution)/shard_map/ppermute | solution.py:233
  18.2 1.6 %collective-permute-start.12 = (bf16[128,1024]{1,0:T(8,128)(2,1)S(1)}, bf16[128,1024]{1,0:T(8,128)(2,1)S(1)}, u32[]{:S(2)}, u32[]{:S(2)}) collective-permute-start(bf16[128,1024]{1,0:T(8,128)(2,1)S(1)} %get-tuple-element.59.refs_0_), channel_id=1, source_target_pairs={{2,0},{4,2},{6,4},{7,6},{5,7},{3,5},{1,3},{0,1},{10,8},{12,10},{14... | collective-permute-start | bytes 786440 | tf_op jit(solution)/shard_map/ppermute | solution.py:233
  19.8 5.2 %collective-permute-done.2.refs_2_ = bf16[128,1024]{1,0:T(8,128)(2,1)S(1)} collective-permute-done((bf16[128,1024]{1,0:T(8,128)(2,1)S(1)}, bf16[128,1024]{1,0:T(8,128)(2,1)S(1)}, u32[]{:S(2)}, u32[]{:S(2)}) %collective-permute-start.2) | collective-permute-done | bytes 262176 | tf_op jit(solution)/shard_map/ppermute | solution.py:232
  25.4 1.5 %collective-permute-start.10 = (bf16[512,512]{1,0:T(8,128)(2,1)S(1)}, bf16[512,512]{1,0:T(8,128)(2,1)S(1)}, u32[]{:S(2)}, u32[]{:S(2)}) collective-permute-start(bf16[512,512]{1,0:T(8,128)(2,1)S(1)} %get-tuple-element.45.refs_10_.refs_4_), channel_id=1, source_target_pairs={{0,16},{8,24},{16,0},{24,8},{1,17},{9,25},{17,1},{25,9},{2,18},{10... | collective-permute-start | bytes 1572872 | tf_op jit(solution)/shard_map/ppermute | solution.py:206
  26.9 1.6 %collective-permute-start.7 = (bf16[128,1024]{1,0:T(8,128)(2,1)S(1)}, bf16[128,1024]{1,0:T(8,128)(2,1)S(1)}, u32[]{:S(2)}, u32[]{:S(2)}) collective-permute-start(bf16[128,1024]{1,0:T(8,128)(2,1)S(1)} %collective-permute-done.6.refs_5_), channel_id=1, source_target_pairs={{2,0},{4,2},{6,4},{7,6},{5,7},{3,5},{1,3},{0,1},{10,8},{12,10},{14... | collective-permute-start | bytes 786440 | tf_op jit(solution)/shard_map/ppermute | solution.py:233
  28.5 2.1 %collective-permute-done.11.refs_3_ = bf16[128,1024]{1,0:T(8,128)(2,1)S(1)} collective-permute-done((bf16[128,1024]{1,0:T(8,128)(2,1)S(1)}, bf16[128,1024]{1,0:T(8,128)(2,1)S(1)}, u32[]{:S(2)}, u32[]{:S(2)}) %collective-permute-start.11) | collective-permute-done | bytes 262176 | tf_op jit(solution)/shard_map/ppermute | solution.py:232
  31.0 1.5 %collective-permute-start.13 = (bf16[512,512]{1,0:T(8,128)(2,1)S(1)}, bf16[512,512]{1,0:T(8,128)(2,1)S(1)}, u32[]{:S(2)}, u32[]{:S(2)}) collective-permute-start(bf16[512,512]{1,0:T(8,128)(2,1)S(1)} %get-tuple-element.49.refs_11_.refs_5_), channel_id=1, source_target_pairs={{0,16},{8,24},{16,0},{24,8},{1,17},{9,25},{17,1},{25,9},{2,18},{10... | collective-permute-start | bytes 1572872 | tf_op jit(solution)/shard_map/ppermute | solution.py:206
  32.5 3.7 %collective-permute-done.3.refs_6_ = bf16[128,1024]{1,0:T(8,128)(2,1)S(1)} collective-permute-done((bf16[128,1024]{1,0:T(8,128)(2,1)S(1)}, bf16[128,1024]{1,0:T(8,128)(2,1)S(1)}, u32[]{:S(2)}, u32[]{:S(2)}) %collective-permute-start.3) | collective-permute-done | bytes 262176 | tf_op jit(solution)/shard_map/ppermute | solution.py:232
  36.2 1.5 %collective-permute-start.16 = (bf16[128,1024]{1,0:T(8,128)(2,1)S(1)}, bf16[128,1024]{1,0:T(8,128)(2,1)S(1)}, u32[]{:S(2)}, u32[]{:S(2)}) collective-permute-start(bf16[128,1024]{1,0:T(8,128)(2,1)S(1)} %collective-permute-done.12.refs_4_), channel_id=1, source_target_pairs={{2,0},{4,2},{6,4},{7,6},{5,7},{3,5},{1,3},{0,1},{10,8},{12,10},{14... | collective-permute-start | bytes 786440 | tf_op jit(solution)/shard_map/ppermute | solution.py:233
  37.7 0.5 collective-permute-start.4
  38.2 3.6 %collective-permute-done.14.refs_7_ = bf16[128,1024]{1,0:T(8,128)(2,1)S(1)} collective-permute-done((bf16[128,1024]{1,0:T(8,128)(2,1)S(1)}, bf16[128,1024]{1,0:T(8,128)(2,1)S(1)}, u32[]{:S(2)}, u32[]{:S(2)}) %collective-permute-start.14) | collective-permute-done | bytes 262176 | tf_op jit(solution)/shard_map/ppermute | solution.py:232
  41.8 1.5 %collective-permute-start.8 = (bf16[128,1024]{1,0:T(8,128)(2,1)S(1)}, bf16[128,1024]{1,0:T(8,128)(2,1)S(1)}, u32[]{:S(2)}, u32[]{:S(2)}) collective-permute-start(bf16[128,1024]{1,0:T(8,128)(2,1)S(1)} %collective-permute-done.7.refs_9_), channel_id=1, source_target_pairs={{2,0},{4,2},{6,4},{7,6},{5,7},{3,5},{1,3},{0,1},{10,8},{12,10},{14... | collective-permute-start | bytes 786440 | tf_op jit(solution)/shard_map/ppermute | solution.py:233
  43.4 1.9 %collective-permute-done.16.refs_8_ = bf16[128,1024]{1,0:T(8,128)(2,1)S(1)} collective-permute-done((bf16[128,1024]{1,0:T(8,128)(2,1)S(1)}, bf16[128,1024]{1,0:T(8,128)(2,1)S(1)}, u32[]{:S(2)}, u32[]{:S(2)}) %collective-permute-start.16) | collective-permute-done | bytes 262176 | tf_op jit(solution)/shard_map/ppermute | solution.py:233
  45.8 1.5 %collective-permute-start.17 = (bf16[128,1024]{1,0:T(8,128)(2,1)S(1)}, bf16[128,1024]{1,0:T(8,128)(2,1)S(1)}, u32[]{:S(2)}, u32[]{:S(2)}) collective-permute-start(bf16[128,1024]{1,0:T(8,128)(2,1)S(1)} %collective-permute-done.16.refs_8_), channel_id=1, source_target_pairs={{2,0},{4,2},{6,4},{7,6},{5,7},{3,5},{1,3},{0,1},{10,8},{12,10},{14... | collective-permute-start | bytes 786440 | tf_op jit(solution)/shard_map/ppermute | solution.py:233
  47.3 0.9 %collective-permute-done.8.refs_3_ = bf16[128,1024]{1,0:T(8,128)(2,1)S(1)} collective-permute-done((bf16[128,1024]{1,0:T(8,128)(2,1)S(1)}, bf16[128,1024]{1,0:T(8,128)(2,1)S(1)}, u32[]{:S(2)}, u32[]{:S(2)}) %collective-permute-start.8) | collective-permute-done | bytes 262176 | tf_op jit(solution)/shard_map/ppermute | solution.py:233
  48.2 3.4 %collective-permute-done.15.refs_1_ = bf16[128,1024]{1,0:T(8,128)(2,1)S(1)} collective-permute-done((bf16[128,1024]{1,0:T(8,128)(2,1)S(1)}, bf16[128,1024]{1,0:T(8,128)(2,1)S(1)}, u32[]{:S(2)}, u32[]{:S(2)}) %collective-permute-start.15) | collective-permute-done | bytes 262176 | tf_op jit(solution)/shard_map/ppermute | solution.py:232
  52.4 1.8 %collective-permute-start.9 = (bf16[128,1024]{1,0:T(8,128)(2,1)S(1)}, bf16[128,1024]{1,0:T(8,128)(2,1)S(1)}, u32[]{:S(2)}, u32[]{:S(2)}) collective-permute-start(bf16[128,1024]{1,0:T(8,128)(2,1)S(1)} %collective-permute-done.8.refs_3_), channel_id=1, source_target_pairs={{2,0},{4,2},{6,4},{7,6},{5,7},{3,5},{1,3},{0,1},{10,8},{12,10},{14... | collective-permute-start | bytes 786440 | tf_op jit(solution)/shard_map/ppermute | solution.py:233
  54.2 3.0 %shard_map.48.refs_12_ = f32[1024,512]{1,0:T(8,128)} custom-call(s32[4,64]{1,0:T(4,128)S(1)} %psum.7.mask_ref, bf16[128,1024]{1,0:T(8,128)(2,1)S(1)} %get-tuple-element.59.refs_0_, bf16[128,1024]{1,0:T(8,128)(2,1)S(1)} %get-tuple-element.60.refs_1_, bf16[128,1024]{1,0:T(8,128)(2,1)S(1)} %collective-permute-done.2.refs_2_, ...), custom_call_target="tpu_custom_call" | custom-call | tf_op jit(solution)/shard_map/pallas_call | solution.py:163
  57.2 2.1 %shard_map.49 = (f32[1024,512]{1,0:T(8,128)}, bf16[2048,512]{1,0:T(8,128)(2,1)S(1)}) custom-call(s32[4,64]{1,0:T(4,128)S(1)} %psum.7.mask_ref, bf16[128,1024]{1,0:T(8,128)(2,1)S(1)} %collective-permute-done.4.refs_0_, bf16[128,1024]{1,0:T(8,128)(2,1)S(1)} %collective-permute-done.15.refs_1_, ...), custom_call_target="tpu_custom_call", output_to_operand_aliasing={{0}: (13, {})} | custom-call | tf_op jit(solution)/shard_map/pallas_call | solution.py:163
  59.3 1.5 %collective-permute-done.5.refs_0_ = bf16[128,1024]{1,0:T(8,128)(2,1)S(1)} collective-permute-done((bf16[128,1024]{1,0:T(8,128)(2,1)S(1)}, bf16[128,1024]{1,0:T(8,128)(2,1)S(1)}, u32[]{:S(2)}, u32[]{:S(2)}) %collective-permute-start.5) | collective-permute-done | bytes 262176 | tf_op jit(solution)/shard_map/ppermute | solution.py:232
  60.9 1.2 %shard_map.50 = f32[1024,512]{1,0:T(8,128)} custom-call(bf16[128,1024]{1,0:T(8,128)(2,1)S(1)} %collective-permute-done.5.refs_0_, bf16[128,1024]{1,0:T(8,128)(2,1)S(1)} %collective-permute-done.9.refs_1_, bf16[2048,512]{1,0:T(8,128)(2,1)S(1)} %get-tuple-element.65.refs_2_, f32[1024,512]{1,0:T(8,128)} %get-tuple-element.66.refs_3_), custom_call_target="tpu_custom_call", output_to_operand_aliasing={{}: (3, {})} | custom-call | tf_op jit(solution)/shard_map/pallas_call | solution.py:264
  (22 shorter events, 3.6 us)
Async XLA Ops:
  1.6 13.6 %collective-permute-start = (bf16[512,512]{1,0:T(8,128)(2,1)S(1)}, bf16[512,512]{1,0:T(8,128)(2,1)S(1)}, u32[]{:S(2)}, u32[]{:S(2)}) collective-permute-start(bf16[512,512]{1,0:T(8,128)(2,1)S(1)} %get-tuple-element.45.refs_10_.refs_4_), channel_id=1, source_target_pairs={{0,8},{8,0},{16,24},{24,16},{1,9},{9,1},{17,25},{25,17},{2,10},{10... | collective-permute-start | bytes 1572872 | tf_op jit(solution)/shard_map/ppermute | solution.py:206
  2.1 13.1 %collective-permute-start.1 = (bf16[512,512]{1,0:T(8,128)(2,1)S(1)}, bf16[512,512]{1,0:T(8,128)(2,1)S(1)}, u32[]{:S(2)}, u32[]{:S(2)}) collective-permute-start(bf16[512,512]{1,0:T(8,128)(2,1)S(1)} %get-tuple-element.49.refs_11_.refs_5_), channel_id=1, source_target_pairs={{0,8},{8,0},{16,24},{24,16},{1,9},{9,1},{17,25},{25,17},{2,10},{10... | collective-permute-start | bytes 1572872 | tf_op jit(solution)/shard_map/ppermute | solution.py:206
  15.7 9.3 %collective-permute-start.2 = (bf16[128,1024]{1,0:T(8,128)(2,1)S(1)}, bf16[128,1024]{1,0:T(8,128)(2,1)S(1)}, u32[]{:S(2)}, u32[]{:S(2)}) collective-permute-start(bf16[128,1024]{1,0:T(8,128)(2,1)S(1)} %get-tuple-element.59.refs_0_), channel_id=1, source_target_pairs={{0,2},{2,4},{4,6},{6,7},{7,5},{5,3},{3,1},{1,0},{8,10},{10,12},{12... | collective-permute-start | bytes 786440 | tf_op jit(solution)/shard_map/ppermute | solution.py:232
  16.2 9.2 %collective-permute-start.6 = (bf16[128,1024]{1,0:T(8,128)(2,1)S(1)}, bf16[128,1024]{1,0:T(8,128)(2,1)S(1)}, u32[]{:S(2)}, u32[]{:S(2)}) collective-permute-start(bf16[128,1024]{1,0:T(8,128)(2,1)S(1)} %get-tuple-element.60.refs_1_), channel_id=1, source_target_pairs={{2,0},{4,2},{6,4},{7,6},{5,7},{3,5},{1,3},{0,1},{10,8},{12,10},{14... | collective-permute-start | bytes 786440 | tf_op jit(solution)/shard_map/ppermute | solution.py:233
  17.8 12.8 %collective-permute-start.11 = (bf16[128,1024]{1,0:T(8,128)(2,1)S(1)}, bf16[128,1024]{1,0:T(8,128)(2,1)S(1)}, u32[]{:S(2)}, u32[]{:S(2)}) collective-permute-start(bf16[128,1024]{1,0:T(8,128)(2,1)S(1)} %get-tuple-element.60.refs_1_), channel_id=1, source_target_pairs={{0,2},{2,4},{4,6},{6,7},{7,5},{5,3},{3,1},{1,0},{8,10},{10,12},{12... | collective-permute-start | bytes 786440 | tf_op jit(solution)/shard_map/ppermute | solution.py:232
  18.2 12.8 %collective-permute-start.12 = (bf16[128,1024]{1,0:T(8,128)(2,1)S(1)}, bf16[128,1024]{1,0:T(8,128)(2,1)S(1)}, u32[]{:S(2)}, u32[]{:S(2)}) collective-permute-start(bf16[128,1024]{1,0:T(8,128)(2,1)S(1)} %get-tuple-element.59.refs_0_), channel_id=1, source_target_pairs={{2,0},{4,2},{6,4},{7,6},{5,7},{3,5},{1,3},{0,1},{10,8},{12,10},{14... | collective-permute-start | bytes 786440 | tf_op jit(solution)/shard_map/ppermute | solution.py:233
  25.0 11.2 %collective-permute-start.3 = (bf16[128,1024]{1,0:T(8,128)(2,1)S(1)}, bf16[128,1024]{1,0:T(8,128)(2,1)S(1)}, u32[]{:S(2)}, u32[]{:S(2)}) collective-permute-start(bf16[128,1024]{1,0:T(8,128)(2,1)S(1)} %collective-permute-done.2.refs_2_), channel_id=1, source_target_pairs={{0,2},{2,4},{4,6},{6,7},{7,5},{5,3},{3,1},{1,0},{8,10},{10,12},{12... | collective-permute-start | bytes 786440 | tf_op jit(solution)/shard_map/ppermute | solution.py:232
  25.4 20.3 %collective-permute-start.10 = (bf16[512,512]{1,0:T(8,128)(2,1)S(1)}, bf16[512,512]{1,0:T(8,128)(2,1)S(1)}, u32[]{:S(2)}, u32[]{:S(2)}) collective-permute-start(bf16[512,512]{1,0:T(8,128)(2,1)S(1)} %get-tuple-element.45.refs_10_.refs_4_), channel_id=1, source_target_pairs={{0,16},{8,24},{16,0},{24,8},{1,17},{9,25},{17,1},{25,9},{2,18},{10... | collective-permute-start | bytes 1572872 | tf_op jit(solution)/shard_map/ppermute | solution.py:206
  26.9 10.8 %collective-permute-start.7 = (bf16[128,1024]{1,0:T(8,128)(2,1)S(1)}, bf16[128,1024]{1,0:T(8,128)(2,1)S(1)}, u32[]{:S(2)}, u32[]{:S(2)}) collective-permute-start(bf16[128,1024]{1,0:T(8,128)(2,1)S(1)} %collective-permute-done.6.refs_5_), channel_id=1, source_target_pairs={{2,0},{4,2},{6,4},{7,6},{5,7},{3,5},{1,3},{0,1},{10,8},{12,10},{14... | collective-permute-start | bytes 786440 | tf_op jit(solution)/shard_map/ppermute | solution.py:233
  30.6 11.2 %collective-permute-start.14 = (bf16[128,1024]{1,0:T(8,128)(2,1)S(1)}, bf16[128,1024]{1,0:T(8,128)(2,1)S(1)}, u32[]{:S(2)}, u32[]{:S(2)}) collective-permute-start(bf16[128,1024]{1,0:T(8,128)(2,1)S(1)} %collective-permute-done.11.refs_3_), channel_id=1, source_target_pairs={{0,2},{2,4},{4,6},{6,7},{7,5},{5,3},{3,1},{1,0},{8,10},{10,12},{12... | collective-permute-start | bytes 786440 | tf_op jit(solution)/shard_map/ppermute | solution.py:232
  31.0 17.2 %collective-permute-start.13 = (bf16[512,512]{1,0:T(8,128)(2,1)S(1)}, bf16[512,512]{1,0:T(8,128)(2,1)S(1)}, u32[]{:S(2)}, u32[]{:S(2)}) collective-permute-start(bf16[512,512]{1,0:T(8,128)(2,1)S(1)} %get-tuple-element.49.refs_11_.refs_5_), channel_id=1, source_target_pairs={{0,16},{8,24},{16,0},{24,8},{1,17},{9,25},{17,1},{25,9},{2,18},{10... | collective-permute-start | bytes 1572872 | tf_op jit(solution)/shard_map/ppermute | solution.py:206
  36.2 9.1 %collective-permute-start.16 = (bf16[128,1024]{1,0:T(8,128)(2,1)S(1)}, bf16[128,1024]{1,0:T(8,128)(2,1)S(1)}, u32[]{:S(2)}, u32[]{:S(2)}) collective-permute-start(bf16[128,1024]{1,0:T(8,128)(2,1)S(1)} %collective-permute-done.12.refs_4_), channel_id=1, source_target_pairs={{2,0},{4,2},{6,4},{7,6},{5,7},{3,5},{1,3},{0,1},{10,8},{12,10},{14... | collective-permute-start | bytes 786440 | tf_op jit(solution)/shard_map/ppermute | solution.py:233
  37.7 9.6 %collective-permute-start.4 = (bf16[128,1024]{1,0:T(8,128)(2,1)S(1)}, bf16[128,1024]{1,0:T(8,128)(2,1)S(1)}, u32[]{:S(2)}, u32[]{:S(2)}) collective-permute-start(bf16[128,1024]{1,0:T(8,128)(2,1)S(1)} %collective-permute-done.3.refs_6_), channel_id=1, source_target_pairs={{0,2},{2,4},{4,6},{6,7},{7,5},{5,3},{3,1},{1,0},{8,10},{10,12},{12... | collective-permute-start | bytes 786440 | tf_op jit(solution)/shard_map/ppermute | solution.py:232
  41.8 6.4 %collective-permute-start.8 = (bf16[128,1024]{1,0:T(8,128)(2,1)S(1)}, bf16[128,1024]{1,0:T(8,128)(2,1)S(1)}, u32[]{:S(2)}, u32[]{:S(2)}) collective-permute-start(bf16[128,1024]{1,0:T(8,128)(2,1)S(1)} %collective-permute-done.7.refs_9_), channel_id=1, source_target_pairs={{2,0},{4,2},{6,4},{7,6},{5,7},{3,5},{1,3},{0,1},{10,8},{12,10},{14... | collective-permute-start | bytes 786440 | tf_op jit(solution)/shard_map/ppermute | solution.py:233
  45.3 6.4 %collective-permute-start.15 = (bf16[128,1024]{1,0:T(8,128)(2,1)S(1)}, bf16[128,1024]{1,0:T(8,128)(2,1)S(1)}, u32[]{:S(2)}, u32[]{:S(2)}) collective-permute-start(bf16[128,1024]{1,0:T(8,128)(2,1)S(1)} %collective-permute-done.14.refs_7_), channel_id=1, source_target_pairs={{0,2},{2,4},{4,6},{6,7},{7,5},{5,3},{3,1},{1,0},{8,10},{10,12},{12... | collective-permute-start | bytes 786440 | tf_op jit(solution)/shard_map/ppermute | solution.py:232
  45.8 6.4 %collective-permute-start.17 = (bf16[128,1024]{1,0:T(8,128)(2,1)S(1)}, bf16[128,1024]{1,0:T(8,128)(2,1)S(1)}, u32[]{:S(2)}, u32[]{:S(2)}) collective-permute-start(bf16[128,1024]{1,0:T(8,128)(2,1)S(1)} %collective-permute-done.16.refs_8_), channel_id=1, source_target_pairs={{2,0},{4,2},{6,4},{7,6},{5,7},{3,5},{1,3},{0,1},{10,8},{12,10},{14... | collective-permute-start | bytes 786440 | tf_op jit(solution)/shard_map/ppermute | solution.py:233
  48.2 6.0 %collective-permute-start.18 = (bf16[512,512]{1,0:T(8,128)(2,1)S(1)}, bf16[512,512]{1,0:T(8,128)(2,1)S(1)}, u32[]{:S(2)}, u32[]{:S(2)}) collective-permute-start(bf16[512,512]{1,0:T(8,128)(2,1)S(1)} %collective-permute-done.10.refs_14_.refs_8_), channel_id=1, source_target_pairs={{0,8},{8,0},{16,24},{24,16},{1,9},{9,1},{17,25},{25,17},{2,10},{10... | collective-permute-start | bytes 1572872 | tf_op jit(solution)/shard_map/ppermute | solution.py:206
  52.1 2.0 %collective-permute-start.19 = (bf16[512,512]{1,0:T(8,128)(2,1)S(1)}, bf16[512,512]{1,0:T(8,128)(2,1)S(1)}, u32[]{:S(2)}, u32[]{:S(2)}) collective-permute-start(bf16[512,512]{1,0:T(8,128)(2,1)S(1)} %collective-permute-done.13.refs_15_.refs_9_), channel_id=1, source_target_pairs={{0,8},{8,0},{16,24},{24,16},{1,9},{9,1},{17,25},{25,17},{2,10},{10... | collective-permute-start | bytes 1572872 | tf_op jit(solution)/shard_map/ppermute | solution.py:206
  52.1 8.7 %collective-permute-start.5 = (bf16[128,1024]{1,0:T(8,128)(2,1)S(1)}, bf16[128,1024]{1,0:T(8,128)(2,1)S(1)}, u32[]{:S(2)}, u32[]{:S(2)}) collective-permute-start(bf16[128,1024]{1,0:T(8,128)(2,1)S(1)} %collective-permute-done.4.refs_0_), channel_id=1, source_target_pairs={{0,2},{2,4},{4,6},{6,7},{7,5},{5,3},{3,1},{1,0},{8,10},{10,12},{12... | collective-permute-start | bytes 786440 | tf_op jit(solution)/shard_map/ppermute | solution.py:232
  52.4 8.5 %collective-permute-start.9 = (bf16[128,1024]{1,0:T(8,128)(2,1)S(1)}, bf16[128,1024]{1,0:T(8,128)(2,1)S(1)}, u32[]{:S(2)}, u32[]{:S(2)}) collective-permute-start(bf16[128,1024]{1,0:T(8,128)(2,1)S(1)} %collective-permute-done.8.refs_3_), channel_id=1, source_target_pairs={{2,0},{4,2},{6,4},{7,6},{5,7},{3,5},{1,3},{0,1},{10,8},{12,10},{14... | collective-permute-start | bytes 786440 | tf_op jit(solution)/shard_map/ppermute | solution.py:233

commit v6 on v5

--- a/solution.py
+++ b/solution.py
@@ -247,7 +247,7 @@
     pieces = {0: masked, 1: sibling}
     for j in range(2, n_row, 2):
         pieces[j] = []
-        for p, turn in zip(masked, (0, 1)):
+        for p, turn in zip(masked, (None, 0)):
             (p,) = after(turn, (p,), "b")
             pieces[j].append(swap(p, j))
         pieces[j + 1] = []

time: 62.2 us -> 60.8 us (0.977)
  starting transfers between devices: 17.8 us -> 16.9 us
    ppermute x7, waiting for transfers between devices: 3.31 us -> 0.54 us  [on_device(): held[b][1 - t] = lax.ppermute(held[(b + 1) % n_col][1 - t], 'col', down)]
    ppermute x7, waiting for transfers between devices: 19.5 us -> 21.8 us  [on_device(): held[k][t] = lax.ppermute(held[k - 1][t], 'col', up)]
    ppermute x6, starting transfers between devices: 3.58 us -> 2.69 us  [swap(): return lax.ppermute(x, 'row', [(i, i ^ j) for i in range(n_row)])]
  transfers between devices with their start and end apart: 20 -> 20, of which waited for: 9 -> 10; matrix products, arithmetic and copies ran while one was open for 0% -> 0% of each run, Pallas kernels for 8% -> 8%
where the time goes in v6:
time: 60.8 us; the launch traced here: 60.7 us
  waiting for transfers between devices  22.4 us (37%)
  starting transfers between devices  16.9 us (28%)
  blocking collectives  13 us (21%)
  Pallas kernels  8.32 us (14%)
    ppermute x7, waiting for transfers between devices, on_device(): held[k][t] = lax.ppermute(held[k - 1][t], 'col', up)  21.8 us
    psum x1, blocking collectives, on_device(): mask = lax.psum(placed, 'col')  13 us
    ppermute x7, starting transfers between devices, on_device(): held[b][1 - t] = lax.ppermute(held[(b + 1) % n_col][1 - t], 'col', down)  11 us
    pallas_call x2, Pallas kernels, ladder_rows(): pl.pallas_call(functools.partial(ladder_kernel, n_row, n_col, kt_local, s...  5.14 us
    ppermute x7, starting transfers between devices, on_device(): held[k][t] = lax.ppermute(held[k - 1][t], 'col', up)  3.15 us
    ppermute x6, starting transfers between devices, swap(): return lax.ppermute(x, 'row', [(i, i ^ j) for i in range(n_row)])  2.69 us
    pallas_call x1, Pallas kernels, on_device(): pl.pallas_call(stage_kernel, out_shape=[jax.ShapeDtypeStruct((kblock, n_c...  1.58 us
  transfers between devices with their start and end apart: 20, of which 10 were waited for; matrix products, arithmetic and copies ran while one was open for 0% of the time, Pallas kernels for 8%

profile of v6, /device:TPU:0, one launch (start us, length us, event | category | flops | bytes accessed | tf_op | source)
XLA Modules:
  0.0 60.7 jit_solution(9990457416632589973)
XLA Ops:
  0.0 1.6 %shard_map.46 = (s32[4,64]{1,0:T(4,128)S(1)}, bf16[128,4096]{1,0:T(8,128)(2,1)S(1)}, bf16[512,512]{1,0:T(8,128)(2,1)S(1)}, bf16[512,512]{1,0:T(8,128)(2,1)S(1)}) custom-call(s32[4,8]{1,0:T(4,128)} %bitcast.2, bf16[128,4096]{1,0:T(8,128)(2,1)} %a_ref.1, s32[4,8]{1,0:T(4,128)} %bitcast.3, bf16[1024,512]{1,0:T(8,128)(2,1)} %x_ref.1), custom_call_target="tpu_custom_call" | custom-call | tf_op jit(solution)/shard_map/pallas_call | solution.py:181
  1.6 0.5 collective-permute-start
  2.2 13.0 %psum.7.mask_ref = s32[4,64]{1,0:T(4,128)S(1)} all-reduce(s32[4,64]{1,0:T(4,128)S(1)} %get-tuple-element.32), channel_id=1, replica_groups=mesh['row'=4,'col'=8] {'col'}, use_global_device_ids=true, to_apply=%region_0.0 | all-reduce | flops 256 | bytes 2048 | tf_op jit(solution)/shard_map/psum | solution.py:209
  15.7 1.6 %collective-permute-start.10 = (bf16[512,512]{1,0:T(8,128)(2,1)S(1)}, bf16[512,512]{1,0:T(8,128)(2,1)S(1)}, u32[]{:S(2)}, u32[]{:S(2)}) collective-permute-start(bf16[512,512]{1,0:T(8,128)(2,1)S(1)} %get-tuple-element.39.refs_10_.refs_4_), channel_id=1, source_target_pairs={{0,16},{8,24},{16,0},{24,8},{1,17},{9,25},{17,1},{25,9},{2,18},{10... | collective-permute-start | bytes 1572872 | tf_op jit(solution)/shard_map/ppermute | solution.py:206
  17.2 0.5 collective-permute-start.2
  17.7 1.6 %collective-permute-start.6 = (bf16[128,1024]{1,0:T(8,128)(2,1)S(1)}, bf16[128,1024]{1,0:T(8,128)(2,1)S(1)}, u32[]{:S(2)}, u32[]{:S(2)}) collective-permute-start(bf16[128,1024]{1,0:T(8,128)(2,1)S(1)} %get-tuple-element.54.refs_1_), channel_id=1, source_target_pairs={{2,0},{4,2},{6,4},{7,6},{5,7},{3,5},{1,3},{0,1},{10,8},{12,10},{14... | collective-permute-start | bytes 786440 | tf_op jit(solution)/shard_map/ppermute | solution.py:233
  19.3 0.5 collective-permute-start.12
  19.7 1.6 %collective-permute-start.15 = (bf16[128,1024]{1,0:T(8,128)(2,1)S(1)}, bf16[128,1024]{1,0:T(8,128)(2,1)S(1)}, u32[]{:S(2)}, u32[]{:S(2)}) collective-permute-start(bf16[128,1024]{1,0:T(8,128)(2,1)S(1)} %get-tuple-element.53.refs_0_), channel_id=1, source_target_pairs={{2,0},{4,2},{6,4},{7,6},{5,7},{3,5},{1,3},{0,1},{10,8},{12,10},{14... | collective-permute-start | bytes 786440 | tf_op jit(solution)/shard_map/ppermute | solution.py:233
  21.3 5.2 %collective-permute-done.2.refs_2_ = bf16[128,1024]{1,0:T(8,128)(2,1)S(1)} collective-permute-done((bf16[128,1024]{1,0:T(8,128)(2,1)S(1)}, bf16[128,1024]{1,0:T(8,128)(2,1)S(1)}, u32[]{:S(2)}, u32[]{:S(2)}) %collective-permute-start.2) | collective-permute-done | bytes 262176 | tf_op jit(solution)/shard_map/ppermute | solution.py:232
  26.9 1.6 %collective-permute-start.7 = (bf16[128,1024]{1,0:T(8,128)(2,1)S(1)}, bf16[128,1024]{1,0:T(8,128)(2,1)S(1)}, u32[]{:S(2)}, u32[]{:S(2)}) collective-permute-start(bf16[128,1024]{1,0:T(8,128)(2,1)S(1)} %collective-permute-done.6.refs_5_), channel_id=1, source_target_pairs={{2,0},{4,2},{6,4},{7,6},{5,7},{3,5},{1,3},{0,1},{10,8},{12,10},{14... | collective-permute-start | bytes 786440 | tf_op jit(solution)/shard_map/ppermute | solution.py:233
  28.5 3.6 %collective-permute-done.12.refs_3_ = bf16[128,1024]{1,0:T(8,128)(2,1)S(1)} collective-permute-done((bf16[128,1024]{1,0:T(8,128)(2,1)S(1)}, bf16[128,1024]{1,0:T(8,128)(2,1)S(1)}, u32[]{:S(2)}, u32[]{:S(2)}) %collective-permute-start.12) | collective-permute-done | bytes 262176 | tf_op jit(solution)/shard_map/ppermute | solution.py:232
  32.1 0.5 collective-permute-start.11
  33.1 1.6 %collective-permute-start.16 = (bf16[128,1024]{1,0:T(8,128)(2,1)S(1)}, bf16[128,1024]{1,0:T(8,128)(2,1)S(1)}, u32[]{:S(2)}, u32[]{:S(2)}) collective-permute-start(bf16[128,1024]{1,0:T(8,128)(2,1)S(1)} %collective-permute-done.15.refs_4_), channel_id=1, source_target_pairs={{2,0},{4,2},{6,4},{7,6},{5,7},{3,5},{1,3},{0,1},{10,8},{12,10},{14... | collective-permute-start | bytes 786440 | tf_op jit(solution)/shard_map/ppermute | solution.py:233
  34.7 3.0 %collective-permute-done.3.refs_6_ = bf16[128,1024]{1,0:T(8,128)(2,1)S(1)} collective-permute-done((bf16[128,1024]{1,0:T(8,128)(2,1)S(1)}, bf16[128,1024]{1,0:T(8,128)(2,1)S(1)}, u32[]{:S(2)}, u32[]{:S(2)}) %collective-permute-start.3) | collective-permute-done | bytes 262176 | tf_op jit(solution)/shard_map/ppermute | solution.py:232
  38.2 1.6 %collective-permute-start.8 = (bf16[128,1024]{1,0:T(8,128)(2,1)S(1)}, bf16[128,1024]{1,0:T(8,128)(2,1)S(1)}, u32[]{:S(2)}, u32[]{:S(2)}) collective-permute-start(bf16[128,1024]{1,0:T(8,128)(2,1)S(1)} %collective-permute-done.7.refs_9_), channel_id=1, source_target_pairs={{2,0},{4,2},{6,4},{7,6},{5,7},{3,5},{1,3},{0,1},{10,8},{12,10},{14... | collective-permute-start | bytes 786440 | tf_op jit(solution)/shard_map/ppermute | solution.py:233
  39.7 3.6 %collective-permute-done.13.refs_7_ = bf16[128,1024]{1,0:T(8,128)(2,1)S(1)} collective-permute-done((bf16[128,1024]{1,0:T(8,128)(2,1)S(1)}, bf16[128,1024]{1,0:T(8,128)(2,1)S(1)}, u32[]{:S(2)}, u32[]{:S(2)}) %collective-permute-start.13) | collective-permute-done | bytes 262176 | tf_op jit(solution)/shard_map/ppermute | solution.py:232
  43.8 1.6 %collective-permute-start.17 = (bf16[128,1024]{1,0:T(8,128)(2,1)S(1)}, bf16[128,1024]{1,0:T(8,128)(2,1)S(1)}, u32[]{:S(2)}, u32[]{:S(2)}) collective-permute-start(bf16[128,1024]{1,0:T(8,128)(2,1)S(1)} %collective-permute-done.16.refs_8_), channel_id=1, source_target_pairs={{2,0},{4,2},{6,4},{7,6},{5,7},{3,5},{1,3},{0,1},{10,8},{12,10},{14... | collective-permute-start | bytes 786440 | tf_op jit(solution)/shard_map/ppermute | solution.py:233
  45.4 2.3 %collective-permute-done.4.refs_0_ = bf16[128,1024]{1,0:T(8,128)(2,1)S(1)} collective-permute-done((bf16[128,1024]{1,0:T(8,128)(2,1)S(1)}, bf16[128,1024]{1,0:T(8,128)(2,1)S(1)}, u32[]{:S(2)}, u32[]{:S(2)}) %collective-permute-start.4) | collective-permute-done | bytes 262176 | tf_op jit(solution)/shard_map/ppermute | solution.py:232
  47.8 2.6 %collective-permute-done.14.refs_1_ = bf16[128,1024]{1,0:T(8,128)(2,1)S(1)} collective-permute-done((bf16[128,1024]{1,0:T(8,128)(2,1)S(1)}, bf16[128,1024]{1,0:T(8,128)(2,1)S(1)}, u32[]{:S(2)}, u32[]{:S(2)}) %collective-permute-start.14) | collective-permute-done | bytes 262176 | tf_op jit(solution)/shard_map/ppermute | solution.py:232
  51.1 1.6 %collective-permute-start.9 = (bf16[128,1024]{1,0:T(8,128)(2,1)S(1)}, bf16[128,1024]{1,0:T(8,128)(2,1)S(1)}, u32[]{:S(2)}, u32[]{:S(2)}) collective-permute-start(bf16[128,1024]{1,0:T(8,128)(2,1)S(1)} %collective-permute-done.8.refs_3_), channel_id=1, source_target_pairs={{2,0},{4,2},{6,4},{7,6},{5,7},{3,5},{1,3},{0,1},{10,8},{12,10},{14... | collective-permute-start | bytes 786440 | tf_op jit(solution)/shard_map/ppermute | solution.py:233
  52.7 3.0 %shard_map.48.refs_12_ = f32[1024,512]{1,0:T(8,128)} custom-call(s32[4,64]{1,0:T(4,128)S(1)} %psum.7.mask_ref, bf16[128,1024]{1,0:T(8,128)(2,1)S(1)} %get-tuple-element.53.refs_0_, bf16[128,1024]{1,0:T(8,128)(2,1)S(1)} %get-tuple-element.54.refs_1_, bf16[128,1024]{1,0:T(8,128)(2,1)S(1)} %collective-permute-done.2.refs_2_, ...), custom_call_target="tpu_custom_call" | custom-call | tf_op jit(solution)/shard_map/pallas_call | solution.py:163
  55.7 2.1 %shard_map.49 = (f32[1024,512]{1,0:T(8,128)}, bf16[2048,512]{1,0:T(8,128)(2,1)S(1)}) custom-call(s32[4,64]{1,0:T(4,128)S(1)} %psum.7.mask_ref, bf16[128,1024]{1,0:T(8,128)(2,1)S(1)} %collective-permute-done.4.refs_0_, bf16[128,1024]{1,0:T(8,128)(2,1)S(1)} %collective-permute-done.14.refs_1_, ...), custom_call_target="tpu_custom_call", output_to_operand_aliasing={{0}: (13, {})} | custom-call | tf_op jit(solution)/shard_map/pallas_call | solution.py:163
  57.8 1.5 %collective-permute-done.5.refs_0_ = bf16[128,1024]{1,0:T(8,128)(2,1)S(1)} collective-permute-done((bf16[128,1024]{1,0:T(8,128)(2,1)S(1)}, bf16[128,1024]{1,0:T(8,128)(2,1)S(1)}, u32[]{:S(2)}, u32[]{:S(2)}) %collective-permute-start.5) | collective-permute-done | bytes 262176 | tf_op jit(solution)/shard_map/ppermute | solution.py:232
  59.5 1.2 %shard_map.50 = f32[1024,512]{1,0:T(8,128)} custom-call(bf16[128,1024]{1,0:T(8,128)(2,1)S(1)} %collective-permute-done.5.refs_0_, bf16[128,1024]{1,0:T(8,128)(2,1)S(1)} %collective-permute-done.9.refs_1_, bf16[2048,512]{1,0:T(8,128)(2,1)S(1)} %get-tuple-element.57.refs_2_, f32[1024,512]{1,0:T(8,128)} %get-tuple-element.58.refs_3_), custom_call_target="tpu_custom_call", output_to_operand_aliasing={{}: (3, {})} | custom-call | tf_op jit(solution)/shard_map/pallas_call | solution.py:264
  (22 shorter events, 3.3 us)
Async XLA Ops:
  1.6 13.6 %collective-permute-start = (bf16[512,512]{1,0:T(8,128)(2,1)S(1)}, bf16[512,512]{1,0:T(8,128)(2,1)S(1)}, u32[]{:S(2)}, u32[]{:S(2)}) collective-permute-start(bf16[512,512]{1,0:T(8,128)(2,1)S(1)} %get-tuple-element.39.refs_10_.refs_4_), channel_id=1, source_target_pairs={{0,8},{8,0},{16,24},{24,16},{1,9},{9,1},{17,25},{25,17},{2,10},{10... | collective-permute-start | bytes 1572872 | tf_op jit(solution)/shard_map/ppermute | solution.py:206
  2.1 13.1 %collective-permute-start.1 = (bf16[512,512]{1,0:T(8,128)(2,1)S(1)}, bf16[512,512]{1,0:T(8,128)(2,1)S(1)}, u32[]{:S(2)}, u32[]{:S(2)}) collective-permute-start(bf16[512,512]{1,0:T(8,128)(2,1)S(1)} %get-tuple-element.43.refs_11_.refs_5_), channel_id=1, source_target_pairs={{0,8},{8,0},{16,24},{24,16},{1,9},{9,1},{17,25},{25,17},{2,10},{10... | collective-permute-start | bytes 1572872 | tf_op jit(solution)/shard_map/ppermute | solution.py:206
  15.7 17.4 %collective-permute-start.10 = (bf16[512,512]{1,0:T(8,128)(2,1)S(1)}, bf16[512,512]{1,0:T(8,128)(2,1)S(1)}, u32[]{:S(2)}, u32[]{:S(2)}) collective-permute-start(bf16[512,512]{1,0:T(8,128)(2,1)S(1)} %get-tuple-element.39.refs_10_.refs_4_), channel_id=1, source_target_pairs={{0,16},{8,24},{16,0},{24,8},{1,17},{9,25},{17,1},{25,9},{2,18},{10... | collective-permute-start | bytes 1572872 | tf_op jit(solution)/shard_map/ppermute | solution.py:206
  17.2 9.2 %collective-permute-start.2 = (bf16[128,1024]{1,0:T(8,128)(2,1)S(1)}, bf16[128,1024]{1,0:T(8,128)(2,1)S(1)}, u32[]{:S(2)}, u32[]{:S(2)}) collective-permute-start(bf16[128,1024]{1,0:T(8,128)(2,1)S(1)} %get-tuple-element.53.refs_0_), channel_id=1, source_target_pairs={{0,2},{2,4},{4,6},{6,7},{7,5},{5,3},{3,1},{1,0},{8,10},{10,12},{12... | collective-permute-start | bytes 786440 | tf_op jit(solution)/shard_map/ppermute | solution.py:232
  17.7 9.2 %collective-permute-start.6 = (bf16[128,1024]{1,0:T(8,128)(2,1)S(1)}, bf16[128,1024]{1,0:T(8,128)(2,1)S(1)}, u32[]{:S(2)}, u32[]{:S(2)}) collective-permute-start(bf16[128,1024]{1,0:T(8,128)(2,1)S(1)} %get-tuple-element.54.refs_1_), channel_id=1, source_target_pairs={{2,0},{4,2},{6,4},{7,6},{5,7},{3,5},{1,3},{0,1},{10,8},{12,10},{14... | collective-permute-start | bytes 786440 | tf_op jit(solution)/shard_map/ppermute | solution.py:233
  19.3 12.8 %collective-permute-start.12 = (bf16[128,1024]{1,0:T(8,128)(2,1)S(1)}, bf16[128,1024]{1,0:T(8,128)(2,1)S(1)}, u32[]{:S(2)}, u32[]{:S(2)}) collective-permute-start(bf16[128,1024]{1,0:T(8,128)(2,1)S(1)} %get-tuple-element.54.refs_1_), channel_id=1, source_target_pairs={{0,2},{2,4},{4,6},{6,7},{7,5},{5,3},{3,1},{1,0},{8,10},{10,12},{12... | collective-permute-start | bytes 786440 | tf_op jit(solution)/shard_map/ppermute | solution.py:232
  19.7 12.9 %collective-permute-start.15 = (bf16[128,1024]{1,0:T(8,128)(2,1)S(1)}, bf16[128,1024]{1,0:T(8,128)(2,1)S(1)}, u32[]{:S(2)}, u32[]{:S(2)}) collective-permute-start(bf16[128,1024]{1,0:T(8,128)(2,1)S(1)} %get-tuple-element.53.refs_0_), channel_id=1, source_target_pairs={{2,0},{4,2},{6,4},{7,6},{5,7},{3,5},{1,3},{0,1},{10,8},{12,10},{14... | collective-permute-start | bytes 786440 | tf_op jit(solution)/shard_map/ppermute | solution.py:233
  26.5 11.2 %collective-permute-start.3 = (bf16[128,1024]{1,0:T(8,128)(2,1)S(1)}, bf16[128,1024]{1,0:T(8,128)(2,1)S(1)}, u32[]{:S(2)}, u32[]{:S(2)}) collective-permute-start(bf16[128,1024]{1,0:T(8,128)(2,1)S(1)} %collective-permute-done.2.refs_2_), channel_id=1, source_target_pairs={{0,2},{2,4},{4,6},{6,7},{7,5},{5,3},{3,1},{1,0},{8,10},{10,12},{12... | collective-permute-start | bytes 786440 | tf_op jit(solution)/shard_map/ppermute | solution.py:232
  26.9 11.2 %collective-permute-start.7 = (bf16[128,1024]{1,0:T(8,128)(2,1)S(1)}, bf16[128,1024]{1,0:T(8,128)(2,1)S(1)}, u32[]{:S(2)}, u32[]{:S(2)}) collective-permute-start(bf16[128,1024]{1,0:T(8,128)(2,1)S(1)} %collective-permute-done.6.refs_5_), channel_id=1, source_target_pairs={{2,0},{4,2},{6,4},{7,6},{5,7},{3,5},{1,3},{0,1},{10,8},{12,10},{14... | collective-permute-start | bytes 786440 | tf_op jit(solution)/shard_map/ppermute | solution.py:233
  32.1 15.7 %collective-permute-start.11 = (bf16[512,512]{1,0:T(8,128)(2,1)S(1)}, bf16[512,512]{1,0:T(8,128)(2,1)S(1)}, u32[]{:S(2)}, u32[]{:S(2)}) collective-permute-start(bf16[512,512]{1,0:T(8,128)(2,1)S(1)} %get-tuple-element.43.refs_11_.refs_5_), channel_id=1, source_target_pairs={{0,16},{8,24},{16,0},{24,8},{1,17},{9,25},{17,1},{25,9},{2,18},{10... | collective-permute-start | bytes 1572872 | tf_op jit(solution)/shard_map/ppermute | solution.py:206
  32.6 10.7 %collective-permute-start.13 = (bf16[128,1024]{1,0:T(8,128)(2,1)S(1)}, bf16[128,1024]{1,0:T(8,128)(2,1)S(1)}, u32[]{:S(2)}, u32[]{:S(2)}) collective-permute-start(bf16[128,1024]{1,0:T(8,128)(2,1)S(1)} %collective-permute-done.12.refs_3_), channel_id=1, source_target_pairs={{0,2},{2,4},{4,6},{6,7},{7,5},{5,3},{3,1},{1,0},{8,10},{10,12},{12... | collective-permute-start | bytes 786440 | tf_op jit(solution)/shard_map/ppermute | solution.py:232
  33.1 10.7 %collective-permute-start.16 = (bf16[128,1024]{1,0:T(8,128)(2,1)S(1)}, bf16[128,1024]{1,0:T(8,128)(2,1)S(1)}, u32[]{:S(2)}, u32[]{:S(2)}) collective-permute-start(bf16[128,1024]{1,0:T(8,128)(2,1)S(1)} %collective-permute-done.15.refs_4_), channel_id=1, source_target_pairs={{2,0},{4,2},{6,4},{7,6},{5,7},{3,5},{1,3},{0,1},{10,8},{12,10},{14... | collective-permute-start | bytes 786440 | tf_op jit(solution)/shard_map/ppermute | solution.py:233
  37.7 9.9 %collective-permute-start.4 = (bf16[128,1024]{1,0:T(8,128)(2,1)S(1)}, bf16[128,1024]{1,0:T(8,128)(2,1)S(1)}, u32[]{:S(2)}, u32[]{:S(2)}) collective-permute-start(bf16[128,1024]{1,0:T(8,128)(2,1)S(1)} %collective-permute-done.3.refs_6_), channel_id=1, source_target_pairs={{0,2},{2,4},{4,6},{6,7},{7,5},{5,3},{3,1},{1,0},{8,10},{10,12},{12... | collective-permute-start | bytes 786440 | tf_op jit(solution)/shard_map/ppermute | solution.py:232
  38.2 9.7 %collective-permute-start.8 = (bf16[128,1024]{1,0:T(8,128)(2,1)S(1)}, bf16[128,1024]{1,0:T(8,128)(2,1)S(1)}, u32[]{:S(2)}, u32[]{:S(2)}) collective-permute-start(bf16[128,1024]{1,0:T(8,128)(2,1)S(1)} %collective-permute-done.7.refs_9_), channel_id=1, source_target_pairs={{2,0},{4,2},{6,4},{7,6},{5,7},{3,5},{1,3},{0,1},{10,8},{12,10},{14... | collective-permute-start | bytes 786440 | tf_op jit(solution)/shard_map/ppermute | solution.py:233
  43.3 7.1 %collective-permute-start.14 = (bf16[128,1024]{1,0:T(8,128)(2,1)S(1)}, bf16[128,1024]{1,0:T(8,128)(2,1)S(1)}, u32[]{:S(2)}, u32[]{:S(2)}) collective-permute-start(bf16[128,1024]{1,0:T(8,128)(2,1)S(1)} %collective-permute-done.13.refs_7_), channel_id=1, source_target_pairs={{0,2},{2,4},{4,6},{6,7},{7,5},{5,3},{3,1},{1,0},{8,10},{10,12},{12... | collective-permute-start | bytes 786440 | tf_op jit(solution)/shard_map/ppermute | solution.py:232
  43.8 6.8 %collective-permute-start.17 = (bf16[128,1024]{1,0:T(8,128)(2,1)S(1)}, bf16[128,1024]{1,0:T(8,128)(2,1)S(1)}, u32[]{:S(2)}, u32[]{:S(2)}) collective-permute-start(bf16[128,1024]{1,0:T(8,128)(2,1)S(1)} %collective-permute-done.16.refs_8_), channel_id=1, source_target_pairs={{2,0},{4,2},{6,4},{7,6},{5,7},{3,5},{1,3},{0,1},{10,8},{12,10},{14... | collective-permute-start | bytes 786440 | tf_op jit(solution)/shard_map/ppermute | solution.py:233
  47.8 4.8 %collective-permute-start.18 = (bf16[512,512]{1,0:T(8,128)(2,1)S(1)}, bf16[512,512]{1,0:T(8,128)(2,1)S(1)}, u32[]{:S(2)}, u32[]{:S(2)}) collective-permute-start(bf16[512,512]{1,0:T(8,128)(2,1)S(1)} %collective-permute-done.10.refs_14_.refs_8_), channel_id=1, source_target_pairs={{0,8},{8,0},{16,24},{24,16},{1,9},{9,1},{17,25},{25,17},{2,10},{10... | collective-permute-start | bytes 1572872 | tf_op jit(solution)/shard_map/ppermute | solution.py:206
  50.6 2.0 %collective-permute-start.19 = (bf16[512,512]{1,0:T(8,128)(2,1)S(1)}, bf16[512,512]{1,0:T(8,128)(2,1)S(1)}, u32[]{:S(2)}, u32[]{:S(2)}) collective-permute-start(bf16[512,512]{1,0:T(8,128)(2,1)S(1)} %collective-permute-done.11.refs_15_.refs_9_), channel_id=1, source_target_pairs={{0,8},{8,0},{16,24},{24,16},{1,9},{9,1},{17,25},{25,17},{2,10},{10... | collective-permute-start | bytes 1572872 | tf_op jit(solution)/shard_map/ppermute | solution.py:206
  50.6 8.7 %collective-permute-start.5 = (bf16[128,1024]{1,0:T(8,128)(2,1)S(1)}, bf16[128,1024]{1,0:T(8,128)(2,1)S(1)}, u32[]{:S(2)}, u32[]{:S(2)}) collective-permute-start(bf16[128,1024]{1,0:T(8,128)(2,1)S(1)} %collective-permute-done.4.refs_0_), channel_id=1, source_target_pairs={{0,2},{2,4},{4,6},{6,7},{7,5},{5,3},{3,1},{1,0},{8,10},{10,12},{12... | collective-permute-start | bytes 786440 | tf_op jit(solution)/shard_map/ppermute | solution.py:232
  51.1 8.4 %collective-permute-start.9 = (bf16[128,1024]{1,0:T(8,128)(2,1)S(1)}, bf16[128,1024]{1,0:T(8,128)(2,1)S(1)}, u32[]{:S(2)}, u32[]{:S(2)}) collective-permute-start(bf16[128,1024]{1,0:T(8,128)(2,1)S(1)} %collective-permute-done.8.refs_3_), channel_id=1, source_target_pairs={{2,0},{4,2},{6,4},{7,6},{5,7},{3,5},{1,3},{0,1},{10,8},{12,10},{14... | collective-permute-start | bytes 786440 | tf_op jit(solution)/shard_map/ppermute | solution.py:233
